TPU v7x, 128 devices: a whole 4x4x4 slice. The times are simulated.
128 devices in a mesh: node: 4 (over z), band: 32 (over x, y, core).
Axes of the slice: x: 4, y: 4, z: 4, core: 2. Of those that a mesh axis runs over, the one named last changes fastest.
Arguments:
- state0: float32 [2, 1024, 4, 3, 512], P(None, 'band'), may hold values from -36 to 36
- iterate: float32 [4, 2, 1024, 4, 3, 512], P('node', None, 'band'), may hold values from -37.2 to 37.2
- legendre: bfloat16 [1024, 512, 512], P('band'), may hold values from -0.25 to 0.25
- lat_weight: float32 [512], replicated, may hold values from 0.25 to 1
- coriolis: float32 [2, 512], replicated, may hold values from -1.5 to 1.5
- damping: float32 [1024, 3, 512], P('band'), may hold values from 0.1 to 10
- quadrature: float32 [4, 4], replicated, may hold values from 0.02 to 0.25
Outputs:
- updated: float32 [4, 2, 1024, 4, 3, 512], P('node', None, 'band')
- sweep_change: float32 [3], replicated
All inputs are finite; a program needn't handle non-finite values.
Results may differ from a plain program's by a relative error of at most 0.0017.
Values may be sent and summed in bfloat16 or wider, within the bound.
No kernel may reach another device: no remote copies, remote signals or barrier semaphores. Data moves between devices by JAX's collectives and lax.ppermute only.
A program may use at most 256 MiB of HBM per device.

v0:
```python
import functools
import math

import jax
import jax.numpy as jnp
from jax import lax
from jax.sharding import Mesh
from jax.sharding import PartitionSpec as P

BAND = ("band_0", "band_1", "band_2")
NODE_BAND = ("node", "band_0", "band_1", "band_2")


def sent_together(arrays, axis, split_dim, concat_dim, along):
    ends, at = ([], 0)
    for a in arrays[:-1]:
        at += a.shape[along]
        ends.append(at)
    both = jnp.concatenate(arrays, axis=along)
    return tuple(
        jnp.split(
            lax.all_to_all(both, axis, split_axis=split_dim, concat_axis=concat_dim, tiled=True),
            ends,
            axis=along,
        )
    )


def by_axis(shard, axes):
    return functools.reduce(lax.psum, axes, shard)


def transform_tables(modes, points):
    wave = lax.iota(jnp.int32, modes)
    cell = lax.iota(jnp.int32, points)
    phase = wave[:, None] * cell[None, :] % points
    angle = phase.astype(jnp.float32) * (2.0 * math.pi / points)
    cosine = jnp.cos(angle)
    sine = jnp.sin(angle)
    scale = 1.0 / math.sqrt(modes)
    ratio = (wave.astype(jnp.float32) / modes)[:, None]
    forward = jnp.stack([cosine, -sine], axis=0) * scale
    slope_table = jnp.stack([-ratio * sine, -ratio * cosine], axis=0) * scale
    backward = jnp.stack([forward, slope_table], axis=2)
    return (forward, backward)


def body(state0, iterate, legendre, lat_weight, coriolis, damping, quadrature):
    spec = iterate[0]
    half = legendre.shape[2] // 2
    local_modes = legendre.shape[0]
    hemi = legendre.shape[1]
    members = spec.shape[2]
    nband = lax.axis_size(BAND)
    modes = local_modes * nband
    points = 2 * modes
    node = lax.axis_index("node")
    band = lax.axis_index(BAND)
    forward, backward = transform_tables(modes, points)
    coeff = spec.astype(jnp.bfloat16)
    even = jnp.einsum(
        "cmefj,mlj->cmefl",
        coeff[..., :half],
        legendre[:, :, :half],
        preferred_element_type=jnp.float32,
    )
    odd = jnp.einsum(
        "cmefj,mlj->cmefl",
        coeff[..., half:],
        legendre[:, :, half:],
        preferred_element_type=jnp.float32,
    )
    groups = 1
    even_grid, odd_grid = sent_together((even, odd), BAND, 4, 1, 0)
    lat_rows = hemi // (groups * nband)
    first = band * lat_rows
    even_grid = even_grid.reshape(2, groups, modes, members, 3, lat_rows)
    odd_grid = odd_grid.reshape(2, groups, modes, members, 3, lat_rows)
    fourier = jnp.stack([even_grid + odd_grid, even_grid - odd_grid], axis=5)
    grid = lax.dot_general(
        fourier, backward, (((0, 2), (0, 1)), ((), ())), precision=lax.Precision.HIGHEST
    )
    values = grid[..., 0, :]
    slopes = grid[..., 1, :]
    cor = lax.dynamic_slice_in_dim(coriolis, first, lat_rows, 1)[:, :, None]
    weight = lax.dynamic_slice_in_dim(lat_weight, first, lat_rows, 0)
    u_wind, v_wind, height = (values[:, :, 0], values[:, :, 1], values[:, :, 2])
    u_slope, v_slope, h_slope = (slopes[:, :, 0], slopes[:, :, 1], slopes[:, :, 2])
    tend_u = -u_wind * u_slope + cor * v_wind - h_slope
    tend_v = -u_wind * v_slope - cor * u_wind
    tend_h = -u_wind * h_slope - (1.0 + height) * u_slope
    tend = jnp.stack([tend_u, tend_v, tend_h], axis=2)
    spectra = jnp.einsum("cmk,qefhlk->cqmefhl", forward, tend, precision=lax.Precision.HIGHEST)
    symmetric = (weight * (spectra[..., 0, :] + spectra[..., 1, :])).astype(jnp.bfloat16)
    antisymmetric = (weight * (spectra[..., 0, :] - spectra[..., 1, :])).astype(jnp.bfloat16)
    symmetric = symmetric.reshape(2, groups * modes, members, 3, lat_rows)
    antisymmetric = antisymmetric.reshape(2, groups * modes, members, 3, lat_rows)
    sym_spec, anti_spec = sent_together((symmetric, antisymmetric), BAND, 1, 4, 0)
    spec_even = jnp.einsum(
        "cmefl,mlj->cmefj", sym_spec, legendre[:, :, :half], preferred_element_type=jnp.float32
    )
    spec_odd = jnp.einsum(
        "cmefl,mlj->cmefj", anti_spec, legendre[:, :, half:], preferred_element_type=jnp.float32
    )
    nonlinear = jnp.concatenate([spec_even, spec_odd], axis=-1)
    rate = damping[None, :, None]
    force = nonlinear - rate * spec
    quad_column = lax.dynamic_slice_in_dim(quadrature, node, 1, 1)[:, 0]
    mixed = lax.psum_scatter(
        quad_column[:, None, None, None, None, None] * force[None],
        "node",
        scatter_dimension=0,
        tiled=True,
    )[0]
    diag = lax.dynamic_slice(quadrature, (node, node), (1, 1))[0, 0]
    updated = (state0 + mixed + diag * rate * spec) / (1.0 + diag * rate)
    change = jnp.sum((updated - spec) ** 2, axis=(0, 1, 2, 4))
    base_local = jnp.sum(state0 * state0, axis=(0, 1, 2, 4))
    total, base_sum = (by_axis(change, NODE_BAND), by_axis(base_local, NODE_BAND))
    ratio = jnp.sqrt(total / (base_sum + 1e-06))
    return (updated[None], ratio)


def solution(mesh):
    torus = Mesh(
        mesh.devices.reshape(mesh.shape["node"], 4, 4, 2), ("node", "band_0", "band_1", "band_2")
    )
    return jax.shard_map(
        body,
        mesh=torus,
        in_specs=(
            P(None, BAND, None, None, None),
            P("node", None, BAND, None, None, None),
            P(BAND, None, None),
            P(),
            P(),
            P(BAND, None, None),
            P(),
        ),
        out_specs=(P("node", None, BAND, None, None, None), P()),
        check_vma=False,
    )
```

profile of v0, /device:TPU:1, one launch (start us, length us, event | category | flops | bytes accessed | tf_op | source)
XLA Modules:
  0.0 538.1 jit_solution(6900981438979276351)
XLA Ops:
  8.9 5.9 %fusion.52 = f32[2,32,4,3,512]{4,2,3,0,1:T(4,128)S(1)} fusion(bf16[32,512,512]{2,1,0:T(8,128)(2,1)} %param.9, bf16[2,32,4,3,512]{4,2,3,0,1:T(4,128)(2,1)S(1)} %bitcast.165), kind=kOutput, calls=%fused_computation.75 | convolution fusion | flops 201326592 | bytes 10354688 | tf_op jit(solution)/shard_map/cmefj,mlj->cmefl/dot_general | solution.py:67
  14.8 5.9 %fusion.55 = f32[2,32,4,3,512]{4,2,3,0,1:T(4,128)S(1)} fusion(bf16[32,512,512]{2,1,0:T(8,128)(2,1)} %param.9, bf16[2,32,4,3,512]{4,2,3,0,1:T(4,128)(2,1)S(1)} %bitcast.166), kind=kOutput, calls=%fused_computation.76 | convolution fusion | flops 201326592 | bytes 10354688 | tf_op jit(solution)/shard_map/cmefj,mlj->cmefl/dot_general | solution.py:61
  21.5 9.6 %copy.69 = f32[4,32,4,3,512]{1,2,3,0,4:T(4,128)} copy(f32[4,32,4,3,512]{4,2,3,0,1:T(4,128)S(1)} %pad_maximum_fusion) | data formatting | bytes 6291456 | tf_op jit(solution)/shard_map/concatenate | solution.py:19
  31.1 12.3 %reshape.338 = f32[32,1,24576]{2,1,0:T(1,128)} reshape(f32[512,4,3,4,32]{4,3,2,1,0:T(4,128)} %bitcast.160) | data formatting | bytes 6291456
  43.4 9.2 %all-to-all-start = ((f32[32,1,24576]{2,1,0:T(1,128)}), f32[32,1,24576]{2,1,0:T(1,128)S(1)}, u32[]{:S(2)}, u32[]{:S(2)}) async-start(f32[32,1,24576]{2,1,0:T(1,128)} %reshape.338), calls=%async_computation | async-start | bytes 6291456 | tf_op jit(solution)/shard_map/all_to_all | solution.py:22
  52.6 34.9 %multiply_bitcast_fusion.1 = (f32[1,1024,1,2048]{3,1,2,0:T(8,128)}, f32[1,1024,1,2048]{3,1,2,0:T(8,128)}) fusion(f32[1024]{0:T(1024)S(1)} %multiply_negate_fusion), kind=kLoop, calls=%fused_computation.28 | loop fusion | flops 33554432 | bytes 16781312 | tf_op jit(solution)/shard_map/stack | solution.py:43
  88.3 11.8 %fusion.3 = f32[2,1024,1,2048]{3,1,0,2:T(8,128)} fusion(f32[1,1024,1,2048]{3,1,2,0:T(8,128)} %get-tuple-element.34, f32[1,1024,1,2048]{3,1,2,0:T(8,128)} %get-tuple-element.33), kind=kLoop, calls=%fused_computation.6 | loop fusion | flops 8388608 | bytes 33554432 | tf_op jit(solution)/shard_map/mul | solution.py:43
  100.1 32.8 %fusion.31 = (f32[1,1024,1,2048]{3,1,0,2:T(8,128)S(1)}, f32[1,1024,1,2048]{3,1,0,2:T(8,128)S(1)}) fusion(), kind=kLoop, calls=%fused_computation.41 | loop fusion | flops 31457280 | bytes 16777216 | tf_op jit(solution)/shard_map/stack | solution.py:42
  133.0 6.1 %maximum_multiply_fusion = f32[2,1024,1,2048]{3,1,0,2:T(8,128)} fusion(f32[1,1024,1,2048]{3,1,0,2:T(8,128)S(1)} %get-tuple-element.36, f32[1,1024,1,2048]{3,1,0,2:T(8,128)S(1)} %get-tuple-element.35), kind=kLoop, calls=%fused_computation.4 | loop fusion | flops 8388608 | bytes 33554432 | tf_op jit(solution)/shard_map/mul | solution.py:42
  139.1 34.6 %fusion.29 = (f32[1,1024,2048]{2,1,0:T(8,128)}, f32[1,1024,2048]{2,1,0:T(8,128)}) fusion(), kind=kLoop, calls=%fused_computation.39 | loop fusion | flops 31457280 | bytes 16777216 | tf_op jit(solution)/shard_map/cos | solution.py:38
  174.2 11.1 %reduce.2 = f32[32,24576]{1,0:T(8,128)} reduce(f32[32,1,24576]{2,1,0:T(1,128)S(1)} %all-to-all-done, f32[]{:T(128)} %broadcast.391), dimensions={1}, to_apply=%all_to_all.22.reduce_sub_computation | reduce | bytes 6291460 | tf_op jit(solution)/shard_map/all_to_all | solution.py:22
  185.3 9.6 %reshape.339 = f32[512,4,3,4,32]{4,3,2,1,0:T(4,128)} reshape(f32[32,24576]{1,0:T(8,128)} %reduce.2) | data formatting | bytes 6291456
  194.9 13.1 %copy.70 = f32[4,32,4,3,512]{1,4,3,2,0:T(8,128)} copy(f32[4,32,4,3,512]{1,2,3,0,4:T(4,128)} %bitcast.159) | data formatting | bytes 6291456 | tf_op jit(solution)/shard_map/all_to_all | solution.py:22
  208.0 8.6 %slice_add_fusion = (f32[2,32,32,4,3,16]{2,5,1,4,3,0:T(8,128)S(1)}, f32[2,32,32,4,3,16]{2,5,1,4,3,0:T(8,128)}) fusion(f32[4,32,32,4,3,16]{2,5,1,4,3,0:T(8,128)} %bitcast.156), kind=kLoop, calls=%fused_computation.37 | loop fusion | flops 786432 | bytes 6291456 | tf_op jit(solution)/shard_map/add | solution.py:79
  221.5 5.0 add.152
  226.5 7.8 %copy.72 = f32[2,32,32,4,3,16]{2,1,5,0,4,3:T(8,128)} copy(f32[2,32,32,4,3,16]{2,5,1,4,3,0:T(8,128)} %get-tuple-element.23) | data formatting | bytes 3145728 | tf_op jit(solution)/shard_map/sub | solution.py:79
  234.3 5.4 %sub.50 = f32[2,1,1024,4,3,1,16]{2,6,0,5,4,3,1:T(8,128)S(1)} reshape(f32[2,32,32,4,3,16]{2,1,5,0,4,3:T(8,128)} %copy.72) | data formatting | bytes 3145728 | tf_op jit(solution)/shard_map/sub | solution.py:79
  239.7 45.1 %fusion.32 = f32[1,4,3,2,16,2,2048]{6,4,5,3,2,1,0:T(8,128)S(1)} fusion(f32[2,1024,1,2048]{3,1,0,2:T(8,128)} %fusion.3, f32[2,1024,1,2048]{3,1,0,2:T(8,128)} %maximum_multiply_fusion, f32[2,1,1024,4,3,1,16]{2,6,0,5,4,3,1:T(8,128)S(1)} %sub.50, f32[2,1,1024,4,3,1,16]{2,6,0,5,4,3,1:T(8,128)S(1)} %add.152), kind=kOutput, calls=%fused_computation.42 | convolution fusion | flops 38663880704 | bytes 42991616 | tf_op jit(solution)/shard_map/dot_general | solution.py:80
  286.1 24.2 %fusion.40 = f32[2,1,1024,4,3,2,16]{2,6,0,5,4,3,1:T(8,128)S(1)} fusion(f32[1,1024,2048]{2,1,0:T(8,128)} %get-tuple-element.38, f32[1,1024,2048]{2,1,0:T(8,128)} %get-tuple-element.37, f32[1,4,1,2,16,2048]{5,4,3,2,1,0:T(8,128)S(1)} %get-tuple-element.28, f32[1,4,1,2,16,2048]{5,4,3,2,1,0:T(8,128)S(1)} %get-tuple-element.25, ...), kind=kOutput, calls=%fused_computation.56 | convolution fusion | flops 19337314304 | bytes 23068672 | tf_op jit(solution)/shard_map/cmk,qefhlk->cqmefhl/dot_general | solution.py:93
  311.1 15.5 %copy.79 = bf16[4,1024,4,3,16]{4,0,3,2,1:T(4,128)(2,1)} copy(bf16[4,1024,4,3,16]{1,4,0,3,2:T(8,128)(2,1)S(1)} %pad_maximum_fusion.1) | data formatting | bytes 3145728 | tf_op jit(solution)/shard_map/concatenate | solution.py:19
  326.7 18.1 %reshape.340 = bf16[32,2,12288]{2,1,0:T(2,128)(2,1)} reshape(bf16[1024,4,3,4,16]{4,3,2,1,0:T(4,128)(2,1)} %bitcast.157) | data formatting | bytes 3145728
  344.7 7.4 %all-to-all-start.1 = ((bf16[32,2,12288]{2,1,0:T(2,128)(2,1)}), bf16[32,2,12288]{2,1,0:T(2,128)(2,1)S(1)}, u32[]{:S(2)}, u32[]{:S(2)}) async-start(bf16[32,2,12288]{2,1,0:T(2,128)(2,1)} %reshape.340), calls=%async_computation.1 | async-start | bytes 3145728 | tf_op jit(solution)/shard_map/all_to_all | solution.py:22
  352.5 22.3 %all-to-all-done.1 = bf16[32,2,12288]{2,1,0:T(2,128)(2,1)S(1)} async-done(((bf16[32,2,12288]{2,1,0:T(2,128)(2,1)}), bf16[32,2,12288]{2,1,0:T(2,128)(2,1)S(1)}, u32[]{:S(2)}, u32[]{:S(2)}) %all-to-all-start.1) | async-done | bytes 1572896 | tf_op jit(solution)/shard_map/all_to_all | solution.py:22
  374.8 10.4 %reshape.341 = bf16[1024,4,3,4,16]{4,3,2,1,0:T(4,128)(2,1)} reshape(bf16[32,2,12288]{2,1,0:T(2,128)(2,1)S(1)} %all-to-all-done.1) | data formatting | bytes 3145728
  385.1 18.2 %copy.80 = bf16[4,32,32,4,3,16]{2,5,1,4,3,0:T(8,128)(2,1)} copy(bf16[4,32,32,4,3,16]{5,0,4,3,2,1:T(4,128)(2,1)} %bitcast.158) | data formatting | bytes 3145728 | tf_op jit(solution)/shard_map/all_to_all | solution.py:22
  403.3 6.0 %fusion.76 = (bf16[2,32,4,3,32,16]{1,5,4,3,2,0:T(8,128)(2,1)}, bf16[2,32,4,3,32,16]{1,5,4,3,2,0:T(8,128)(2,1)S(1)}) fusion(bf16[4,32,4,3,32,16]{1,5,4,3,2,0:T(8,128)(2,1)} %bitcast.161), kind=kLoop, calls=%fused_computation.100 | loop fusion | bytes 3145728 | tf_op jit(solution)/shard_map/split | solution.py:21
  411.8 5.2 fusion.58
  433.5 60.1 %reduce-scatter.2.cloned.1.call-done = f32[1,2,32,4,3,512]{5,2,4,3,1,0:T(8,128)} async-done(((f32[4,2,32,4,3,512]{5,2,4,3,1,0:T(8,128)}), f32[1,2,32,4,3,512]{5,2,4,3,1,0:T(8,128)}) %reduce-scatter.2.cloned.1.call-update) | async-done | bytes 1572880 | tf_op jit(solution)/shard_map/reduce_scatter | solution.py:109
  498.4 6.4 %all-reduce.2 = (f32[3]{0:T(128)S(1)}, f32[3]{0:T(128)S(1)}) all-reduce(f32[3]{0:T(128)S(1)} %get-tuple-element.18, f32[3]{0:T(128)S(1)} %multiply_reduce_fusion), channel_id=1, replica_groups=mesh['node'=4,'band_0'=4,'band_1'=4,'band_2'=2] {'node'}, use_global_device_ids=true, to_apply=%region_2.3 | all-reduce | flops 6 | bytes 48 | tf_op jit(solution)/shard_map/psum | solution.py:30
  504.9 8.7 %all-reduce.1 = (f32[3]{0:T(128)S(1)}, f32[3]{0:T(128)S(1)}) all-reduce(f32[3]{0:T(128)S(1)} %get-tuple-element.14, f32[3]{0:T(128)S(1)} %get-tuple-element.15), channel_id=1, replica_groups=mesh['node'=4,'band_0'=4,'band_1'=4,'band_2'=2] {'band_0'}, use_global_device_ids=true, to_apply=%region_3.4 | all-reduce | flops 6 | bytes 48 | tf_op jit(solution)/shard_map/psum | solution.py:30
  513.6 8.4 %all-reduce = (f32[3]{0:T(128)S(1)}, f32[3]{0:T(128)S(1)}) all-reduce(f32[3]{0:T(128)S(1)} %get-tuple-element.12, f32[3]{0:T(128)S(1)} %get-tuple-element.13), channel_id=1, replica_groups=mesh['node'=4,'band_0'=4,'band_1'=4,'band_2'=2] {'band_1'}, use_global_device_ids=true, to_apply=%region_4.5 | all-reduce | flops 6 | bytes 48 | tf_op jit(solution)/shard_map/psum | solution.py:30
  522.0 8.5 %all-reduce.3 = (f32[3]{0:T(128)S(1)}, f32[3]{0:T(128)S(1)}) all-reduce(f32[3]{0:T(128)S(1)} %get-tuple-element.10, f32[3]{0:T(128)S(1)} %get-tuple-element.11), channel_id=1, replica_groups=mesh['node'=4,'band_0'=4,'band_1'=4,'band_2'=2] {'band_2'}, use_global_device_ids=true, to_apply=%region_5.6 | all-reduce | flops 6 | bytes 48 | tf_op jit(solution)/shard_map/psum | solution.py:30
  (44 shorter events, 35.5 us)
Async XLA Ops:
  7.2 80.3 %copy-start = (f32[2,512]{1,0:T(2,128)S(1)}, f32[2,512]{1,0:T(2,128)}, u32[]{:S(2)}) copy-start(f32[2,512]{1,0:T(2,128)} %param.11) | copy-start | bytes 12292
  43.4 130.3 %all-to-all-start = ((f32[32,1,24576]{2,1,0:T(1,128)}), f32[32,1,24576]{2,1,0:T(1,128)S(1)}, u32[]{:S(2)}, u32[]{:S(2)}) async-start(f32[32,1,24576]{2,1,0:T(1,128)} %reshape.338), calls=%async_computation | async-start | bytes 6291456 | tf_op jit(solution)/shard_map/all_to_all | solution.py:22
  326.7 25.5 %copy-start.4 = (f32[32,3,512]{2,0,1:T(8,128)S(1)}, f32[32,3,512]{2,0,1:T(8,128)}, u32[]{:S(2)}) copy-start(f32[32,3,512]{2,0,1:T(8,128)} %param.12) | copy-start | bytes 589828
  326.7 25.7 %copy-start.6 = (f32[4,4]{1,0:T(4,128)S(1)}, f32[4,4]{1,0:T(4,128)}, u32[]{:S(2)}) copy-start(f32[4,4]{1,0:T(4,128)} %param.13) | copy-start | bytes 196
  344.7 30.1 %all-to-all-start.1 = ((bf16[32,2,12288]{2,1,0:T(2,128)(2,1)}), bf16[32,2,12288]{2,1,0:T(2,128)(2,1)S(1)}, u32[]{:S(2)}, u32[]{:S(2)}) async-start(bf16[32,2,12288]{2,1,0:T(2,128)(2,1)} %reshape.340), calls=%async_computation.1 | async-start | bytes 3145728 | tf_op jit(solution)/shard_map/all_to_all | solution.py:22
  352.1 141.5 %reduce-scatter.2.cloned.1.call-start = ((), (), s32[]{:S(2)}) async-start(), calls=%async_computation.3 | async-start | bytes 7864320 | tf_op jit(solution)/shard_map/reduce_scatter | solution.py:109
  416.9 8.5 %copy-start.2 = (f32[1,2,32,4,3,512]{5,3,4,2,1,0:T(4,128)S(1)}, f32[1,2,32,4,3,512]{5,3,4,2,1,0:T(4,128)}, u32[]{:S(2)}) copy-start(f32[1,2,32,4,3,512]{5,3,4,2,1,0:T(4,128)} %param.8) | copy-start | bytes 4718596
  426.1 5.2 copy-start.5
  427.1 6.0 %copy-start.3 = (f32[2,32,4,3,512]{4,2,3,1,0:T(4,128)S(1)}, f32[2,32,4,3,512]{4,2,3,1,0:T(4,128)}, u32[]{:S(2)}) copy-start(f32[2,32,4,3,512]{4,2,3,1,0:T(4,128)} %param.7) | copy-start | bytes 4718596
  430.7 100.3 %copy-start.1 = (f32[2,512]{1,0:T(2,128)S(1)}, f32[2,512]{1,0:T(2,128)}, u32[]{:S(2)}) copy-start(f32[2,512]{1,0:T(2,128)} %param.11) | copy-start | bytes 12292
Sparse Core Ops, SparseCore 0:
  430.9 62.6 reduce-scatter.1
where the time goes:
time: 544 us; the launch traced here: 538 us
  other arithmetic  152 us (28%)
  local copies, waits for them, and re-layouts  150 us (28%)
  matrix products  91.2 us (17%)
  waiting for transfers between devices  82.4 us (15%)
  blocking collectives  32.1 us (6%)
  starting transfers between devices  16.6 us (3%)
  between operations  14.6 us (3%)
    reduce_scatter x1, waiting for transfers between devices, body(): lax.psum_scatter(quad_column[:, None, None, None, None, None] * force[Non...  60.1 us
    unnamed x21, local copies, waits for them, and re-layouts  53.6 us
    dot_general x1, matrix products, body(): lax.dot_general(fourier, backward, (((0, 2), (0, 1)), ((), ())), precisio...  45.1 us
    another operation x1, other arithmetic, transform_tables(): slope_table = jnp.stack([-ratio * sine, -ratio * cosine], axis=0) * scale  34.9 us
    cos x1, other arithmetic, transform_tables(): cosine = jnp.cos(angle)  34.6 us
    another operation x1, other arithmetic, transform_tables(): forward = jnp.stack([cosine, -sine], axis=0) * scale  32.8 us
    psum x4, blocking collectives, by_axis(): return functools.reduce(lax.psum, axes, shard)  32.1 us
    all_to_all x3, local copies, waits for them, and re-layouts, sent_together(): lax.all_to_all(both, axis, split_axis=split_dim, concat_axis=concat_dim,...  31.8 us
  transfers between devices with their start and end apart: 3, of which 2 were waited for; matrix products, arithmetic and copies ran while one was open for 23% of the time, Pallas kernels for 0%

commit v1 on v0

v1 whole, which is shorter than its diff:
```python
import functools
import math

import jax
import jax.numpy as jnp
import numpy as np
from jax import lax
from jax.experimental import pallas as pl
from jax.experimental.pallas import tpu as pltpu
from jax.sharding import Mesh
from jax.sharding import PartitionSpec as P

BAND = ("band_0", "band_1", "band_2")
MODES = 1024
POINTS = 2 * MODES
HALF = MODES // 2
QUARTER = POINTS // 4
ROWS = QUARTER + 16
LATS = 512
DEGREES = 512
NBAND = 32
PAIRS = 16
COLS = 24
LANES = 384
MB = 4
MIB = 1 << 20

NT = (((1,), (1,)), ((), ()))


def mm(a, b):
    return jnp.dot(a, b, preferred_element_type=jnp.float32)


def swap_groups(arrays, lane):
    for step in range(3):
        width = 16 << step
        low = (lane & width) == 0
        out = list(arrays)
        for i in range(8):
            if not i & (1 << step):
                j = i | (1 << step)
                a, b = arrays[i], arrays[j]
                out[i] = jnp.where(low, a, pltpu.roll(b, width, 1))
                out[j] = jnp.where(low, pltpu.roll(a, 128 - width, 1), b)
        arrays = out
    return arrays


def synthesis_kernel(it_ref, leg_ref, out_ref, coef_ref, wide_ref):
    step = pl.program_id(0)
    for k in range(MB):
        for c in range(2):
            for e in range(4):
                coef_ref[k, pl.ds((c * 4 + e) * 3, 3), :] = it_ref[c, k, e]
        coeff = coef_ref[k].astype(jnp.bfloat16)
        table = leg_ref[k]
        even = lax.dot_general(
            coeff[:, :256], table[:, :256], NT, preferred_element_type=jnp.float32
        )
        odd = lax.dot_general(
            coeff[:, 256:], table[:, 256:], NT, preferred_element_type=jnp.float32
        )
        at = step * MB + k
        for t in range(4):
            cut = slice(128 * t, 128 * (t + 1))
            wide_ref[0, t, pl.ds(at, COLS, stride=PAIRS), :] = (even + odd)[:, cut]
            wide_ref[1, t, pl.ds(at, COLS, stride=PAIRS), :] = (even - odd)[:, cut]

    @pl.when(step == pl.num_programs(0) - 1)
    def _():
        lane = lax.broadcasted_iota(jnp.int32, (PAIRS, 128), 1)
        for c in range(2):
            for f in range(3):
                for t in range(4):
                    parts = [
                        wide_ref[h, t, pl.ds(((c * 4 + e) * 3 + f) * PAIRS, PAIRS), :]
                        for h in range(2)
                        for e in range(4)
                    ]
                    for g, part in enumerate(swap_groups(parts, lane)):
                        out_ref[
                            8 * t + g, pl.ds(c * PAIRS, PAIRS), pl.ds(128 * f, 128)
                        ] = part.astype(jnp.bfloat16)


def synthesis(it6, leg4, par):
    return pl.pallas_call(
        synthesis_kernel,
        grid=(PAIRS // MB,),
        in_specs=[
            pl.BlockSpec((2, MB, None, 4, 3, DEGREES), lambda i: (0, i, par, 0, 0, 0)),
            pl.BlockSpec((MB, None, LATS, DEGREES), lambda i: (i, par, 0, 0)),
        ],
        out_specs=pl.BlockSpec((NBAND, 2 * PAIRS, LANES), lambda i: (0, 0, 0)),
        out_shape=jax.ShapeDtypeStruct((NBAND, 2 * PAIRS, LANES), jnp.bfloat16),
        scratch_shapes=[
            pltpu.VMEM((MB, COLS, DEGREES), jnp.float32),
            pltpu.VMEM((2, 4, COLS * PAIRS, 128), jnp.float32),
        ],
        compiler_params=pltpu.CompilerParams(vmem_limit_bytes=24 * MIB),
        cost_estimate=pl.CostEstimate(
            flops=2 * PAIRS * COLS * LATS * DEGREES, bytes_accessed=11 * MIB, transcendentals=0
        ),
        name="synthesis",
    )(it6, leg4)


def split(x):
    high = x.astype(jnp.bfloat16)
    return high, (x - high.astype(jnp.float32)).astype(jnp.bfloat16)


def table_kernel(row1_ref, row2_ref, col1_ref, col2_ref, tab_ref, back_ref):
    for par in range(2):
        wave = (
            2 * lax.broadcasted_iota(jnp.int32, (1, HALF), 1) + par
        ).astype(jnp.float32) * (1.0 / MODES)

        def rows(j, _, par=par, wave=wave):
            lead_c = row1_ref[par, 0, pl.ds(j, 1), :]
            lead_s = row1_ref[par, 1, pl.ds(j, 1), :]
            cosine = lead_c * row2_ref[par, 0] - lead_s * row2_ref[par, 1]
            sine = lead_s * row2_ref[par, 0] + lead_c * row2_ref[par, 1]
            at = pl.ds(pl.multiple_of(16 * j, 16), 16)
            for t, value in enumerate((cosine, sine, -wave * cosine, wave * sine)):
                high, low = split(value)
                tab_ref[4 * par + t, 0, at, :] = high
                tab_ref[4 * par + t, 1, at, :] = low
            return 0

        lax.fori_loop(0, ROWS // 16, rows, 0)
        for block in range(4):
            lead_c = col1_ref[par, 0, :, pl.ds(block, 1)]
            lead_s = col1_ref[par, 1, :, pl.ds(block, 1)]
            cosine = lead_c * col2_ref[par, 0] - lead_s * col2_ref[par, 1]
            sine = lead_s * col2_ref[par, 0] + lead_c * col2_ref[par, 1]
            if block == 0:
                first = lax.broadcasted_iota(jnp.int32, (1, 128), 1) == 0
                halve = jnp.where(first, 0.5, 1.0)
                cosine, sine = cosine * halve, sine * halve
            for t, value in enumerate((cosine, -sine)):
                high, low = split(value)
                back_ref[2 * par + t, 0, :, pl.ds(128 * block, 128)] = high
                back_ref[2 * par + t, 1, :, pl.ds(128 * block, 128)] = low


def small_tables():
    scale = 1.0 / math.sqrt(MODES)
    step = 2.0 * math.pi / POINTS
    rows1, rows2, cols1, cols2 = [], [], [], []
    for par in range(2):
        m = 2 * np.arange(HALF) + par

        def pair(k, factor):
            angle = ((k[:, None] * m[None, :]) % POINTS) * step
            return np.stack([np.cos(angle), np.sin(angle)]) * factor

        rows1.append(pair(16 * np.arange(ROWS // 16), 1.0))
        rows2.append(pair(np.arange(16), scale))
        cols1.append(pair(128 * np.arange(4), 1.0).transpose(0, 2, 1))
        cols2.append(pair(np.arange(128), scale).transpose(0, 2, 1))
    return [np.stack(x).astype(np.float32) for x in (rows1, rows2, cols1, cols2)]


def tables(parts):
    return pl.pallas_call(
        table_kernel,
        out_shape=(
            jax.ShapeDtypeStruct((8, 2, ROWS, HALF), jnp.bfloat16),
            jax.ShapeDtypeStruct((4, 2, HALF, QUARTER), jnp.bfloat16),
        ),
        compiler_params=pltpu.CompilerParams(vmem_limit_bytes=24 * MIB),
        cost_estimate=pl.CostEstimate(
            flops=16 * ROWS * HALF, bytes_accessed=15 * MIB, transcendentals=0
        ),
        name="tables",
    )(*parts)


def grid_kernel(
    xe_ref, xo_ref, tab_ref, back_ref, cor_ref, weight_ref,
    ye_ref, yo_ref,
    x_ref, wave_ref, high_ref, low_ref, edge_ref,
):
    for par, ref in enumerate((xe_ref, xo_ref)):
        for c in range(2):
            x_ref[2 * par + c] = ref[:, c * PAIRS : (c + 1) * PAIRS, :].reshape(HALF, LANES)
    which = (0, 1, 1, 0)
    for t in range(8):
        x = x_ref[4 * (t // 4) // 2 + which[t % 4]]
        wave_ref[t] = mm(tab_ref[t, 0], x) + mm(tab_ref[t, 1], x)
    cor = cor_ref[...]

    def quads(base, at, lanes):
        ce, se = wave_ref[base, at, lanes], wave_ref[base + 1, at, lanes]
        co, so = wave_ref[base + 4, at, lanes], wave_ref[base + 5, at, lanes]
        a, b, s, d = ce + co, ce - co, se + so, se - so
        return a - s, b + d, b - d, a + s

    def tendency(at):
        cuts = [pl.ds(128 * f, 128) for f in range(3)]
        values = [quads(0, at, cut) for cut in cuts]
        slopes = [quads(2, at, cut) for cut in cuts]
        out = [[], [], []]
        for q in range(4):
            u, v, h = (values[f][q] for f in range(3))
            us, vs, hs = (slopes[f][q] for f in range(3))
            out[0].append(cor * v - u * us - hs)
            out[1].append(-u * vs - cor * u)
            out[2].append(-u * hs - (1.0 + h) * us)
        folded = []
        for t1, t2, t3, t4 in out:
            a, b, c, d = t1 + t4, t2 + t3, t1 - t4, t3 - t2
            folded.append((a + b, c + d, a - b, c - d))
        return folded

    def block(j, _):
        at = pl.ds(pl.multiple_of(16 * j, 16), 16)
        for f, folded in enumerate(tendency(at)):
            for i, value in enumerate(folded):
                high, low = split(value)
                high_ref[i, at, pl.ds(128 * f, 128)] = high
                low_ref[i, at, pl.ds(128 * f, 128)] = low
        return 0

    lax.fori_loop(0, QUARTER // 16, block, 0)
    for f, folded in enumerate(tendency(pl.ds(QUARTER, 16))):
        edge_ref[0, :, pl.ds(128 * f, 128)] = folded[0]
        edge_ref[1, :, pl.ds(128 * f, 128)] = folded[3]

    odd_row = (lax.broadcasted_iota(jnp.int32, (HALF, 1), 0) & 1) == 1
    half_scale = 0.5 / math.sqrt(MODES)
    sign = jnp.where(odd_row, -half_scale, half_scale)
    lane = lax.broadcasted_iota(jnp.int32, (1, 128), 1)
    weight = weight_ref[...]
    signed = jnp.where(lane < 64, weight, -weight)
    for i in range(4):
        out = mm(back_ref[i, 0], high_ref[i]) + mm(back_ref[i, 1], high_ref[i])
        out = out + mm(back_ref[i, 0], low_ref[i])
        if i == 0:
            out = out + sign * edge_ref[0, 0:1, :]
        if i == 3:
            out = out - sign * edge_ref[1, 0:1, :]
        ref, c = (ye_ref, yo_ref)[i // 2], i % 2
        for f in range(3):
            part = out[:, 128 * f : 128 * (f + 1)]
            both = pltpu.roll(part, 64, 1) * weight + part * signed
            ref[:, c * PAIRS : (c + 1) * PAIRS, 128 * f : 128 * (f + 1)] = both.astype(
                jnp.bfloat16
            ).reshape(NBAND, PAIRS, 128)


def grid_stage(xe, xo, tab, back, cor, weight):
    shape = jax.ShapeDtypeStruct((NBAND, 2 * PAIRS, LANES), jnp.bfloat16)
    return pl.pallas_call(
        grid_kernel,
        out_shape=(shape, shape),
        scratch_shapes=[
            pltpu.VMEM((4, HALF, LANES), jnp.bfloat16),
            pltpu.VMEM((8, ROWS, LANES), jnp.float32),
            pltpu.VMEM((4, QUARTER, LANES), jnp.bfloat16),
            pltpu.VMEM((4, QUARTER, LANES), jnp.bfloat16),
            pltpu.VMEM((2, 16, LANES), jnp.float32),
        ],
        compiler_params=pltpu.CompilerParams(vmem_limit_bytes=48 * MIB),
        cost_estimate=pl.CostEstimate(
            flops=2 * 28 * ROWS * HALF * LANES, bytes_accessed=17 * MIB, transcendentals=0
        ),
        name="grid",
    )(xe, xo, tab, back, cor, weight)


def analysis_kernel(y_ref, leg_ref, it_ref, st_ref, damp_ref, out_ref, wide_ref, lin_ref, pair_ref):
    step = pl.program_id(0)

    @pl.when(step == 0)
    def _():
        lane = lax.broadcasted_iota(jnp.int32, (PAIRS, 128), 1)
        for c in range(2):
            for f in range(3):
                for t in range(4):
                    parts = [
                        y_ref[
                            8 * t + g, pl.ds(c * PAIRS, PAIRS), pl.ds(128 * f, 128)
                        ].astype(jnp.float32)
                        for g in range(8)
                    ]
                    for i, part in enumerate(swap_groups(parts, lane)):
                        row = ((c * 4 + i % 4) * 3 + f) * PAIRS
                        wide_ref[i // 4, t, pl.ds(row, PAIRS), :] = part

    for k in range(MB):
        rate = damp_ref[k]
        for c in range(2):
            for e in range(4):
                lin_ref[k, pl.ds((c * 4 + e) * 3, 3), :] = rate * (it_ref[c, k, e] - st_ref[c, k, e])
        at = step * MB + k
        for h in range(2):
            spec = jnp.concatenate(
                [wide_ref[h, t, pl.ds(at, COLS, stride=PAIRS), :] for t in range(4)], axis=1
            ).astype(jnp.bfloat16)
            cut = slice(256 * h, 256 * (h + 1))
            pair_ref[pl.ds(COLS * k, COLS), cut] = (
                mm(spec, leg_ref[k, :, cut]) - lin_ref[k, :, cut]
            )
    out_ref[...] = pair_ref[...].astype(jnp.bfloat16)


def analysis(y, leg4, it6, st6, damp4, par):
    state = pl.BlockSpec((2, MB, None, 4, 3, DEGREES), lambda i: (0, i, par, 0, 0, 0))
    return pl.pallas_call(
        analysis_kernel,
        grid=(PAIRS // MB,),
        in_specs=[
            pl.BlockSpec((NBAND, 2 * PAIRS, LANES), lambda i: (0, 0, 0)),
            pl.BlockSpec((MB, None, LATS, DEGREES), lambda i: (i, par, 0, 0)),
            state,
            state,
            pl.BlockSpec((MB, None, 3, DEGREES), lambda i: (i, par, 0, 0)),
        ],
        out_specs=pl.BlockSpec((MB * COLS, DEGREES), lambda i: (i, 0)),
        out_shape=jax.ShapeDtypeStruct((PAIRS * COLS, DEGREES), jnp.bfloat16),
        scratch_shapes=[
            pltpu.VMEM((2, 4, COLS * PAIRS, 128), jnp.float32),
            pltpu.VMEM((MB, COLS, DEGREES), jnp.float32),
            pltpu.VMEM((MB * COLS, DEGREES), jnp.float32),
        ],
        compiler_params=pltpu.CompilerParams(vmem_limit_bytes=24 * MIB),
        cost_estimate=pl.CostEstimate(
            flops=2 * PAIRS * COLS * LATS * DEGREES, bytes_accessed=13 * MIB, transcendentals=0
        ),
        name="analysis",
    )(y, leg4, it6, st6, damp4)


def update_kernel(
    quad_ref, own0, own1, up0, up1, dn0, dn1, fa0, fa1, fb0, fb1,
    st_ref, it_ref, damp_ref, out_ref, sums_ref, mix_ref, acc_ref,
):
    step = pl.program_id(0)
    w_own, w_up, w_dn, w_far = quad_ref[0], quad_ref[1], quad_ref[2], quad_ref[3]
    total, diag = quad_ref[4], quad_ref[5]
    rows = own0.shape[0]

    @pl.when(step == 0)
    def _():
        acc_ref[...] = jnp.zeros_like(acc_ref)

    for par, (own, up, dn, fa, fb) in enumerate(
        ((own0, up0, dn0, fa0, fb0), (own1, up1, dn1, fa1, fb1))
    ):
        near = (
            w_own * own[...].astype(jnp.float32)
            + w_up * up[...].astype(jnp.float32)
            + w_dn * dn[...].astype(jnp.float32)
        )
        far = jnp.where(step < pl.num_programs(0) // 2, fa[...].astype(jnp.float32), fb[...].astype(jnp.float32))
        mix_ref[par] = near + w_far * far

    for k in range(rows // COLS):
        for par in range(2):
            rate = damp_ref[k, par]
            keep = 1.0 - rate * total
            mine = diag * rate
            inverse = 1.0 / (1.0 + mine)
            for c in range(2):
                for e in range(4):
                    start = st_ref[c, k, par, e]
                    old = it_ref[c, k, par, e]
                    mixed = mix_ref[par, pl.ds(COLS * k + (c * 4 + e) * 3, 3), :]
                    new = (start * keep + mixed + mine * old) * inverse
                    out_ref[c, k, par, e] = new
                    acc_ref[0] += (new - old) * (new - old)
                    acc_ref[1] += start * start
    sums_ref[...] = acc_ref[...]


def update(quad, own, up, dn, fa, fb, st6, it6, damp4):
    steps = 4
    mb = PAIRS // steps
    dense = pl.BlockSpec((mb * COLS, DEGREES), lambda i: (i, 0))
    first = pl.BlockSpec((mb * COLS, DEGREES), lambda i: (jnp.minimum(i, steps // 2 - 1), 0))
    second = pl.BlockSpec((mb * COLS, DEGREES), lambda i: (jnp.maximum(i - steps // 2, 0), 0))
    state = pl.BlockSpec((2, mb, 2, 4, 3, DEGREES), lambda i: (0, i, 0, 0, 0, 0))
    return pl.pallas_call(
        update_kernel,
        grid=(steps,),
        in_specs=[pl.BlockSpec(memory_space=pltpu.SMEM)]
        + [dense] * 6
        + [first] * 2
        + [second] * 2
        + [state, state, pl.BlockSpec((mb, 2, 3, DEGREES), lambda i: (i, 0, 0, 0))],
        out_specs=(state, pl.BlockSpec((2, 3, DEGREES), lambda i: (0, 0, 0))),
        out_shape=(
            jax.ShapeDtypeStruct(it6.shape, jnp.float32),
            jax.ShapeDtypeStruct((2, 3, DEGREES), jnp.float32),
        ),
        scratch_shapes=[
            pltpu.VMEM((2, mb * COLS, DEGREES), jnp.float32),
            pltpu.VMEM((2, 3, DEGREES), jnp.float32),
        ],
        compiler_params=pltpu.CompilerParams(vmem_limit_bytes=32 * MIB),
        cost_estimate=pl.CostEstimate(
            flops=20 * 2 * PAIRS * COLS * DEGREES, bytes_accessed=10 * MIB, transcendentals=0
        ),
        name="update",
    )(quad, *own, *up, *dn, *fa, *fb, st6, it6, damp4)


def body(state0, iterate, legendre, lat_weight, coriolis, damping, quadrature):
    node = lax.axis_index("node")
    band = lax.axis_index(BAND)
    lat_rows = LATS // NBAND
    it6 = iterate.reshape(2, PAIRS, 2, 4, 3, DEGREES)
    st6 = state0.reshape(2, PAIRS, 2, 4, 3, DEGREES)
    leg4 = legendre.reshape(PAIRS, 2, LATS, DEGREES)
    damp4 = damping.reshape(PAIRS, 2, 3, DEGREES)

    def exchange(x):
        return lax.all_to_all(x, BAND, split_axis=0, concat_axis=0, tiled=True)

    def shift(x, by):
        return lax.ppermute(x, "node", [(i, (i + by) % 4) for i in range(4)])

    sent = [synthesis(it6, leg4, par) for par in range(2)]
    got = [exchange(x) for x in sent]
    parts = [jnp.asarray(x) for x in small_tables()]
    parts, _ = lax.optimization_barrier((parts, sent))
    tab, back = tables(parts)
    first = band * lat_rows
    cor = lax.dynamic_slice_in_dim(coriolis, first, lat_rows, 1)
    cor = jnp.broadcast_to(cor[:, None, :], (2, 4, lat_rows)).reshape(1, 128)
    weight = lax.dynamic_slice_in_dim(lat_weight, first, lat_rows, 0)
    weight = jnp.broadcast_to(weight[None, :], (8, lat_rows)).reshape(1, 128)
    back_sent = grid_stage(*got, tab, back, cor, weight)
    spectra = [exchange(y) for y in back_sent]
    own = [analysis(spectra[par], leg4, it6, st6, damp4, par) for par in range(2)]
    rows = own[0].shape[0] // 2
    up = [shift(x, 1) for x in own]
    dn = [shift(x, -1) for x in own]
    fa = [shift(x[:rows], 1) for x in up]
    fb = [shift(x[rows:], -1) for x in dn]
    row = lax.dynamic_slice_in_dim(quadrature, node, 1, 0)[0]
    weights = jnp.roll(jnp.concatenate([row, row]), 0)
    pick = lax.dynamic_slice_in_dim(weights, node, 4, 0)
    quad = jnp.stack([pick[0], pick[3], pick[1], pick[2], jnp.sum(row), pick[0]])
    out, sums = update(quad, own, up, dn, fa, fb, st6, it6, damp4)
    partial = jnp.sum(sums, axis=2)
    for axis in ("node",) + BAND:
        partial = lax.psum(partial, axis)
    change, base = partial[0], partial[1]
    ratio = jnp.sqrt(change / (base + 1e-06))
    return (out.reshape(iterate.shape), ratio)


def solution(mesh):
    torus = Mesh(
        mesh.devices.reshape(mesh.shape["node"], 4, 4, 2), ("node", "band_0", "band_1", "band_2")
    )
    return jax.shard_map(
        body,
        mesh=torus,
        in_specs=(
            P(None, BAND, None, None, None),
            P("node", None, BAND, None, None, None),
            P(BAND, None, None),
            P(),
            P(),
            P(BAND, None, None),
            P(),
        ),
        out_specs=(P("node", None, BAND, None, None, None), P()),
        check_vma=False,
    )
```

time: 544 us -> 203 us (0.37)
  other arithmetic: 152 us -> 2.7 us
  local copies, waits for them, and re-layouts: 150 us -> 53.5 us
  matrix products: 91.2 us -> 0 us
  waiting for transfers between devices: 82.4 us -> 4.21 us
  Pallas kernels: 0 us -> 52 us
  blocking collectives: 32.1 us -> 57 us
  starting transfers between devices: 16.6 us -> 31.9 us
  between operations: 14.6 us -> 0.89 us
    dot_general x6 -> x0, matrix products: 91.2 us -> none  [the longest x1 45.1 us: body(): lax.dot_general(fourier, backward, (((0, 2), (0, 1)), ((), ())), precisio...]
    another operation x2 -> x0, other arithmetic: 67.7 us -> none  [the longest x1 34.9 us: transform_tables(): slope_table = jnp.stack([-ratio * sine, -ratio * cosine], axis=0) * scale]
    reduce_scatter x1 -> x0, waiting for transfers between devices: 60.1 us -> none  [body(): lax.psum_scatter(quad_column[:, None, None, None, None, None] * force[Non...]
    pallas_call x0 -> x7, Pallas kernels: none -> 52 us  [the longest x2 16.3 us: synthesis(): pl.pallas_call(synthesis_kernel, grid=(PAIRS // MB,), in_specs=[pl.BlockS...]
    cos x1 -> x0, other arithmetic: 34.6 us -> none  [transform_tables(): cosine = jnp.cos(angle)]
    all_to_all x3 -> x0, local copies, waits for them, and re-layouts: 31.8 us -> none  [sent_together(): lax.all_to_all(both, axis, split_axis=split_dim, concat_axis=concat_dim,...]
    concatenate x2 -> x0, local copies, waits for them, and re-layouts: 25.2 us -> none  [sent_together(): both = jnp.concatenate(arrays, axis=along)]
    mul x4 -> x0, other arithmetic: 22.2 us -> none  [the longest x1 11.8 us: transform_tables(): slope_table = jnp.stack([-ratio * sine, -ratio * cosine], axis=0) * scale]
  transfers between devices with their start and end apart: 3 -> 11, of which waited for: 2 -> 3; matrix products, arithmetic and copies ran while one was open for 23% -> 6% of each run, Pallas kernels for 0% -> 12%
where the time goes in v1:
time: 203 us; the launch traced here: 202 us
  blocking collectives  57 us (28%)
  local copies, waits for them, and re-layouts  53.5 us (26%)
  Pallas kernels  52 us (26%)
  starting transfers between devices  31.9 us (16%)
  waiting for transfers between devices  4.21 us (2%)
  other arithmetic  2.7 us (1%)
    unnamed x42, local copies, waits for them, and re-layouts  44.5 us
    psum x4, blocking collectives, body(): partial = lax.psum(partial, axis)  37.6 us
    all_to_all x3, starting transfers between devices, exchange(): return lax.all_to_all(x, BAND, split_axis=0, concat_axis=0, tiled=True)  19.7 us
    all_to_all x1, blocking collectives, exchange(): return lax.all_to_all(x, BAND, split_axis=0, concat_axis=0, tiled=True)  19.3 us
    pallas_call x2, Pallas kernels, synthesis(): pl.pallas_call(synthesis_kernel, grid=(PAIRS // MB,), in_specs=[pl.BlockS...  16.3 us
    pallas_call x1, Pallas kernels, grid_stage(): pl.pallas_call(grid_kernel, out_shape=(shape, shape), scratch_shapes=[plt...  15.2 us
    pallas_call x2, Pallas kernels, analysis(): pl.pallas_call(analysis_kernel, grid=(PAIRS // MB,), in_specs=[pl.BlockSp...  12.3 us
    ppermute x8, starting transfers between devices, shift(): return lax.ppermute(x, 'node', [(i, (i + by) % 4) for i in range(4)])  12.2 us
  transfers between devices with their start and end apart: 11, of which 3 were waited for; matrix products, arithmetic and copies ran while one was open for 6% of the time, Pallas kernels for 12%

profile of v1, /device:TPU:1, one launch (start us, length us, event | category | flops | bytes accessed | tf_op | source)
XLA Modules:
  0.0 202.2 jit_solution(5390668652073279296)
XLA Ops:
  0.6 2.3 %copy.13 = f32[1,2,32,4,3,512]{5,4,3,2,1,0:T(4,128)S(1)} copy(f32[1,2,32,4,3,512]{5,3,4,2,1,0:T(4,128)} %param.12) | data formatting | bytes 3145728 | tf_op args[1]
  2.9 5.8 %copy-done.1 = bf16[32,512,512]{2,1,0:T(8,128)(2,1)S(1)} copy-done((bf16[32,512,512]{2,1,0:T(8,128)(2,1)S(1)}, bf16[32,512,512]{2,1,0:T(8,128)(2,1)}, u32[]{:S(2)}) %copy-start.1) | copy-done | bytes 16777240
  8.7 8.2 %synthesis.2 = bf16[32,32,384]{2,1,0:T(8,128)(2,1)} custom-call(f32[2,16,2,4,3,512]{5,4,3,2,1,0:T(4,128)S(1)} %bitcast.14, bf16[16,2,512,512]{3,2,1,0:T(8,128)(2,1)S(1)} %bitcast.10), custom_call_target="tpu_custom_call" | custom-call | flops 201326592 | bytes 11534336 | tf_op jit(solution)/shard_map/synthesis/pallas_call | solution.py:88
  16.9 8.6 %all-to-all-start = ((bf16[32,32,384]{2,1,0:T(8,128)(2,1)}), bf16[32,32,384]{2,1,0:T(8,128)(2,1)}, u32[]{:S(2)}, u32[]{:S(2)}) async-start(bf16[32,32,384]{2,1,0:T(8,128)(2,1)} %synthesis.2), calls=%async_computation | async-start | bytes 1572864 | tf_op jit(solution)/shard_map/all_to_all | solution.py:421
  25.5 5.8 %copy-done.2 = bf16[32,512,512]{2,1,0:T(8,128)(2,1)S(1)} copy-done((bf16[32,512,512]{2,1,0:T(8,128)(2,1)S(1)}, bf16[32,512,512]{2,1,0:T(8,128)(2,1)}, u32[]{:S(2)}) %copy-start.2) | copy-done | bytes 16777240
  31.3 8.2 %synthesis.3 = bf16[32,32,384]{2,1,0:T(8,128)(2,1)} custom-call(f32[2,16,2,4,3,512]{5,4,3,2,1,0:T(4,128)S(1)} %bitcast.15, bf16[16,2,512,512]{3,2,1,0:T(8,128)(2,1)S(1)} %bitcast.11), custom_call_target="tpu_custom_call" | custom-call | flops 201326592 | bytes 11534336 | tf_op jit(solution)/shard_map/synthesis/pallas_call | solution.py:88
  39.8 7.2 %all-to-all-start.1 = ((bf16[32,32,384]{2,1,0:T(8,128)(2,1)}), bf16[32,32,384]{2,1,0:T(8,128)(2,1)}, u32[]{:S(2)}, u32[]{:S(2)}) async-start(bf16[32,32,384]{2,1,0:T(8,128)(2,1)} %synthesis.3), calls=%async_computation.1 | async-start | bytes 1572864 | tf_op jit(solution)/shard_map/all_to_all | solution.py:421
  50.2 3.6 %tables.1 = (bf16[8,2,528,512]{3,2,1,0:T(8,128)(2,1)S(1)}, bf16[4,2,512,512]{3,2,1,0:T(8,128)(2,1)S(1)}) custom-call(f32[2,2,33,512]{3,2,1,0:T(8,128)S(1)} %copy-done.13, f32[2,2,16,512]{3,2,1,0:T(8,128)S(1)} %copy-done.14, f32[2,2,512,4]{3,2,1,0:T(8,128)S(1)} %copy-done.10, f32[2,2,512,128]{3,2,1,0:T(8,128)S(1)} %copy-done.11), custom_call_target="tpu_custom_call" | custom-call | flops 4325376 | bytes 15728640 | tf_op jit(solution)/shard_map/tables/pallas_call | solution.py:167
  53.8 3.3 %copy-done.16 = bf16[8,2,528,512]{3,2,1,0:T(8,128)(2,1)} copy-done((bf16[8,2,528,512]{3,2,1,0:T(8,128)(2,1)}, bf16[8,2,528,512]{3,2,1,0:T(8,128)(2,1)S(1)}, u32[]{:S(2)}) %copy-start.16) | copy-done | bytes 8650776
  57.1 2.0 copy-done.17
  59.1 2.2 %all-to-all-done.1.xo_ref = bf16[32,32,384]{2,1,0:T(8,128)(2,1)} async-done(((bf16[32,32,384]{2,1,0:T(8,128)(2,1)}), bf16[32,32,384]{2,1,0:T(8,128)(2,1)}, u32[]{:S(2)}, u32[]{:S(2)}) %all-to-all-start.1) | async-done | bytes 786464 | tf_op jit(solution)/shard_map/all_to_all | solution.py:421
  61.3 15.2 %grid.1 = (bf16[32,32,384]{2,1,0:T(8,128)(2,1)S(1)}, bf16[32,32,384]{2,1,0:T(8,128)(2,1)S(1)}) custom-call(bf16[32,32,384]{2,1,0:T(8,128)(2,1)} %all-to-all-done.xe_ref, bf16[32,32,384]{2,1,0:T(8,128)(2,1)} %all-to-all-done.1.xo_ref, bf16[8,2,528,512]{3,2,1,0:T(8,128)(2,1)} %copy-done.16, bf16[4,2,512,512]{3,2,1,0:T(8,128)(2,1)} %copy-done.17, ...), custom_call_target="tpu_custom_call" | custom-call | flops 5813305344 | bytes 17825792 | tf_op jit(solution)/shard_map/grid/pallas_call | solution.py:256
  76.5 19.3 %all_to_all.20.y_ref = bf16[32,32,384]{2,1,0:T(8,128)(2,1)} all-to-all(bf16[32,32,384]{2,1,0:T(8,128)(2,1)S(1)} %get-tuple-element.19), channel_id=1, replica_groups=mesh['node'=4,'band_0'=4,'band_1'=4,'band_2'=2] {'band_0','band_1','band..., dimensions={0} | all-to-all | bytes 1572864 | tf_op jit(solution)/shard_map/all_to_all | solution.py:421
  95.8 3.8 %all-to-all-start.2 = ((bf16[32,32,384]{2,1,0:T(8,128)(2,1)}), bf16[32,32,384]{2,1,0:T(8,128)(2,1)S(1)}, u32[]{:S(2)}, u32[]{:S(2)}) async-start(bf16[32,32,384]{2,1,0:T(8,128)(2,1)} %copy-done.12), calls=%async_computation.2 | async-start | bytes 1572864 | tf_op jit(solution)/shard_map/all_to_all | solution.py:421
  99.7 2.4 %copy.14 = f32[2,32,4,3,512]{4,3,2,1,0:T(4,128)S(1)} copy(f32[2,32,4,3,512]{4,2,3,1,0:T(4,128)} %param.11) | data formatting | bytes 3145728 | tf_op args[0]
  102.3 6.4 %copy-done.3 = bf16[32,512,512]{2,1,0:T(8,128)(2,1)S(1)} copy-done((bf16[32,512,512]{2,1,0:T(8,128)(2,1)S(1)}, bf16[32,512,512]{2,1,0:T(8,128)(2,1)}, u32[]{:S(2)}) %copy-start.3) | copy-done | bytes 16777240
  108.6 5.8 %analysis.3.own1 = bf16[384,512]{1,0:T(8,128)(2,1)S(1)} custom-call(bf16[32,32,384]{2,1,0:T(8,128)(2,1)S(1)} %copy-done.8, bf16[16,2,512,512]{3,2,1,0:T(8,128)(2,1)S(1)} %bitcast.12, f32[2,16,2,4,3,512]{5,4,3,2,1,0:T(4,128)S(1)} %bitcast.16, f32[2,16,2,4,3,512]{5,4,3,2,1,0:T(4,128)S(1)} %bitcast.19, f32[16,2,3,512]{3,2,1,0:T(4,128)S(1)} %bitcast.22), custom_call_target="tpu_custom_call" | custom-call | flops 201326592 | bytes 13631488 | tf_op jit(solution)/shard_map/analysis/pallas_call | solution.py:312
  114.5 1.7 collective-permute-start.1
  116.2 2.4 %collective-permute-start.3 = (bf16[384,512]{1,0:T(8,128)(2,1)S(1)}, bf16[384,512]{1,0:T(8,128)(2,1)}, u32[]{:S(2)}, u32[]{:S(2)}) collective-permute-start(bf16[384,512]{1,0:T(8,128)(2,1)S(1)} %analysis.3.own1), channel_id=1, source_target_pairs={{0,96},{32,0},{64,32},{96,64},{1,97},{33,1},{65,33},{97,65},{2,98}... | collective-permute-start | bytes 1179656 | tf_op jit(solution)/shard_map/ppermute | solution.py:424
  118.6 5.8 %copy-done.4 = bf16[32,512,512]{2,1,0:T(8,128)(2,1)S(1)} copy-done((bf16[32,512,512]{2,1,0:T(8,128)(2,1)S(1)}, bf16[32,512,512]{2,1,0:T(8,128)(2,1)}, u32[]{:S(2)}) %copy-start.4) | copy-done | bytes 16777240
  126.0 6.5 %analysis.2.own0 = bf16[384,512]{1,0:T(8,128)(2,1)} custom-call(bf16[32,32,384]{2,1,0:T(8,128)(2,1)S(1)} %all-to-all-done.2.y_ref, bf16[16,2,512,512]{3,2,1,0:T(8,128)(2,1)S(1)} %bitcast.13, f32[2,16,2,4,3,512]{5,4,3,2,1,0:T(4,128)S(1)} %bitcast.17, f32[2,16,2,4,3,512]{5,4,3,2,1,0:T(4,128)S(1)} %bitcast.20, f32[16,2,3,512]{3,2,1,0:T(4,128)S(1)} %bitcast.23), custom_call_target="tpu_custom_call" | custom-call | flops 201326592 | bytes 13631488 | tf_op jit(solution)/shard_map/analysis/pallas_call | solution.py:312
  132.5 2.7 %collective-permute-start.2 = (bf16[384,512]{1,0:T(8,128)(2,1)}, bf16[384,512]{1,0:T(8,128)(2,1)S(1)}, u32[]{:S(2)}, u32[]{:S(2)}) collective-permute-start(bf16[384,512]{1,0:T(8,128)(2,1)} %analysis.2.own0), channel_id=1, source_target_pairs={{0,96},{32,0},{64,32},{96,64},{1,97},{33,1},{65,33},{97,65},{2,98}... | collective-permute-start | bytes 1179656 | tf_op jit(solution)/shard_map/ppermute | solution.py:424
  139.7 2.7 %collective-permute-start.7 = (bf16[192,512]{1,0:T(8,128)(2,1)}, bf16[192,512]{1,0:T(8,128)(2,1)}, u32[]{:S(2)}, u32[]{:S(2)}) collective-permute-start(bf16[192,512]{1,0:T(8,128)(2,1)} %slice.42), channel_id=1, source_target_pairs={{0,96},{32,0},{64,32},{96,64},{1,97},{33,1},{65,33},{97,65},{2,98}... | collective-permute-start | bytes 589832 | tf_op jit(solution)/shard_map/ppermute | solution.py:424
  142.3 1.7 collective-permute-done.up0
  145.5 2.7 %collective-permute-start.6 = (bf16[192,512]{1,0:T(8,128)(2,1)}, bf16[192,512]{1,0:T(8,128)(2,1)}, u32[]{:S(2)}, u32[]{:S(2)}) collective-permute-start(bf16[192,512]{1,0:T(8,128)(2,1)} %slice.41), channel_id=1, source_target_pairs={{0,96},{32,0},{64,32},{96,64},{1,97},{33,1},{65,33},{97,65},{2,98}... | collective-permute-start | bytes 589832 | tf_op jit(solution)/shard_map/ppermute | solution.py:424
  149.0 2.6 %stack.7.quad_ref = f32[6]{0:T(128)S(1)} concatenate(f32[1]{0:T(128)} %get-tuple-element.27, f32[1]{0:T(128)} %get-tuple-element.26, f32[2]{0:T(128)S(1)} %slice.32, f32[1]{0:T(128)} %bitcast.1, f32[1]{0:T(128)} %get-tuple-element.27), dimensions={0} | concatenate | bytes 48 | tf_op jit(solution)/shard_map/stack | solution.py:447
  153.2 4.6 %update.1 = (f32[2,16,2,4,3,512]{5,4,3,2,1,0:T(4,128)S(1)}, f32[2,3,512]{2,1,0:T(4,128)S(1)}) custom-call(f32[6]{0:T(128)S(1)} %stack.7.quad_ref, bf16[384,512]{1,0:T(8,128)(2,1)} %analysis.2.own0, bf16[384,512]{1,0:T(8,128)(2,1)S(1)} %analysis.3.own1, bf16[384,512]{1,0:T(8,128)(2,1)S(1)} %collective-permute-done.up0, ...), custom_call_target="tpu_custom_call" | custom-call | flops 7864320 | bytes 10485760 | tf_op jit(solution)/shard_map/update/pallas_call | solution.py:386
  160.5 8.5 %psum.28 = f32[2,3]{1,0:T(2,128)S(1)} all-reduce(f32[2,3]{1,0:T(2,128)S(1)} %reduce_sum.19), channel_id=1, replica_groups=mesh['node'=4,'band_0'=4,'band_1'=4,'band_2'=2] {'node'}, use_global_device_ids=true, to_apply=%region_2.3 | all-reduce | flops 6 | bytes 48 | tf_op jit(solution)/shard_map/psum | solution.py:451
  169.1 8.5 %psum.29 = f32[2,3]{1,0:T(2,128)S(1)} all-reduce(f32[2,3]{1,0:T(2,128)S(1)} %psum.28), channel_id=1, replica_groups=mesh['node'=4,'band_0'=4,'band_1'=4,'band_2'=2] {'band_0'}, use_global_device_ids=true, to_apply=%region_3.4 | all-reduce | flops 6 | bytes 48 | tf_op jit(solution)/shard_map/psum | solution.py:451
  177.6 8.4 %psum.30 = f32[2,3]{1,0:T(2,128)S(1)} all-reduce(f32[2,3]{1,0:T(2,128)S(1)} %psum.29), channel_id=1, replica_groups=mesh['node'=4,'band_0'=4,'band_1'=4,'band_2'=2] {'band_1'}, use_global_device_ids=true, to_apply=%region_4.5 | all-reduce | flops 6 | bytes 48 | tf_op jit(solution)/shard_map/psum | solution.py:451
  186.0 3.5 %copy.16 = f32[1,2,32,4,3,512]{5,3,4,2,1,0:T(4,128)} copy(f32[1,2,32,4,3,512]{5,4,3,2,1,0:T(4,128)} %bitcast.25) | data formatting | bytes 3145728
  189.4 12.2 %psum.31 = f32[2,3]{1,0:T(2,128)S(1)} all-reduce(f32[2,3]{1,0:T(2,128)S(1)} %psum.30), channel_id=1, replica_groups=mesh['node'=4,'band_0'=4,'band_1'=4,'band_2'=2] {'band_2'}, use_global_device_ids=true, to_apply=%region_5.6 | all-reduce | flops 6 | bytes 48 | tf_op jit(solution)/shard_map/psum | solution.py:451
  (62 shorter events, 16.9 us)
Async XLA Ops:
  0.6 46.4 %copy-start = (f32[2,512]{1,0:T(2,128)S(1)}, f32[2,512]{1,0:T(2,128)}, u32[]{:S(2)}) copy-start(f32[2,512]{1,0:T(2,128)} %param.15) | copy-start | bytes 12292
  2.9 5.8 %copy-start.1 = (bf16[32,512,512]{2,1,0:T(8,128)(2,1)S(1)}, bf16[32,512,512]{2,1,0:T(8,128)(2,1)}, u32[]{:S(2)}) copy-start(bf16[32,512,512]{2,1,0:T(8,128)(2,1)} %param.13) | copy-start | bytes 50331652
  16.9 22.9 %all-to-all-start = ((bf16[32,32,384]{2,1,0:T(8,128)(2,1)}), bf16[32,32,384]{2,1,0:T(8,128)(2,1)}, u32[]{:S(2)}, u32[]{:S(2)}) async-start(bf16[32,32,384]{2,1,0:T(8,128)(2,1)} %synthesis.2), calls=%async_computation | async-start | bytes 1572864 | tf_op jit(solution)/shard_map/all_to_all | solution.py:421
  25.5 5.8 %copy-start.2 = (bf16[32,512,512]{2,1,0:T(8,128)(2,1)S(1)}, bf16[32,512,512]{2,1,0:T(8,128)(2,1)}, u32[]{:S(2)}) copy-start(bf16[32,512,512]{2,1,0:T(8,128)(2,1)} %param.13) | copy-start | bytes 50331652
  31.3 16.8 %copy-start.13 = (f32[2,2,33,512]{3,2,1,0:T(8,128)S(1)}, f32[2,2,33,512]{3,2,1,0:T(8,128)}, u32[]{:S(2)}) copy-start(f32[2,2,33,512]{3,2,1,0:T(8,128)} %constant.39.clone.row1_ref) | copy-start | bytes 811012
  39.5 8.6 %copy-start.10 = (f32[2,2,512,4]{3,2,1,0:T(8,128)S(1)}, f32[2,2,512,4]{3,2,1,0:T(8,128)}, u32[]{:S(2)}) copy-start(f32[2,2,512,4]{3,2,1,0:T(8,128)} %constant.41.clone.col1_ref) | copy-start | bytes 98308
  39.8 21.5 %all-to-all-start.1 = ((bf16[32,32,384]{2,1,0:T(8,128)(2,1)}), bf16[32,32,384]{2,1,0:T(8,128)(2,1)}, u32[]{:S(2)}, u32[]{:S(2)}) async-start(bf16[32,32,384]{2,1,0:T(8,128)(2,1)} %synthesis.3), calls=%async_computation.1 | async-start | bytes 1572864 | tf_op jit(solution)/shard_map/all_to_all | solution.py:421
  48.1 1.2 copy-start.11
  49.3 0.9 copy-start.14
  53.8 3.4 %copy-start.16 = (bf16[8,2,528,512]{3,2,1,0:T(8,128)(2,1)}, bf16[8,2,528,512]{3,2,1,0:T(8,128)(2,1)S(1)}, u32[]{:S(2)}) copy-start(bf16[8,2,528,512]{3,2,1,0:T(8,128)(2,1)S(1)} %get-tuple-element.16.tab_ref) | copy-start | bytes 25952260
  57.1 2.0 copy-start.17
  76.5 19.4 %copy-start.12 = (bf16[32,32,384]{2,1,0:T(8,128)(2,1)}, bf16[32,32,384]{2,1,0:T(8,128)(2,1)S(1)}, u32[]{:S(2)}) copy-start(bf16[32,32,384]{2,1,0:T(8,128)(2,1)S(1)} %get-tuple-element.18) | copy-start | bytes 2359300
  95.8 22.8 %all-to-all-start.2 = ((bf16[32,32,384]{2,1,0:T(8,128)(2,1)}), bf16[32,32,384]{2,1,0:T(8,128)(2,1)S(1)}, u32[]{:S(2)}, u32[]{:S(2)}) async-start(bf16[32,32,384]{2,1,0:T(8,128)(2,1)} %copy-done.12), calls=%async_computation.2 | async-start | bytes 1572864 | tf_op jit(solution)/shard_map/all_to_all | solution.py:421
  99.7 2.4 %copy-start.18 = (f32[32,3,512]{2,0,1:T(8,128)S(1)}, f32[32,3,512]{2,0,1:T(8,128)}, u32[]{:S(2)}) copy-start(f32[32,3,512]{2,0,1:T(8,128)} %param.16) | copy-start | bytes 589828
  99.7 2.5 %copy-start.8 = (bf16[32,32,384]{2,1,0:T(8,128)(2,1)S(1)}, bf16[32,32,384]{2,1,0:T(8,128)(2,1)}, u32[]{:S(2)}) copy-start(bf16[32,32,384]{2,1,0:T(8,128)(2,1)} %all_to_all.20.y_ref) | copy-start | bytes 2359300
  102.1 12.4 %copy-start.5 = (f32[2,32,4,3,512]{4,3,2,1,0:T(4,128)}, f32[2,32,4,3,512]{4,3,2,1,0:T(4,128)S(1)}, u32[]{:S(2)}) copy-start(f32[2,32,4,3,512]{4,3,2,1,0:T(4,128)S(1)} %copy.14) | copy-start | bytes 4718596
  102.3 6.4 %copy-start.3 = (bf16[32,512,512]{2,1,0:T(8,128)(2,1)S(1)}, bf16[32,512,512]{2,1,0:T(8,128)(2,1)}, u32[]{:S(2)}) copy-start(bf16[32,512,512]{2,1,0:T(8,128)(2,1)} %param.13) | copy-start | bytes 50331652
  114.5 22.0 %collective-permute-start.1 = (bf16[384,512]{1,0:T(8,128)(2,1)S(1)}, bf16[384,512]{1,0:T(8,128)(2,1)}, u32[]{:S(2)}, u32[]{:S(2)}) collective-permute-start(bf16[384,512]{1,0:T(8,128)(2,1)S(1)} %analysis.3.own1), channel_id=1, source_target_pairs={{0,32},{32,64},{64,96},{96,0},{1,33},{33,65},{65,97},{97,1},{2,34}... | collective-permute-start | bytes 1179656 | tf_op jit(solution)/shard_map/ppermute | solution.py:424
  116.2 21.9 %collective-permute-start.3 = (bf16[384,512]{1,0:T(8,128)(2,1)S(1)}, bf16[384,512]{1,0:T(8,128)(2,1)}, u32[]{:S(2)}, u32[]{:S(2)}) collective-permute-start(bf16[384,512]{1,0:T(8,128)(2,1)S(1)} %analysis.3.own1), channel_id=1, source_target_pairs={{0,96},{32,0},{64,32},{96,64},{1,97},{33,1},{65,33},{97,65},{2,98}... | collective-permute-start | bytes 1179656 | tf_op jit(solution)/shard_map/ppermute | solution.py:424
  118.6 5.8 %copy-start.4 = (bf16[32,512,512]{2,1,0:T(8,128)(2,1)S(1)}, bf16[32,512,512]{2,1,0:T(8,128)(2,1)}, u32[]{:S(2)}) copy-start(bf16[32,512,512]{2,1,0:T(8,128)(2,1)} %param.13) | copy-start | bytes 50331652
  124.4 1.6 copy-start.6
  132.5 11.6 %collective-permute-start = (bf16[384,512]{1,0:T(8,128)(2,1)}, bf16[384,512]{1,0:T(8,128)(2,1)S(1)}, u32[]{:S(2)}, u32[]{:S(2)}) collective-permute-start(bf16[384,512]{1,0:T(8,128)(2,1)} %analysis.2.own0), channel_id=1, source_target_pairs={{0,32},{32,64},{64,96},{96,0},{1,33},{33,65},{65,97},{97,1},{2,34}... | collective-permute-start | bytes 1179656 | tf_op jit(solution)/shard_map/ppermute | solution.py:424
  132.5 12.3 %collective-permute-start.2 = (bf16[384,512]{1,0:T(8,128)(2,1)}, bf16[384,512]{1,0:T(8,128)(2,1)S(1)}, u32[]{:S(2)}, u32[]{:S(2)}) collective-permute-start(bf16[384,512]{1,0:T(8,128)(2,1)} %analysis.2.own0), channel_id=1, source_target_pairs={{0,96},{32,0},{64,32},{96,64},{1,97},{33,1},{65,33},{97,65},{2,98}... | collective-permute-start | bytes 1179656 | tf_op jit(solution)/shard_map/ppermute | solution.py:424
  138.1 13.5 %collective-permute-start.5 = (bf16[192,512]{1,0:T(8,128)(2,1)}, bf16[192,512]{1,0:T(8,128)(2,1)}, u32[]{:S(2)}, u32[]{:S(2)}) collective-permute-start(bf16[192,512]{1,0:T(8,128)(2,1)} %slice.40), channel_id=1, source_target_pairs={{0,32},{32,64},{64,96},{96,0},{1,33},{33,65},{65,97},{97,1},{2,34}... | collective-permute-start | bytes 589832 | tf_op jit(solution)/shard_map/ppermute | solution.py:424
  139.7 11.9 %collective-permute-start.7 = (bf16[192,512]{1,0:T(8,128)(2,1)}, bf16[192,512]{1,0:T(8,128)(2,1)}, u32[]{:S(2)}, u32[]{:S(2)}) collective-permute-start(bf16[192,512]{1,0:T(8,128)(2,1)} %slice.42), channel_id=1, source_target_pairs={{0,96},{32,0},{64,32},{96,64},{1,97},{33,1},{65,33},{97,65},{2,98}... | collective-permute-start | bytes 589832 | tf_op jit(solution)/shard_map/ppermute | solution.py:424
  144.7 6.8 %collective-permute-start.4 = (bf16[192,512]{1,0:T(8,128)(2,1)}, bf16[192,512]{1,0:T(8,128)(2,1)}, u32[]{:S(2)}, u32[]{:S(2)}) collective-permute-start(bf16[192,512]{1,0:T(8,128)(2,1)} %slice.39), channel_id=1, source_target_pairs={{0,32},{32,64},{64,96},{96,0},{1,33},{33,65},{65,97},{97,1},{2,34}... | collective-permute-start | bytes 589832 | tf_op jit(solution)/shard_map/ppermute | solution.py:424
  145.5 6.1 %collective-permute-start.6 = (bf16[192,512]{1,0:T(8,128)(2,1)}, bf16[192,512]{1,0:T(8,128)(2,1)}, u32[]{:S(2)}, u32[]{:S(2)}) collective-permute-start(bf16[192,512]{1,0:T(8,128)(2,1)} %slice.41), channel_id=1, source_target_pairs={{0,96},{32,0},{64,32},{96,64},{1,97},{33,1},{65,33},{97,65},{2,98}... | collective-permute-start | bytes 589832 | tf_op jit(solution)/shard_map/ppermute | solution.py:424
  151.6 1.6 copy-start.7
  157.8 1.3 copy-start.9
  159.1 0.6 copy-start.15

commit v2 on v1

v2 whole, which is shorter than its diff:
```python
import functools
import math

import jax
import jax.numpy as jnp
import numpy as np
from jax import lax
from jax.experimental import pallas as pl
from jax.experimental.pallas import tpu as pltpu
from jax.sharding import Mesh
from jax.sharding import PartitionSpec as P

BAND = ("band_0", "band_1", "band_2")
NODE_BAND = ("node",) + BAND
MODES = 1024
POINTS = 2 * MODES
HALF = MODES // 2
QUARTER = POINTS // 4
ROWS = QUARTER + 16
LATS = 512
DEGREES = 512
NBAND = 32
PAIRS = 16
COLS = 24
LANES = 384
MB = 4
MIB = 1 << 20


def mm(a, b):
    return jnp.dot(a, b, preferred_element_type=jnp.float32)


def swap_groups(arrays, lane):
    for step in range(3):
        width = 16 << step
        low = (lane & width) == 0
        out = list(arrays)
        for i in range(8):
            if not i & (1 << step):
                j = i | (1 << step)
                a, b = arrays[i], arrays[j]
                out[i] = jnp.where(low, a, pltpu.roll(b, width, 1))
                out[j] = jnp.where(low, pltpu.roll(a, 128 - width, 1), b)
        arrays = out
    return arrays


def synthesis_kernel(it_ref, leg_ref, out_ref, send_ref, coef_ref, wide_ref):
    step = pl.program_id(0)

    @pl.when(step == 0)
    def _():
        coef_ref[...] = jnp.zeros_like(coef_ref)

    for k in range(MB):
        for c in range(2):
            for f in range(3):
                row = (c * 3 + f) * 4
                coef_ref[pl.ds(32 * k + row, 4), :] = it_ref[c, k, f]
                send_ref[pl.ds(COLS * k + row, 4), :] = it_ref[c, k, f]
    turned = jnp.transpose(coef_ref[...].astype(jnp.bfloat16).astype(jnp.float32))
    owner = lax.broadcasted_iota(jnp.int32, (DEGREES, 128), 1) // 32
    total = jnp.zeros((LATS, 256), jnp.float32)
    for k in range(MB):
        mine = jnp.where(owner == k, turned, 0.0)
        north = mine.astype(jnp.bfloat16)
        south = jnp.concatenate([mine[:256], -mine[256:]], axis=0).astype(jnp.bfloat16)
        total = total + mm(leg_ref[k], jnp.concatenate([north, south], axis=1))
    par = step // 4
    at = par * PAIRS + (step % 4) * MB
    for h in range(2):
        for t in range(4):
            block = jnp.transpose(total[128 * t : 128 * (t + 1), 128 * h : 128 * (h + 1)])
            for k in range(MB):
                wide_ref[h, t, pl.ds(at + k, COLS, stride=2 * PAIRS), :] = block[
                    32 * k : 32 * k + COLS
                ]

    @pl.when(step == pl.num_programs(0) - 1)
    def _():
        lane = lax.broadcasted_iota(jnp.int32, (PAIRS, 128), 1)
        for p in range(2):
            for c in range(2):
                for f in range(3):
                    for t in range(4):
                        parts = [
                            wide_ref[
                                h, t, pl.ds((((c * 3 + f) * 4 + e) * 2 + p) * PAIRS, PAIRS), :
                            ]
                            for h in range(2)
                            for e in range(4)
                        ]
                        for g, part in enumerate(swap_groups(parts, lane)):
                            out_ref[
                                8 * t + g, pl.ds((2 * p + c) * PAIRS, PAIRS), pl.ds(128 * f, 128)
                            ] = part.astype(jnp.bfloat16)


def synthesis(it6, leg4):
    return pl.pallas_call(
        synthesis_kernel,
        grid=(8,),
        in_specs=[
            pl.BlockSpec((2, MB, None, 3, 4, DEGREES), lambda i: (0, i % 4, i // 4, 0, 0, 0)),
            pl.BlockSpec((MB, None, LATS, DEGREES), lambda i: (i % 4, i // 4, 0, 0)),
        ],
        out_specs=(
            pl.BlockSpec((NBAND, 4 * PAIRS, LANES), lambda i: (0, 0, 0)),
            pl.BlockSpec((None, MB * COLS, DEGREES), lambda i: (i // 2, i % 2, 0)),
        ),
        out_shape=(
            jax.ShapeDtypeStruct((NBAND, 4 * PAIRS, LANES), jnp.bfloat16),
            jax.ShapeDtypeStruct((4, 8 * COLS, DEGREES), jnp.float32),
        ),
        scratch_shapes=[
            pltpu.VMEM((MB * 32, DEGREES), jnp.float32),
            pltpu.VMEM((2, 4, COLS * 2 * PAIRS, 128), jnp.float32),
        ],
        compiler_params=pltpu.CompilerParams(vmem_limit_bytes=56 * MIB),
        cost_estimate=pl.CostEstimate(
            flops=4 * 32 * COLS * LATS * DEGREES, bytes_accessed=21 * MIB, transcendentals=0
        ),
        name="synthesis",
    )(it6, leg4)


def split(x):
    high = x.astype(jnp.bfloat16)
    return high, (x - high.astype(jnp.float32)).astype(jnp.bfloat16)


def table_kernel(row1_ref, row2_ref, col1_ref, col2_ref, tab_ref, back_ref):
    for par in range(2):
        wave = (
            2 * lax.broadcasted_iota(jnp.int32, (1, HALF), 1) + par
        ).astype(jnp.float32) * (1.0 / MODES)

        def rows(j, _, par=par, wave=wave):
            lead_c = row1_ref[par, 0, pl.ds(j, 1), :]
            lead_s = row1_ref[par, 1, pl.ds(j, 1), :]
            cosine = lead_c * row2_ref[par, 0] - lead_s * row2_ref[par, 1]
            sine = lead_s * row2_ref[par, 0] + lead_c * row2_ref[par, 1]
            at = pl.ds(pl.multiple_of(16 * j, 16), 16)
            for t, value in enumerate((cosine, sine, -wave * cosine, wave * sine)):
                high, low = split(value)
                tab_ref[4 * par + t, 0, at, :] = high
                tab_ref[4 * par + t, 1, at, :] = low
            return 0

        lax.fori_loop(0, ROWS // 16, rows, 0)
        for block in range(4):
            lead_c = col1_ref[par, 0, :, pl.ds(block, 1)]
            lead_s = col1_ref[par, 1, :, pl.ds(block, 1)]
            cosine = lead_c * col2_ref[par, 0] - lead_s * col2_ref[par, 1]
            sine = lead_s * col2_ref[par, 0] + lead_c * col2_ref[par, 1]
            if block == 0:
                first = lax.broadcasted_iota(jnp.int32, (1, 128), 1) == 0
                halve = jnp.where(first, 0.5, 1.0)
                cosine, sine = cosine * halve, sine * halve
            for t, value in enumerate((cosine, -sine)):
                high, low = split(value)
                back_ref[2 * par + t, 0, :, pl.ds(128 * block, 128)] = high
                back_ref[2 * par + t, 1, :, pl.ds(128 * block, 128)] = low


def small_tables():
    scale = 1.0 / math.sqrt(MODES)
    step = 2.0 * math.pi / POINTS
    rows1, rows2, cols1, cols2 = [], [], [], []
    for par in range(2):
        m = 2 * np.arange(HALF) + par

        def pair(k, factor):
            angle = ((k[:, None] * m[None, :]) % POINTS) * step
            return np.stack([np.cos(angle), np.sin(angle)]) * factor

        rows1.append(pair(16 * np.arange(ROWS // 16), 1.0))
        rows2.append(pair(np.arange(16), scale))
        cols1.append(pair(128 * np.arange(4), 1.0).transpose(0, 2, 1))
        cols2.append(pair(np.arange(128), scale).transpose(0, 2, 1))
    return [np.stack(x).astype(np.float32) for x in (rows1, rows2, cols1, cols2)]


def tables(parts):
    return pl.pallas_call(
        table_kernel,
        out_shape=(
            jax.ShapeDtypeStruct((8, 2, ROWS, HALF), jnp.bfloat16),
            jax.ShapeDtypeStruct((4, 2, HALF, QUARTER), jnp.bfloat16),
        ),
        compiler_params=pltpu.CompilerParams(vmem_limit_bytes=24 * MIB),
        cost_estimate=pl.CostEstimate(
            flops=16 * ROWS * HALF, bytes_accessed=15 * MIB, transcendentals=0
        ),
        name="tables",
    )(*parts)


def grid_kernel(
    got_ref, tab_ref, back_ref, cor_ref, weight_ref,
    out_ref,
    x_ref, wave_ref, high_ref, low_ref, edge_ref,
):
    for i in range(4):
        x_ref[i] = got_ref[:, i * PAIRS : (i + 1) * PAIRS, :].reshape(HALF, LANES)
    which = (0, 1, 1, 0, 2, 3, 3, 2)
    for t in range(8):
        x = x_ref[which[t]]
        wave_ref[t] = mm(tab_ref[t, 0], x) + mm(tab_ref[t, 1], x)
    cor = cor_ref[...]

    def quads(base, at, lanes):
        ce, se = wave_ref[base, at, lanes], wave_ref[base + 1, at, lanes]
        co, so = wave_ref[base + 4, at, lanes], wave_ref[base + 5, at, lanes]
        a, b, s, d = ce + co, ce - co, se + so, se - so
        return a - s, b + d, b - d, a + s

    def tendency(at):
        cuts = [pl.ds(128 * f, 128) for f in range(3)]
        values = [quads(0, at, cut) for cut in cuts]
        slopes = [quads(2, at, cut) for cut in cuts]
        out = [[], [], []]
        for q in range(4):
            u, v, h = (values[f][q] for f in range(3))
            us, vs, hs = (slopes[f][q] for f in range(3))
            out[0].append(cor * v - u * us - hs)
            out[1].append(-u * vs - cor * u)
            out[2].append(-u * hs - (1.0 + h) * us)
        folded = []
        for t1, t2, t3, t4 in out:
            a, b, c, d = t1 + t4, t2 + t3, t1 - t4, t3 - t2
            folded.append((a + b, c + d, a - b, c - d))
        return folded

    def block(j, _):
        at = pl.ds(pl.multiple_of(16 * j, 16), 16)
        for f, folded in enumerate(tendency(at)):
            for i, value in enumerate(folded):
                high, low = split(value)
                high_ref[i, at, pl.ds(128 * f, 128)] = high
                low_ref[i, at, pl.ds(128 * f, 128)] = low
        return 0

    lax.fori_loop(0, QUARTER // 16, block, 0)
    for f, folded in enumerate(tendency(pl.ds(QUARTER, 16))):
        edge_ref[0, :, pl.ds(128 * f, 128)] = folded[0]
        edge_ref[1, :, pl.ds(128 * f, 128)] = folded[3]

    odd_row = (lax.broadcasted_iota(jnp.int32, (HALF, 1), 0) & 1) == 1
    half_scale = 0.5 / math.sqrt(MODES)
    sign = jnp.where(odd_row, -half_scale, half_scale)
    lane = lax.broadcasted_iota(jnp.int32, (1, 128), 1)
    weight = weight_ref[...]
    signed = jnp.where(lane < 64, weight, -weight)
    for par in range(2):
        both = []
        for c in range(2):
            i = 2 * par + c
            out = mm(back_ref[i, 0], high_ref[i]) + mm(back_ref[i, 1], high_ref[i])
            out = out + mm(back_ref[i, 0], low_ref[i])
            if i == 0:
                out = out + sign * edge_ref[0, 0:1, :]
            if i == 3:
                out = out - sign * edge_ref[1, 0:1, :]
            both.append(out)
        for f in range(3):
            parts = []
            for out in both:
                part = out[:, 128 * f : 128 * (f + 1)]
                part = pltpu.roll(part, 64, 1) * weight + part * signed
                parts.append(part.reshape(NBAND, 2, 8, 128))
            joined = jnp.concatenate(parts, axis=2).astype(jnp.bfloat16)
            for h in range(2):
                z = 2 * par + h
                out_ref[z * NBAND : (z + 1) * NBAND, :, 128 * f : 128 * (f + 1)] = joined[:, h]


def grid_stage(got, tab, back, cor, weight):
    return pl.pallas_call(
        grid_kernel,
        out_shape=jax.ShapeDtypeStruct((4 * NBAND, 16, LANES), jnp.bfloat16),
        scratch_shapes=[
            pltpu.VMEM((4, HALF, LANES), jnp.bfloat16),
            pltpu.VMEM((8, ROWS, LANES), jnp.float32),
            pltpu.VMEM((4, QUARTER, LANES), jnp.bfloat16),
            pltpu.VMEM((4, QUARTER, LANES), jnp.bfloat16),
            pltpu.VMEM((2, 16, LANES), jnp.float32),
        ],
        compiler_params=pltpu.CompilerParams(vmem_limit_bytes=28 * MIB),
        cost_estimate=pl.CostEstimate(
            flops=2 * 28 * ROWS * HALF * LANES, bytes_accessed=17 * MIB, transcendentals=0
        ),
        name="grid",
    )(got, tab, back, cor, weight)


def analysis_kernel(
    id_ref, quad_ref, y_ref, leg_ref, it_ref, st_ref, damp_ref,
    out_ref, sums_ref,
    wide_ref, rate_ref, start_ref, mix_ref, acc_ref,
):
    step = pl.program_id(0)

    @pl.when(step == 0)
    def _():
        acc_ref[...] = jnp.zeros_like(acc_ref)
        lane = lax.broadcasted_iota(jnp.int32, (16, 128), 1)
        for p in range(4):
            for f in range(3):
                for t in range(4):
                    parts = [
                        y_ref[p * NBAND + 8 * t + g, :, pl.ds(128 * f, 128)].astype(jnp.float32)
                        for g in range(8)
                    ]
                    for i, part in enumerate(swap_groups(parts, lane)):
                        for c in range(2):
                            row = (((p * 2 + c) * 3 + f) * 4 + i % 4) * 8
                            wide_ref[i // 4, t, pl.ds(row, 8), :] = part[8 * c : 8 * c + 8]

    node = id_ref[0]
    for k in range(MB):
        at = step * MB + k
        mode = 2 * (8 * (node % 2) + at) + node // 2
        for c in range(2):
            for f in range(3):
                row = (c * 3 + f) * 4
                rate_ref[pl.ds(row, 4), :] = jnp.broadcast_to(
                    damp_ref[f, pl.ds(mode, 1), :], (4, DEGREES)
                )
                start_ref[pl.ds(row, 4), :] = st_ref[c, k, f]
        halves = []
        for h in range(2):
            spec = jnp.concatenate(
                [wide_ref[h, t, pl.ds(at, 4 * COLS, stride=8), :] for t in range(4)], axis=1
            ).astype(jnp.bfloat16)
            halves.append(mm(spec, leg_ref[k, :, 256 * h : 256 * (h + 1)]))
        for h in range(2):
            cut = slice(256 * h, 256 * (h + 1))
            rate, start = rate_ref[:, cut], start_ref[:, cut]
            olds = [it_ref[p, COLS * k : COLS * (k + 1), cut] for p in range(4)]
            forces = [
                halves[h][COLS * p : COLS * (p + 1)] - rate * (olds[p] - start) for p in range(4)
            ]
            change = jnp.zeros_like(start)
            for q in range(4):
                row = [quad_ref[q, p] for p in range(4)]
                mine = row[q] * rate
                inverse = 1.0 / (1.0 + mine)
                mixed = (
                    row[0] * forces[0] + row[1] * forces[1] + row[2] * forces[2] + row[3] * forces[3]
                ) * inverse
                total = row[0] + row[1] + row[2] + row[3]
                new = mixed + (start * (1.0 - rate * total) + mine * olds[q]) * inverse
                moved = new - olds[q]
                change = change + moved * moved
                mix_ref[q, COLS * k : COLS * (k + 1), cut] = mixed
            acc_ref[0, :, cut] += change
            acc_ref[1, :, cut] += start * start
    out_ref[...] = mix_ref[...].astype(jnp.bfloat16)

    @pl.when(step == pl.num_programs(0) - 1)
    def _():
        field = lax.broadcasted_iota(jnp.int32, (COLS, 1), 0) // 4 % 3
        lane = lax.broadcasted_iota(jnp.int32, (1, 128), 1)
        sums = jnp.zeros((1, 128), jnp.float32)
        for s in range(2):
            per_row = jnp.sum(acc_ref[s], axis=1, keepdims=True)
            for f in range(3):
                value = jnp.sum(jnp.where(field == f, per_row, 0.0), axis=0, keepdims=True)
                sums = sums + jnp.where(lane == 3 * s + f, value, 0.0)
        sums_ref[...] = sums


def analysis(ids, quad, y, leg4, it_all, st6, damp):
    spec = pl.BlockSpec
    return pl.pallas_call(
        analysis_kernel,
        grid_spec=pltpu.PrefetchScalarGridSpec(
            num_scalar_prefetch=1,
            grid=(2,),
            in_specs=[
                spec(memory_space=pltpu.SMEM),
                spec((4 * NBAND, 16, LANES), lambda i, s: (0, 0, 0)),
                spec(
                    (MB, None, LATS, DEGREES), lambda i, s: (s[0] % 2 * 2 + i, s[0] // 2, 0, 0)
                ),
                spec((4, MB * COLS, DEGREES), lambda i, s: (0, i, 0)),
                spec(
                    (2, MB, None, 3, 4, DEGREES),
                    lambda i, s: (0, s[0] % 2 * 2 + i, s[0] // 2, 0, 0, 0),
                ),
                spec((3, 32, DEGREES), lambda i, s: (0, 0, 0)),
            ],
            out_specs=(
                spec((4, MB * COLS, DEGREES), lambda i, s: (0, i, 0)),
                spec((1, 128), lambda i, s: (0, 0)),
            ),
            scratch_shapes=[
                pltpu.VMEM((2, 4, 4 * COLS * 8, 128), jnp.float32),
                pltpu.VMEM((COLS, DEGREES), jnp.float32),
                pltpu.VMEM((COLS, DEGREES), jnp.float32),
                pltpu.VMEM((4, MB * COLS, DEGREES), jnp.float32),
                pltpu.VMEM((2, COLS, DEGREES), jnp.float32),
            ],
        ),
        out_shape=(
            jax.ShapeDtypeStruct((4, 8 * COLS, DEGREES), jnp.bfloat16),
            jax.ShapeDtypeStruct((1, 128), jnp.float32),
        ),
        compiler_params=pltpu.CompilerParams(vmem_limit_bytes=56 * MIB),
        cost_estimate=pl.CostEstimate(
            flops=2 * 32 * COLS * LATS * DEGREES, bytes_accessed=10 * MIB, transcendentals=0
        ),
        name="analysis",
    )(ids, quad, y, leg4, it_all, st6, damp)


def update_kernel(id_ref, quad_ref, mixed_ref, st_ref, it_ref, damp_ref, out_ref, mix_ref):
    z = pl.program_id(0)
    node = id_ref[0]
    total = quad_ref[node, 0] + quad_ref[node, 1] + quad_ref[node, 2] + quad_ref[node, 3]
    diag = quad_ref[node, node]
    mix_ref[...] = mixed_ref[...].astype(jnp.float32)
    for k in range(8):
        mode = 2 * (8 * (z % 2) + k) + z // 2
        for f in range(3):
            rate = damp_ref[f, pl.ds(mode, 1), :]
            mine = diag * rate
            inverse = 1.0 / (1.0 + mine)
            keep = (1.0 - rate * total) * inverse
            mine = mine * inverse
            for c in range(2):
                mixed = mix_ref[pl.ds(COLS * k + (c * 3 + f) * 4, 4), :]
                out_ref[c, k, f] = mixed + st_ref[c, k, f] * keep + mine * it_ref[c, k, f]


def update(ids, quad, mixed, st7, it7, damp):
    spec = pl.BlockSpec
    state = spec((2, None, 8, None, 3, 4, DEGREES), lambda i, s: (0, i % 2, 0, i // 2, 0, 0, 0))
    return pl.pallas_call(
        update_kernel,
        grid_spec=pltpu.PrefetchScalarGridSpec(
            num_scalar_prefetch=1,
            grid=(4,),
            in_specs=[
                spec(memory_space=pltpu.SMEM),
                spec((None, 8 * COLS, DEGREES), lambda i, s: (i, 0, 0)),
                state,
                state,
                spec((3, 32, DEGREES), lambda i, s: (0, 0, 0)),
            ],
            out_specs=state,
            scratch_shapes=[pltpu.VMEM((8 * COLS, DEGREES), jnp.float32)],
        ),
        out_shape=jax.ShapeDtypeStruct(it7.shape, jnp.float32),
        compiler_params=pltpu.CompilerParams(vmem_limit_bytes=32 * MIB),
        cost_estimate=pl.CostEstimate(
            flops=4 * 32 * COLS * DEGREES, bytes_accessed=6 * MIB, transcendentals=0
        ),
        name="update",
    )(ids, quad, mixed, st7, it7, damp)


def exchange(x, axes):
    return lax.all_to_all(x, axes, split_axis=0, concat_axis=0, tiled=True)


def body(state0, iterate, legendre, lat_weight, coriolis, damping, quadrature):
    node = lax.axis_index("node")
    band = lax.axis_index(BAND)
    lat_rows = LATS // NBAND
    spec = iterate[0].transpose(0, 1, 3, 2, 4)
    base = state0.transpose(0, 1, 3, 2, 4)
    it6 = spec.reshape(2, PAIRS, 2, 3, 4, DEGREES)
    st6 = base.reshape(2, PAIRS, 2, 3, 4, DEGREES)
    leg4 = legendre.reshape(PAIRS, 2, LATS, DEGREES)
    damp = damping.transpose(1, 0, 2)
    ids = jnp.reshape(node, (1,)).astype(jnp.int32)

    sent, spread = synthesis(it6, leg4)
    got = exchange(sent, BAND)
    spread = exchange(spread, "node")
    parts = [jnp.asarray(x) for x in small_tables()]
    parts, _ = lax.optimization_barrier((parts, sent))
    tab, back = tables(parts)
    first = band * lat_rows
    cor = lax.dynamic_slice_in_dim(coriolis, first, lat_rows, 1)
    cor = jnp.broadcast_to(cor[:, None, :], (2, 4, lat_rows)).reshape(1, 128)
    weight = lax.dynamic_slice_in_dim(lat_weight, first, lat_rows, 0)
    weight = jnp.broadcast_to(weight[None, :], (8, lat_rows)).reshape(1, 128)
    spectra = exchange(grid_stage(got, tab, back, cor, weight), NODE_BAND)
    mixed, sums = analysis(ids, quadrature, spectra, leg4, spread, st6, damp)
    mixed = exchange(mixed, "node")
    sums = exchange(jnp.broadcast_to(sums[None], (4 * NBAND, 1, 128)), NODE_BAND)
    shape7 = (2, 2, 8, 2, 3, 4, DEGREES)
    out = update(ids, quadrature, mixed, base.reshape(shape7), spec.reshape(shape7), damp)
    total = jnp.sum(sums, axis=(0, 1))
    ratio = jnp.sqrt(total[:3] / (4.0 * total[3:6] + 1e-06))
    out = out.reshape(2, 32, 3, 4, DEGREES).transpose(0, 1, 3, 2, 4)
    return (out[None], ratio)


def solution(mesh):
    torus = Mesh(
        mesh.devices.reshape(mesh.shape["node"], 4, 4, 2), ("node", "band_0", "band_1", "band_2")
    )
    return jax.shard_map(
        body,
        mesh=torus,
        in_specs=(
            P(None, BAND, None, None, None),
            P("node", None, BAND, None, None, None),
            P(BAND, None, None),
            P(),
            P(),
            P(BAND, None, None),
            P(),
        ),
        out_specs=(P("node", None, BAND, None, None, None), P()),
        check_vma=False,
    )
```

time: 203 us -> 157 us (0.77)
  local copies, waits for them, and re-layouts: 53.5 us -> 4.22 us
  waiting for transfers between devices: 4.21 us -> 39.6 us
  starting transfers between devices: 31.9 us -> 13.8 us
  blocking collectives: 57 us -> 45.2 us
  other arithmetic: 2.7 us -> 0.63 us
    unnamed x42 -> x20, local copies, waits for them, and re-layouts: 44.5 us -> 2.4 us
    psum x4 -> x0, blocking collectives: 37.6 us -> none  [body(): partial = lax.psum(partial, axis)]
    all_to_all x3, waiting for transfers between devices: 2.5 us -> 39.6 us  [exchange(): return lax.all_to_all(x, axes, split_axis=0, concat_axis=0, tiled=True)]
    all_to_all x1 -> x2, blocking collectives: 19.3 us -> 45.2 us  [exchange(): return lax.all_to_all(x, axes, split_axis=0, concat_axis=0, tiled=True)]
    ppermute x8 -> x0, starting transfers between devices: 12.2 us -> none  [shift(): return lax.ppermute(x, 'node', [(i, (i + by) % 4) for i in range(4)])]
    all_to_all x3, starting transfers between devices: 19.7 us -> 13.8 us  [exchange(): return lax.all_to_all(x, axes, split_axis=0, concat_axis=0, tiled=True)]
    slice x6 -> x0, local copies, waits for them, and re-layouts: 5.31 us -> none  [the longest x2 2.32 us: body(): fa = [shift(x[:rows], 1) for x in up]]
    another operation x1 -> x0, local copies, waits for them, and re-layouts: 2.62 us -> none  [body(): jnp.stack([pick[0], pick[3], pick[1], pick[2], jnp.sum(row), pick[0]])]
  transfers between devices with their start and end apart: 11 -> 3, of which waited for: 3 -> 3; matrix products, arithmetic and copies ran while one was open for 6% -> 1% of each run, Pallas kernels for 12% -> 9%
where the time goes in v2:
time: 157 us; the launch traced here: 156 us
  Pallas kernels  52.2 us (33%)
  blocking collectives  45.2 us (29%)
  waiting for transfers between devices  39.6 us (25%)
  starting transfers between devices  13.8 us (9%)
  local copies, waits for them, and re-layouts  4.22 us (3%)
    all_to_all x2, blocking collectives, exchange(): return lax.all_to_all(x, axes, split_axis=0, concat_axis=0, tiled=True)  45.2 us
    all_to_all x3, waiting for transfers between devices, exchange(): return lax.all_to_all(x, axes, split_axis=0, concat_axis=0, tiled=True)  39.6 us
    pallas_call x1, Pallas kernels, synthesis(): pl.pallas_call(synthesis_kernel, grid=(8,), in_specs=[pl.BlockSpec((2, MB...  20.8 us
    all_to_all x3, starting transfers between devices, exchange(): return lax.all_to_all(x, axes, split_axis=0, concat_axis=0, tiled=True)  13.8 us
    pallas_call x1, Pallas kernels, analysis(): pl.pallas_call(analysis_kernel, grid_spec=pltpu.PrefetchScalarGridSpec(nu...  12.7 us
    pallas_call x1, Pallas kernels, grid_stage(): pl.pallas_call(grid_kernel, out_shape=jax.ShapeDtypeStruct((4 * NBAND, 16...  11.3 us
    pallas_call x1, Pallas kernels, update(): pl.pallas_call(update_kernel, grid_spec=pltpu.PrefetchScalarGridSpec(num_...  3.89 us
    pallas_call x1, Pallas kernels, tables(): pl.pallas_call(table_kernel, out_shape=(jax.ShapeDtypeStruct((8, 2, ROWS,...  3.56 us
  transfers between devices with their start and end apart: 3, of which 3 were waited for; matrix products, arithmetic and copies ran while one was open for 1% of the time, Pallas kernels for 9%

profile of v2, /device:TPU:1, one launch (start us, length us, event | category | flops | bytes accessed | tf_op | source)
XLA Modules:
  0.0 156.4 jit_solution(4501724273188209200)
XLA Ops:
  0.6 0.0 copy-start
  0.6 20.8 %synthesis.1 = (bf16[32,64,384]{2,1,0:T(8,128)(2,1)}, f32[4,192,512]{2,1,0:T(8,128)}) custom-call(f32[2,16,2,3,4,512]{5,4,3,2,1,0:T(4,128)} %bitcast.22, bf16[16,2,512,512]{3,2,1,0:T(8,128)(2,1)} %bitcast.28), custom_call_target="tpu_custom_call" | custom-call | flops 805306368 | bytes 22020096 | tf_op jit(solution)/shard_map/synthesis/pallas_call | solution.py:101
  21.5 31.4 %all_to_all.25.got_ref = bf16[32,64,384]{2,1,0:T(8,128)(2,1)S(1)} all-to-all(bf16[32,64,384]{2,1,0:T(8,128)(2,1)} %get-tuple-element.12), channel_id=1, replica_groups=mesh['node'=4,'band_0'=4,'band_1'=4,'band_2'=2] {'band_0','band_1','band..., dimensions={0} | all-to-all | bytes 3145728 | tf_op jit(solution)/shard_map/all_to_all | solution.py:466
  52.9 5.2 %all-to-all-start.2 = ((f32[4,192,512]{2,1,0:T(8,128)}), f32[4,192,512]{2,1,0:T(8,128)}, u32[]{:S(2)}, u32[]{:S(2)}) async-start(f32[4,192,512]{2,1,0:T(8,128)} %get-tuple-element.19), calls=%async_computation.2 | async-start | bytes 3145728 | tf_op jit(solution)/shard_map/all_to_all | solution.py:466
  58.1 0.8 dynamic_slice.7
  58.8 0.0 copy-done
  58.8 0.1 constant_dynamic-slice_fusion
  58.9 0.1 reshape.39.cor_ref
  59.0 0.1 reshape.40.weight_ref
  59.1 0.0 copy-done.3
  59.1 0.0 copy-done.6
  59.1 0.0 copy-done.7
  59.1 0.0 copy-start.4
  59.1 1.2 copy-done.4
  60.3 3.6 %tables.1 = (bf16[8,2,528,512]{3,2,1,0:T(8,128)(2,1)S(1)}, bf16[4,2,512,512]{3,2,1,0:T(8,128)(2,1)S(1)}) custom-call(f32[2,2,33,512]{3,2,1,0:T(8,128)S(1)} %copy-done.6, f32[2,2,16,512]{3,2,1,0:T(8,128)S(1)} %copy-done.7, f32[2,2,512,4]{3,2,1,0:T(8,128)S(1)} %copy-done.4, f32[2,2,512,128]{3,2,1,0:T(8,128)S(1)} %copy-done.3), custom_call_target="tpu_custom_call" | custom-call | flops 4325376 | bytes 15728640 | tf_op jit(solution)/shard_map/tables/pallas_call | solution.py:186
  63.9 11.3 %grid.1 = bf16[128,16,384]{2,1,0:T(8,128)(2,1)} custom-call(bf16[32,64,384]{2,1,0:T(8,128)(2,1)S(1)} %all_to_all.25.got_ref, bf16[8,2,528,512]{3,2,1,0:T(8,128)(2,1)S(1)} %get-tuple-element.17.tab_ref, bf16[4,2,512,512]{3,2,1,0:T(8,128)(2,1)S(1)} %get-tuple-element.18.back_ref, f32[1,128]{1,0:T(1,128)S(1)} %reshape.39.cor_ref, f32[1,128]{1,0:T(1,128)S(1)} %reshape.40.weight_ref), custom_call_target="tpu_custom_call" | custom-call | flops 5813305344 | bytes 17825792 | tf_op jit(solution)/shard_map/grid/pallas_call | solution.py:280
  75.2 3.9 %all-to-all-done.2.it_ref = f32[4,192,512]{2,1,0:T(8,128)} async-done(((f32[4,192,512]{2,1,0:T(8,128)}), f32[4,192,512]{2,1,0:T(8,128)}, u32[]{:S(2)}, u32[]{:S(2)}) %all-to-all-start.2) | async-done | bytes 1572896 | tf_op jit(solution)/shard_map/all_to_all | solution.py:466
  79.1 4.5 %all-to-all-start.1 = ((bf16[128,16,384]{2,1,0:T(8,128)(2,1)}), bf16[128,16,384]{2,1,0:T(8,128)(2,1)S(1)}, u32[]{:S(2)}, u32[]{:S(2)}) async-start(bf16[128,16,384]{2,1,0:T(8,128)(2,1)} %grid.1), calls=%async_computation.1 | async-start | bytes 3145728 | tf_op jit(solution)/shard_map/all_to_all | solution.py:466
  83.6 24.7 %all-to-all-done.1.y_ref = bf16[128,16,384]{2,1,0:T(8,128)(2,1)S(1)} async-done(((bf16[128,16,384]{2,1,0:T(8,128)(2,1)}), bf16[128,16,384]{2,1,0:T(8,128)(2,1)S(1)}, u32[]{:S(2)}, u32[]{:S(2)}) %all-to-all-start.1) | async-done | bytes 1572896 | tf_op jit(solution)/shard_map/all_to_all | solution.py:466
  108.3 1.1 copy-done.9
  109.4 12.7 %analysis.1 = (bf16[4,192,512]{2,1,0:T(8,128)(2,1)}, f32[1,128]{1,0:T(1,128)}) custom-call(s32[1]{0:T(128)} %bitcast.id_ref, f32[4,4]{1,0:T(4,128)} %quad_ref.3, bf16[128,16,384]{2,1,0:T(8,128)(2,1)} %copy-done.9, bf16[16,2,512,512]{3,2,1,0:T(8,128)(2,1)} %bitcast.29, f32[4,192,512]{2,1,0:T(8,128)} %all-to-all-done.2.it_ref, ...), custom_call_target="tpu_custom_call" | custom-call | flops 402653184 | bytes 10485760 | tf_op jit(solution)/shard_map/analysis/pallas_call | solution.py:377
  122.1 0.0 copy-start.8
  122.1 0.8 broadcast_in_dim.27
  122.9 13.8 %all_to_all.26 = f32[128,1,128]{2,1,0:T(1,128)S(1)} all-to-all(f32[128,1,128]{2,1,0:T(1,128)S(1)} %broadcast_in_dim.27), channel_id=1, replica_groups=mesh['node'=4,'band_0'=4,'band_1'=4,'band_2'=2] {'node','band_0','band_1..., dimensions={0} | all-to-all | bytes 131072 | tf_op jit(solution)/shard_map/all_to_all | solution.py:466
  136.7 4.2 %all-to-all-start.3 = ((bf16[4,192,512]{2,1,0:T(8,128)(2,1)}), bf16[4,192,512]{2,1,0:T(8,128)(2,1)}, u32[]{:S(2)}, u32[]{:S(2)}) async-start(bf16[4,192,512]{2,1,0:T(8,128)(2,1)} %get-tuple-element.20), calls=%async_computation.3 | async-start | bytes 1572864 | tf_op jit(solution)/shard_map/all_to_all | solution.py:466
  140.9 0.6 fusion
  141.5 11.0 %all-to-all-done.3.mixed_ref = bf16[4,192,512]{2,1,0:T(8,128)(2,1)} async-done(((bf16[4,192,512]{2,1,0:T(8,128)(2,1)}), bf16[4,192,512]{2,1,0:T(8,128)(2,1)}, u32[]{:S(2)}, u32[]{:S(2)}) %all-to-all-start.3) | async-done | bytes 786464 | tf_op jit(solution)/shard_map/all_to_all | solution.py:466
  152.5 0.0 copy-done.2
  152.5 0.0 copy-done.1
  152.5 0.0 copy-done.5
  152.5 0.0 copy-done.8
  152.6 3.9 %update.1 = f32[2,2,8,2,3,4,512]{6,5,4,3,2,1,0:T(4,128)} custom-call(s32[1]{0:T(128)} %bitcast.id_ref, f32[4,4]{1,0:T(4,128)S(1)} %copy-done.8, bf16[4,192,512]{2,1,0:T(8,128)(2,1)} %all-to-all-done.3.mixed_ref, f32[2,2,8,2,3,4,512]{6,5,4,3,2,1,0:T(4,128)S(1)} %bitcast.25, f32[2,2,8,2,3,4,512]{6,5,4,3,2,1,0:T(4,128)S(1)} %bitcast.23, f32[3,32,512]{2,1,0:T(8,128)S(1)} %bitcast.27), custom_call_target="tpu_custom_call" | custom-call | flops 1572864 | bytes 6291456 | tf_op jit(solution)/shard_map/update/pallas_call | solution.py:441
  (10 shorter events, 0.1 us)
Async XLA Ops:
  0.6 58.2 %copy-start = (f32[2,512]{1,0:T(2,128)S(1)}, f32[2,512]{1,0:T(2,128)}, u32[]{:S(2)}) copy-start(f32[2,512]{1,0:T(2,128)} %param.15) | copy-start | bytes 12292
  52.9 6.2 %copy-start.3 = (f32[2,2,512,128]{3,2,1,0:T(8,128)S(1)}, f32[2,2,512,128]{3,2,1,0:T(8,128)}, u32[]{:S(2)}) copy-start(f32[2,2,512,128]{3,2,1,0:T(8,128)} %constant.42.clone.col2_ref) | copy-start | bytes 3145732
  52.9 6.2 %copy-start.6 = (f32[2,2,33,512]{3,2,1,0:T(8,128)S(1)}, f32[2,2,33,512]{3,2,1,0:T(8,128)}, u32[]{:S(2)}) copy-start(f32[2,2,33,512]{3,2,1,0:T(8,128)} %constant.39.clone.row1_ref) | copy-start | bytes 811012
  52.9 6.2 %copy-start.7 = (f32[2,2,16,512]{3,2,1,0:T(8,128)S(1)}, f32[2,2,16,512]{3,2,1,0:T(8,128)}, u32[]{:S(2)}) copy-start(f32[2,2,16,512]{3,2,1,0:T(8,128)} %constant.40.clone.row2_ref) | copy-start | bytes 393220
  52.9 26.1 %all-to-all-start.2 = ((f32[4,192,512]{2,1,0:T(8,128)}), f32[4,192,512]{2,1,0:T(8,128)}, u32[]{:S(2)}, u32[]{:S(2)}) async-start(f32[4,192,512]{2,1,0:T(8,128)} %get-tuple-element.19), calls=%async_computation.2 | async-start | bytes 3145728 | tf_op jit(solution)/shard_map/all_to_all | solution.py:466
  59.1 1.2 copy-start.4
  79.1 29.2 %all-to-all-start.1 = ((bf16[128,16,384]{2,1,0:T(8,128)(2,1)}), bf16[128,16,384]{2,1,0:T(8,128)(2,1)S(1)}, u32[]{:S(2)}, u32[]{:S(2)}) async-start(bf16[128,16,384]{2,1,0:T(8,128)(2,1)} %grid.1), calls=%async_computation.1 | async-start | bytes 3145728 | tf_op jit(solution)/shard_map/all_to_all | solution.py:466
  108.3 1.1 copy-start.9
  109.4 43.1 %copy-start.2 = (f32[2,32,4,3,512]{4,2,3,1,0:T(4,128)S(1)}, f32[2,32,4,3,512]{4,2,3,1,0:T(4,128)}, u32[]{:S(2)}) copy-start(f32[2,32,4,3,512]{4,2,3,1,0:T(4,128)} %param.11) | copy-start | bytes 4718596
  122.1 30.5 %copy-start.1 = (f32[1,2,32,4,3,512]{5,3,4,2,1,0:T(4,128)S(1)}, f32[1,2,32,4,3,512]{5,3,4,2,1,0:T(4,128)}, u32[]{:S(2)}) copy-start(f32[1,2,32,4,3,512]{5,3,4,2,1,0:T(4,128)} %param.12) | copy-start | bytes 4718596
  122.1 30.5 %copy-start.5 = (f32[32,3,512]{2,0,1:T(8,128)S(1)}, f32[32,3,512]{2,0,1:T(8,128)}, u32[]{:S(2)}) copy-start(f32[32,3,512]{2,0,1:T(8,128)} %param.16) | copy-start | bytes 589828
  122.1 30.5 %copy-start.8 = (f32[4,4]{1,0:T(4,128)S(1)}, f32[4,4]{1,0:T(4,128)}, u32[]{:S(2)}) copy-start(f32[4,4]{1,0:T(4,128)} %quad_ref.3) | copy-start | bytes 196
  136.7 15.8 %all-to-all-start.3 = ((bf16[4,192,512]{2,1,0:T(8,128)(2,1)}), bf16[4,192,512]{2,1,0:T(8,128)(2,1)}, u32[]{:S(2)}, u32[]{:S(2)}) async-start(bf16[4,192,512]{2,1,0:T(8,128)(2,1)} %get-tuple-element.20), calls=%async_computation.3 | async-start | bytes 1572864 | tf_op jit(solution)/shard_map/all_to_all | solution.py:466

commit v3 on v2

v3 whole, which is shorter than its diff:
```python
import functools
import math

import jax
import jax.numpy as jnp
import numpy as np
from jax import lax
from jax.experimental import pallas as pl
from jax.experimental.pallas import tpu as pltpu
from jax.sharding import Mesh
from jax.sharding import PartitionSpec as P

BAND = ("band_0", "band_1", "band_2")
NODE_BAND = ("node",) + BAND
MODES = 1024
POINTS = 2 * MODES
HALF = MODES // 2
QUARTER = POINTS // 4
ROWS = QUARTER + 16
LATS = 512
DEGREES = 512
NBAND = 32
PAIRS = 16
COLS = 24
LANES = 384
MB = 4
MIB = 1 << 20


NT = (((1,), (1,)), ((), ()))


def mm(a, b):
    return jnp.dot(a, b, preferred_element_type=jnp.float32)


STREAMS = 16


def synthesis_kernel(it_hbm, leg_hbm, out_ref, it_ref, leg_ref, sems, coef_ref, wide_ref):
    def stream(j):
        return pltpu.make_async_copy(
            leg_hbm.at[pl.ds(j % 8 * 2, 2), j // 8], leg_ref.at[j], sems.at[j]
        )

    coefficients = pltpu.make_async_copy(it_hbm, it_ref, sems.at[STREAMS])
    coefficients.start()
    for j in range(STREAMS):
        stream(j).start()
    coefficients.wait()
    low = lax.broadcasted_iota(jnp.int32, (COLS, 128), 1) < 64

    def pair(j, _):
        stream(j).wait()
        par = j // 8
        for k in range(2):
            i = j % 8 * 2 + k
            for c in range(2):
                for f in range(3):
                    row = (c * 3 + f) * 4
                    coef_ref[k, row : row + 4, :] = it_ref[c, i, par, f]
            coeff = coef_ref[k].astype(jnp.bfloat16)
            even = lax.dot_general(
                coeff[:, :256], leg_ref[j, k, :, :256], NT, preferred_element_type=jnp.float32
            )
            odd = lax.dot_general(
                coeff[:, 256:], leg_ref[j, k, :, 256:], NT, preferred_element_type=jnp.float32
            )
            for t in range(4):
                cut = slice(128 * t, 128 * (t + 1))
                north = even[:, cut] + odd[:, cut]
                south = pltpu.roll(even[:, cut] - odd[:, cut], 64, 1)
                rows = pl.ds(par * PAIRS + i, COLS, stride=2 * PAIRS)
                wide_ref[2 * t, rows, :] = jnp.where(low, north, south)
                wide_ref[2 * t + 1, rows, :] = jnp.where(low, south, north)
        return 0

    lax.fori_loop(0, STREAMS, pair, 0)
    for p in range(2):
        for c in range(2):
            for f in range(3):
                for e in range(4):
                    row = (((c * 3 + f) * 4 + e) * 2 + p) * PAIRS
                    out_ref[
                        8 * e : 8 * e + 8,
                        (2 * p + c) * PAIRS : (2 * p + c + 1) * PAIRS,
                        128 * f : 128 * (f + 1),
                    ] = wide_ref[:, row : row + PAIRS, :].astype(jnp.bfloat16)


def synthesis(it6, leg4):
    return pl.pallas_call(
        synthesis_kernel,
        in_specs=[pl.BlockSpec(memory_space=pl.ANY)] * 2,
        out_shape=jax.ShapeDtypeStruct((NBAND, 4 * PAIRS, LANES), jnp.bfloat16),
        scratch_shapes=[
            pltpu.VMEM(it6.shape, jnp.float32),
            pltpu.VMEM((STREAMS, 2, LATS, DEGREES), jnp.bfloat16),
            pltpu.SemaphoreType.DMA((STREAMS + 1,)),
            pltpu.VMEM((2, COLS, DEGREES), jnp.float32),
            pltpu.VMEM((8, COLS * 2 * PAIRS, 128), jnp.float32),
        ],
        compiler_params=pltpu.CompilerParams(vmem_limit_bytes=56 * MIB),
        cost_estimate=pl.CostEstimate(
            flops=2 * 32 * COLS * LATS * DEGREES, bytes_accessed=20 * MIB, transcendentals=0
        ),
        name="synthesis",
    )(it6, leg4)


def encode(x):
    return (x * jnp.abs(x)).astype(jnp.bfloat16)


def decode(coded):
    coded = coded.astype(jnp.float32)
    root = jnp.sqrt(jnp.abs(coded))
    return jnp.where(coded < 0, -root, root)


def prepare_kernel(
    id_ref, quad_ref, st_ref, it_ref, damp_ref,
    send0_ref, send1_ref, send2_ref, send3_ref, base_ref, dense_ref,
):
    node = id_ref[0]
    place = pl.program_id(0)
    z = (node + place) % 4
    total = quad_ref[node, 0] + quad_ref[node, 1] + quad_ref[node, 2] + quad_ref[node, 3]
    diag = quad_ref[node, node]
    for k in range(8):
        mode = 2 * (8 * (z % 2) + k) + z // 2
        for f in range(3):
            rate = damp_ref[f, pl.ds(mode, 1), :]
            mine = diag * rate
            inverse = 1.0 / (1.0 + mine)
            keep = (1.0 - rate * total) * inverse
            mine = mine * inverse
            for c in range(2):
                row = COLS * k + (c * 3 + f) * 4
                start, old = st_ref[c, k, f], it_ref[c, k, f]
                dense_ref[row : row + 4, :] = old - start
                base_ref[c, k, f] = start * keep + mine * old
    for s, ref in enumerate((send0_ref, send1_ref, send2_ref, send3_ref)):

        @pl.when(place == s)
        def _(ref=ref):
            ref[...] = encode(dense_ref[...])


def own_subset(i, s):
    z = (s[0] + i) % 4
    return (0, z % 2, 0, z // 2, 0, 0, 0)


STATE = (2, None, 8, None, 3, 4, DEGREES)


def prepare(ids, quad, st7, it7, damp):
    spec = pl.BlockSpec
    state = spec(STATE, own_subset)
    return pl.pallas_call(
        prepare_kernel,
        grid_spec=pltpu.PrefetchScalarGridSpec(
            num_scalar_prefetch=1,
            grid=(4,),
            in_specs=[
                spec(memory_space=pltpu.SMEM),
                state,
                state,
                spec((3, 32, DEGREES), lambda i, s: (0, 0, 0)),
            ],
            out_specs=[spec((8 * COLS, DEGREES), lambda i, s: (0, 0))] * 4 + [state],
            scratch_shapes=[pltpu.VMEM((8 * COLS, DEGREES), jnp.float32)],
        ),
        out_shape=[jax.ShapeDtypeStruct((8 * COLS, DEGREES), jnp.bfloat16)] * 4
        + [jax.ShapeDtypeStruct(it7.shape, jnp.float32)],
        compiler_params=pltpu.CompilerParams(vmem_limit_bytes=32 * MIB),
        cost_estimate=pl.CostEstimate(
            flops=8 * 32 * COLS * DEGREES, bytes_accessed=6 * MIB, transcendentals=0
        ),
        name="prepare",
    )(ids, quad, st7, it7, damp)


def split(x):
    high = x.astype(jnp.bfloat16)
    return high, (x - high.astype(jnp.float32)).astype(jnp.bfloat16)


def table_kernel(row1_ref, row2_ref, tab_ref, back_ref, keep_ref):
    first = lax.broadcasted_iota(jnp.int32, (1, 128), 1) == 0
    halve = jnp.where(first, 0.5, 1.0)
    for par in range(2):
        wave = (
            2 * lax.broadcasted_iota(jnp.int32, (1, HALF), 1) + par
        ).astype(jnp.float32) * (1.0 / MODES)

        def rows(j, _, par=par, wave=wave):
            lead_c = row1_ref[par, 0, pl.ds(j, 1), :]
            lead_s = row1_ref[par, 1, pl.ds(j, 1), :]
            cosine = lead_c * row2_ref[par, 0] - lead_s * row2_ref[par, 1]
            sine = lead_s * row2_ref[par, 0] + lead_c * row2_ref[par, 1]
            at = pl.ds(pl.multiple_of(16 * j, 16), 16)
            keep_ref[0, at, :] = cosine
            keep_ref[1, at, :] = sine
            for t, value in enumerate((cosine, sine, -wave * cosine, wave * sine)):
                high, low = split(value)
                tab_ref[4 * par + t, 0, at, :] = high
                tab_ref[4 * par + t, 1, at, :] = low
            return 0

        lax.fori_loop(0, ROWS // 16, rows, 0)
        for t in range(2):
            for block in range(4):
                cut = slice(128 * block, 128 * (block + 1))
                value = jnp.transpose(keep_ref[t, cut, :])
                if t == 1:
                    value = -value
                if block == 0:
                    value = value * halve
                high, low = split(value)
                back_ref[2 * par + t, 0, :, cut] = high
                back_ref[2 * par + t, 1, :, cut] = low


def small_tables():
    scale = 1.0 / math.sqrt(MODES)
    step = 2.0 * math.pi / POINTS
    rows1, rows2 = [], []
    for par in range(2):
        m = 2 * np.arange(HALF) + par

        def pair(k, factor):
            angle = ((k[:, None] * m[None, :]) % POINTS) * step
            return np.stack([np.cos(angle), np.sin(angle)]) * factor

        rows1.append(pair(16 * np.arange(ROWS // 16), 1.0))
        rows2.append(pair(np.arange(16), scale))
    return [np.stack(x).astype(np.float32) for x in (rows1, rows2)]


def tables(parts):
    return pl.pallas_call(
        table_kernel,
        out_shape=(
            jax.ShapeDtypeStruct((8, 2, ROWS, HALF), jnp.bfloat16),
            jax.ShapeDtypeStruct((4, 2, HALF, QUARTER), jnp.bfloat16),
        ),
        scratch_shapes=[pltpu.VMEM((2, ROWS, HALF), jnp.float32)],
        compiler_params=pltpu.CompilerParams(vmem_limit_bytes=48 * MIB),
        cost_estimate=pl.CostEstimate(
            flops=16 * ROWS * HALF, bytes_accessed=15 * MIB, transcendentals=0
        ),
        name="tables",
    )(*parts)


def grid_kernel(
    got_ref, tab_hbm, back_hbm, rows_ref,
    out_ref,
    tab_ref, back_ref, sems, x_ref, wave_ref, high_ref, low_ref, edge_ref,
):
    copies = [
        pltpu.make_async_copy(tab_hbm.at[t], tab_ref.at[t], sems.at[t]) for t in range(8)
    ] + [
        pltpu.make_async_copy(back_hbm.at[i], back_ref.at[i], sems.at[8 + i]) for i in range(4)
    ]
    for copy in copies[:3]:
        copy.start()
    for i in range(4):
        x_ref[i] = got_ref[:, i * PAIRS : (i + 1) * PAIRS, :].reshape(HALF, LANES)
    which = (0, 1, 1, 0, 2, 3, 3, 2)
    for t in range(8):
        copies[t].wait()
        copies[t + 3].start()
        x = x_ref[which[t]]
        wave_ref[t] = mm(tab_ref[t, 0], x) + mm(tab_ref[t, 1], x)
    copies[11].start()
    cor = rows_ref[0:1, :]

    def quads(base, at, lanes):
        ce, se = wave_ref[base, at, lanes], wave_ref[base + 1, at, lanes]
        co, so = wave_ref[base + 4, at, lanes], wave_ref[base + 5, at, lanes]
        a, b, s, d = ce + co, ce - co, se + so, se - so
        return a - s, b + d, b - d, a + s

    def tendency(at):
        cuts = [pl.ds(128 * f, 128) for f in range(3)]
        values = [quads(0, at, cut) for cut in cuts]
        slopes = [quads(2, at, cut) for cut in cuts]
        out = [[], [], []]
        for q in range(4):
            u, v, h = (values[f][q] for f in range(3))
            us, vs, hs = (slopes[f][q] for f in range(3))
            out[0].append(cor * v - u * us - hs)
            out[1].append(-u * vs - cor * u)
            out[2].append(-u * hs - (1.0 + h) * us)
        folded = []
        for t1, t2, t3, t4 in out:
            a, b, c, d = t1 + t4, t2 + t3, t1 - t4, t3 - t2
            folded.append((a + b, c + d, a - b, c - d))
        return folded

    def block(j, _):
        at = pl.ds(pl.multiple_of(16 * j, 16), 16)
        for f, folded in enumerate(tendency(at)):
            for i, value in enumerate(folded):
                high, low = split(value)
                high_ref[i, at, pl.ds(128 * f, 128)] = high
                low_ref[i, at, pl.ds(128 * f, 128)] = low
        return 0

    lax.fori_loop(0, QUARTER // 16, block, 0)
    for f, folded in enumerate(tendency(pl.ds(QUARTER, 16))):
        edge_ref[0, :, pl.ds(128 * f, 128)] = folded[0]
        edge_ref[1, :, pl.ds(128 * f, 128)] = folded[3]

    odd_row = (lax.broadcasted_iota(jnp.int32, (HALF, 1), 0) & 1) == 1
    half_scale = 0.5 / math.sqrt(MODES)
    sign = jnp.where(odd_row, -half_scale, half_scale)
    weight, signed = rows_ref[1:2, :], rows_ref[2:3, :]
    for par in range(2):
        both = []
        for c in range(2):
            i = 2 * par + c
            copies[8 + i].wait()
            out = mm(back_ref[i, 0], high_ref[i]) + mm(back_ref[i, 1], high_ref[i])
            out = out + mm(back_ref[i, 0], low_ref[i])
            if i == 0:
                out = out + sign * edge_ref[0, 0:1, :]
            if i == 3:
                out = out - sign * edge_ref[1, 0:1, :]
            both.append(out)
        for f in range(3):
            parts = []
            for out in both:
                part = out[:, 128 * f : 128 * (f + 1)]
                part = pltpu.roll(part, 64, 1) * weight + part * signed
                parts.append(part.reshape(NBAND, 2, 8, 128))
            joined = jnp.concatenate(parts, axis=2).astype(jnp.bfloat16)
            for h in range(2):
                z = 2 * par + h
                out_ref[z * NBAND : (z + 1) * NBAND, :, 128 * f : 128 * (f + 1)] = joined[:, h]


def grid_stage(got, tab, back, rows):
    return pl.pallas_call(
        grid_kernel,
        in_specs=[
            pl.BlockSpec(memory_space=pltpu.VMEM),
            pl.BlockSpec(memory_space=pl.ANY),
            pl.BlockSpec(memory_space=pl.ANY),
            pl.BlockSpec(memory_space=pltpu.VMEM),
        ],
        out_shape=jax.ShapeDtypeStruct((4 * NBAND, 16, LANES), jnp.bfloat16),
        scratch_shapes=[
            pltpu.VMEM((8, 2, ROWS, HALF), jnp.bfloat16),
            pltpu.VMEM((4, 2, HALF, QUARTER), jnp.bfloat16),
            pltpu.SemaphoreType.DMA((12,)),
            pltpu.VMEM((4, HALF, LANES), jnp.bfloat16),
            pltpu.VMEM((8, ROWS, LANES), jnp.float32),
            pltpu.VMEM((4, QUARTER, LANES), jnp.bfloat16),
            pltpu.VMEM((4, QUARTER, LANES), jnp.bfloat16),
            pltpu.VMEM((2, 16, LANES), jnp.float32),
        ],
        compiler_params=pltpu.CompilerParams(vmem_limit_bytes=48 * MIB),
        cost_estimate=pl.CostEstimate(
            flops=2 * 28 * ROWS * HALF * LANES, bytes_accessed=17 * MIB, transcendentals=0
        ),
        name="grid",
    )(got, tab, back, rows)


def analysis_kernel(
    id_ref, quad_ref, y_ref, leg_ref, move0_ref, move1_ref, move2_ref, move3_ref, st_ref, damp_ref,
    out0_ref, out1_ref, out2_ref, out3_ref, sums_ref,
    wide_ref, rate_ref, start_ref, mix_ref, acc_ref,
):
    step = pl.program_id(0)
    node = id_ref[0]
    order = [(node + 4 - s) % 4 for s in range(4)]

    @pl.when(step == 0)
    def _():
        acc_ref[...] = jnp.zeros_like(acc_ref)
        low = lax.broadcasted_iota(jnp.int32, (16, 128), 1) < 64
        for s in range(4):
            for f in range(3):
                for e in range(4):
                    for t in range(4):
                        first, second = (
                            y_ref[
                                order[s] * NBAND + 8 * e + 2 * t + g, :, 128 * f : 128 * (f + 1)
                            ].astype(jnp.float32)
                            for g in range(2)
                        )
                        symmetric = jnp.where(low, first, second)
                        antisymmetric = jnp.where(low, second, first)
                        for c in range(2):
                            row = (((s * 2 + c) * 3 + f) * 4 + e) * 8
                            wide_ref[0, t, row : row + 8, :] = symmetric[8 * c : 8 * c + 8]
                            wide_ref[1, t, row : row + 8, :] = antisymmetric[8 * c : 8 * c + 8]

    for k in range(MB):
        at = step * MB + k
        mode = 2 * (8 * (node % 2) + at) + node // 2
        for c in range(2):
            for f in range(3):
                row = (c * 3 + f) * 4
                rate_ref[pl.ds(row, 4), :] = jnp.broadcast_to(
                    damp_ref[f, pl.ds(mode, 1), :], (4, DEGREES)
                )
                start_ref[pl.ds(row, 4), :] = st_ref[c, k, f]
        halves = []
        for h in range(2):
            spec = jnp.concatenate(
                [wide_ref[h, t, pl.ds(at, 4 * COLS, stride=8), :] for t in range(4)], axis=1
            ).astype(jnp.bfloat16)
            if h == 0:
                table = leg_ref[k, :, :256]
            else:
                blocks = [leg_ref[k, 64 * (b ^ 1) : 64 * (b ^ 1) + 64, 256:] for b in range(8)]
                table = jnp.concatenate(blocks, axis=0)
            halves.append(mm(spec, table))
        for h in range(2):
            cut = slice(256 * h, 256 * (h + 1))
            rate, start = rate_ref[:, cut], start_ref[:, cut]
            moves = [
                decode(ref[k // 2, COLS * (k % 2) : COLS * (k % 2 + 1), cut])
                for ref in (move0_ref, move1_ref, move2_ref, move3_ref)
            ]
            forces = [
                halves[h][COLS * p : COLS * (p + 1)] - rate * moves[p] for p in range(4)
            ]
            change = jnp.zeros_like(start)
            for q in range(4):
                row = [quad_ref[order[q], order[p]] for p in range(4)]
                mine = row[q] * rate
                inverse = 1.0 / (1.0 + mine)
                mixed = (
                    row[0] * forces[0] + row[1] * forces[1] + row[2] * forces[2] + row[3] * forces[3]
                ) * inverse
                total = row[0] + row[1] + row[2] + row[3]
                old = start + moves[q]
                moved = mixed + (start * (1.0 - rate * total) + mine * old) * inverse - old
                change = change + moved * moved
                mix_ref[q, COLS * k : COLS * (k + 1), cut] = mixed
            acc_ref[0, :, cut] += change
            acc_ref[1, :, cut] += start * start
    for s, ref in enumerate((out0_ref, out1_ref, out2_ref, out3_ref)):
        ref[...] = encode(mix_ref[s])

    @pl.when(step == pl.num_programs(0) - 1)
    def _():
        field = lax.broadcasted_iota(jnp.int32, (COLS, 1), 0) // 4 % 3
        lane = lax.broadcasted_iota(jnp.int32, (1, 128), 1)
        sums = jnp.zeros((1, 128), jnp.float32)
        for s in range(2):
            per_row = jnp.sum(acc_ref[s], axis=1, keepdims=True)
            for f in range(3):
                value = jnp.sum(jnp.where(field == f, per_row, 0.0), axis=0, keepdims=True)
                sums = sums + jnp.where(lane == 3 * s + f, value, 0.0)
        sums_ref[...] = sums


def analysis(ids, quad, y, leg4, moves, st6, damp):
    spec = pl.BlockSpec
    return pl.pallas_call(
        analysis_kernel,
        grid_spec=pltpu.PrefetchScalarGridSpec(
            num_scalar_prefetch=1,
            grid=(2,),
            in_specs=[
                spec(memory_space=pltpu.SMEM),
                spec((4 * NBAND, 16, LANES), lambda i, s: (0, 0, 0)),
                spec(
                    (MB, None, LATS, DEGREES), lambda i, s: (s[0] % 2 * 2 + i, s[0] // 2, 0, 0)
                ),
                *[spec((2, 2 * COLS, DEGREES), lambda i, s: (i, 0, 0))] * 4,
                spec(
                    (2, MB, None, 3, 4, DEGREES),
                    lambda i, s: (0, s[0] % 2 * 2 + i, s[0] // 2, 0, 0, 0),
                ),
                spec((3, 32, DEGREES), lambda i, s: (0, 0, 0)),
            ],
            out_specs=(
                *[spec((MB * COLS, DEGREES), lambda i, s: (i, 0))] * 4,
                spec((1, 128), lambda i, s: (0, 0)),
            ),
            scratch_shapes=[
                pltpu.VMEM((2, 4, 4 * COLS * 8, 128), jnp.float32),
                pltpu.VMEM((COLS, DEGREES), jnp.float32),
                pltpu.VMEM((COLS, DEGREES), jnp.float32),
                pltpu.VMEM((4, MB * COLS, DEGREES), jnp.float32),
                pltpu.VMEM((2, COLS, DEGREES), jnp.float32),
            ],
        ),
        out_shape=(
            *[jax.ShapeDtypeStruct((8 * COLS, DEGREES), jnp.bfloat16)] * 4,
            jax.ShapeDtypeStruct((1, 128), jnp.float32),
        ),
        compiler_params=pltpu.CompilerParams(vmem_limit_bytes=56 * MIB),
        cost_estimate=pl.CostEstimate(
            flops=2 * 32 * COLS * LATS * DEGREES, bytes_accessed=10 * MIB, transcendentals=0
        ),
        name="analysis",
    )(ids, quad, y, leg4, *moves, st6, damp)


def update_kernel(
    id_ref, mixed0_ref, mixed1_ref, mixed2_ref, mixed3_ref, base_ref, out_ref, mix_ref
):
    place = pl.program_id(0)
    for s, ref in enumerate((mixed0_ref, mixed1_ref, mixed2_ref, mixed3_ref)):

        @pl.when(place == s)
        def _(ref=ref):
            mix_ref[...] = decode(ref[...])

    for k in range(8):
        for c in range(2):
            for f in range(3):
                row = COLS * k + (c * 3 + f) * 4
                out_ref[c, k, f] = base_ref[c, k, f] + mix_ref[row : row + 4, :]


def update(ids, mixed, base):
    spec = pl.BlockSpec
    state = spec(STATE, own_subset)
    return pl.pallas_call(
        update_kernel,
        grid_spec=pltpu.PrefetchScalarGridSpec(
            num_scalar_prefetch=1,
            grid=(4,),
            in_specs=[*[spec((8 * COLS, DEGREES), lambda i, s: (0, 0))] * 4, state],
            out_specs=state,
            scratch_shapes=[pltpu.VMEM((8 * COLS, DEGREES), jnp.float32)],
        ),
        out_shape=jax.ShapeDtypeStruct(base.shape, jnp.float32),
        compiler_params=pltpu.CompilerParams(vmem_limit_bytes=32 * MIB),
        cost_estimate=pl.CostEstimate(
            flops=4 * 32 * COLS * DEGREES, bytes_accessed=5 * MIB, transcendentals=0
        ),
        name="update",
    )(ids, *mixed, base)


def exchange(x, axes):
    return lax.all_to_all(x, axes, split_axis=0, concat_axis=0, tiled=True)


def shift(x, axis, by):
    return lax.ppermute(x, axis, [(i, (i + by) % 4) for i in range(4)])


def latitude_rows(band, coriolis, lat_weight):
    count = LATS // 8
    group = band % 8
    cor = lax.dynamic_slice_in_dim(coriolis, group * count, count, 1)
    weight = lax.dynamic_slice_in_dim(lat_weight, group * count, count, 0)
    swapped = group % 2 == 1
    cor = jnp.where(swapped, cor[::-1], cor).reshape(1, 128)
    weight = jnp.concatenate([weight, weight])[None]
    south = lax.broadcasted_iota(jnp.int32, (1, 128), 1) >= count
    signed = jnp.where(south != swapped, -weight, weight)
    return jnp.concatenate([cor, weight, signed], axis=0)


def body(state0, iterate, legendre, lat_weight, coriolis, damping, quadrature):
    node = lax.axis_index("node")
    band = lax.axis_index(BAND)
    spec = iterate[0].transpose(0, 1, 3, 2, 4)
    base = state0.transpose(0, 1, 3, 2, 4)
    it6 = spec.reshape(2, PAIRS, 2, 3, 4, DEGREES)
    st6 = base.reshape(2, PAIRS, 2, 3, 4, DEGREES)
    leg4 = legendre.reshape(PAIRS, 2, LATS, DEGREES)
    damp = damping.transpose(1, 0, 2)
    ids = jnp.reshape(node, (1,)).astype(jnp.int32)

    shape7 = (2, 2, 8, 2, 3, 4, DEGREES)
    sent = synthesis(it6, leg4)
    got = exchange(sent, BAND)
    parts = [jnp.asarray(x) for x in small_tables()]
    late, _ = lax.optimization_barrier(((parts, quadrature), sent))
    parts, quad = late
    *moves, settled = prepare(ids, quad, base.reshape(shape7), spec.reshape(shape7), damp)
    moves = [moves[0]] + [shift(moves[s], "node", s) for s in (1, 2, 3)]
    tab, back = tables(parts)
    rows = latitude_rows(band, coriolis, lat_weight)
    rows, moves = lax.optimization_barrier((rows, moves))
    moves = [x.reshape(4, 2 * COLS, DEGREES) for x in moves]
    spectra = exchange(grid_stage(got, tab, back, rows), NODE_BAND)
    *mixed, sums = analysis(ids, quadrature, spectra, leg4, moves, st6, damp)
    mixed = [mixed[0]] + [shift(mixed[s], "node", -s) for s in (1, 2, 3)]
    sums = exchange(jnp.broadcast_to(sums[None], (4 * NBAND, 1, 128)), NODE_BAND)
    out = update(ids, mixed, settled)
    sums, out = lax.optimization_barrier((sums, out))
    total = jnp.sum(sums, axis=(0, 1))
    ratio = jnp.sqrt(total[:3] / (4.0 * total[3:6] + 1e-06))
    out = out.reshape(2, 32, 3, 4, DEGREES).transpose(0, 1, 3, 2, 4)
    return (out[None], ratio)


def solution(mesh):
    torus = Mesh(
        mesh.devices.reshape(mesh.shape["node"], 4, 4, 2), ("node", "band_0", "band_1", "band_2")
    )
    return jax.shard_map(
        body,
        mesh=torus,
        in_specs=(
            P(None, BAND, None, None, None),
            P("node", None, BAND, None, None, None),
            P(BAND, None, None),
            P(),
            P(),
            P(BAND, None, None),
            P(),
        ),
        out_specs=(P("node", None, BAND, None, None, None), P()),
        check_vma=False,
    )
```

time: 157 us -> 119 us (0.76)
  waiting for transfers between devices: 39.6 us -> 8.93 us
  blocking collectives: 45.2 us -> 31.2 us
  starting transfers between devices: 13.8 us -> 23.9 us
  Pallas kernels: 52.2 us -> 45.7 us
  local copies, waits for them, and re-layouts: 4.22 us -> 7.44 us
    all_to_all x3 -> x2, waiting for transfers between devices: 39.6 us -> 7.08 us  [exchange(): return lax.all_to_all(x, axes, split_axis=0, concat_axis=0, tiled=True)]
    all_to_all x2 -> x1, blocking collectives: 45.2 us -> 31.2 us  [exchange(): return lax.all_to_all(x, axes, split_axis=0, concat_axis=0, tiled=True)]
    ppermute x0 -> x6, starting transfers between devices: none -> 8 us  [shift(): return lax.ppermute(x, axis, [(i, (i + by) % 4) for i in range(4)])]
    pallas_call x1, Pallas kernels: 12.7 us -> 6.73 us  [analysis(): pl.pallas_call(analysis_kernel, grid_spec=pltpu.PrefetchScalarGridSpec(nu...]
    unnamed x20 -> x32, local copies, waits for them, and re-layouts: 2.4 us -> 5.82 us
    pallas_call x1, Pallas kernels: 3.56 us -> 5.92 us  [tables(): pl.pallas_call(table_kernel, out_shape=(jax.ShapeDtypeStruct((8, 2, ROWS,...]
    all_to_all x3 -> x2, starting transfers between devices: 13.8 us -> 16 us  [exchange(): return lax.all_to_all(x, axes, split_axis=0, concat_axis=0, tiled=True)]
    ppermute x0 -> x6, waiting for transfers between devices: none -> 1.85 us  [shift(): return lax.ppermute(x, axis, [(i, (i + by) % 4) for i in range(4)])]
  transfers between devices with their start and end apart: 3 -> 8, of which waited for: 3 -> 3; matrix products, arithmetic and copies ran while one was open for 1% -> 2% of each run, Pallas kernels for 9% -> 9%
where the time goes in v3:
time: 119 us
  Pallas kernels  45.7 us (38%)
  blocking collectives  31.2 us (26%)
  starting transfers between devices  23.9 us (20%)
  waiting for transfers between devices  8.93 us (8%)
  local copies, waits for them, and re-layouts  7.44 us (6%)
    all_to_all x1, blocking collectives, exchange(): return lax.all_to_all(x, axes, split_axis=0, concat_axis=0, tiled=True)  31.2 us
    all_to_all x2, starting transfers between devices, exchange(): return lax.all_to_all(x, axes, split_axis=0, concat_axis=0, tiled=True)  16 us
    pallas_call x1, Pallas kernels, grid_stage(): pl.pallas_call(grid_kernel, in_specs=[pl.BlockSpec(memory_space=pltpu.VME...  14.6 us
    pallas_call x1, Pallas kernels, synthesis(): pl.pallas_call(synthesis_kernel, in_specs=[pl.BlockSpec(memory_space=pl.A...  13.1 us
    ppermute x6, starting transfers between devices, shift(): return lax.ppermute(x, axis, [(i, (i + by) % 4) for i in range(4)])  8 us
    all_to_all x2, waiting for transfers between devices, exchange(): return lax.all_to_all(x, axes, split_axis=0, concat_axis=0, tiled=True)  7.08 us
    pallas_call x1, Pallas kernels, analysis(): pl.pallas_call(analysis_kernel, grid_spec=pltpu.PrefetchScalarGridSpec(nu...  6.73 us
    pallas_call x1, Pallas kernels, tables(): pl.pallas_call(table_kernel, out_shape=(jax.ShapeDtypeStruct((8, 2, ROWS,...  5.92 us
  transfers between devices with their start and end apart: 8, of which 3 were waited for; matrix products, arithmetic and copies ran while one was open for 2% of the time, Pallas kernels for 9%

profile of v3, /device:TPU:1, one launch (start us, length us, event | category | flops | bytes accessed | tf_op | source)
XLA Modules:
  0.0 119.0 jit_solution(372656982070592018)
XLA Ops:
  0.6 13.1 %synthesis.1 = bf16[32,64,384]{2,1,0:T(8,128)(2,1)} custom-call(f32[2,16,2,3,4,512]{5,4,3,2,1,0:T(4,128)} %bitcast.29, bf16[16,2,512,512]{3,2,1,0:T(8,128)(2,1)} %bitcast.36), custom_call_target="tpu_custom_call" | custom-call | flops 402653184 | bytes 20971520 | tf_op jit(solution)/shard_map/synthesis/pallas_call | solution.py:92
  13.8 8.9 %all-to-all-start = ((bf16[32,64,384]{2,1,0:T(8,128)(2,1)}), bf16[32,64,384]{2,1,0:T(8,128)(2,1)}, u32[]{:S(2)}, u32[]{:S(2)}) async-start(bf16[32,64,384]{2,1,0:T(8,128)(2,1)} %synthesis.1), calls=%async_computation | async-start | bytes 3145728 | tf_op jit(solution)/shard_map/all_to_all | solution.py:549
  22.8 3.0 %prepare.1 = (bf16[192,512]{1,0:T(8,128)(2,1)S(1)}, bf16[192,512]{1,0:T(8,128)(2,1)}, bf16[192,512]{1,0:T(8,128)(2,1)}, bf16[192,512]{1,0:T(8,128)(2,1)}, f32[2,2,8,2,3,4,512]{6,5,4,3,2,1,0:T(4,128)S(1)}) custom-call(s32[1]{0:T(128)} %bitcast.id_ref, f32[4,4]{1,0:T(4,128)S(1)} %copy-done.9, f32[2,2,8,2,3,4,512]{6,5,4,3,2,1,0:T(4,128)S(1)} %bitcast.32, ...), custom_call_target="tpu_custom_call" | custom-call | flops 3145728 | bytes 6291456 | tf_op jit(solution)/shard_map/prepare/pallas_call | solution.py:161
  25.8 1.2 copy-done.2
  27.0 0.7 copy-done.6
  27.6 1.6 %collective-permute-start = (bf16[192,512]{1,0:T(8,128)(2,1)}, bf16[192,512]{1,0:T(8,128)(2,1)S(1)}, u32[]{:S(2)}, u32[]{:S(2)}) collective-permute-start(bf16[192,512]{1,0:T(8,128)(2,1)} %get-tuple-element.30), channel_id=1, source_target_pairs={{0,32},{32,64},{64,96},{96,0},{1,33},{33,65},{65,97},{97,1},{2,34}... | collective-permute-start | bytes 589832 | tf_op jit(solution)/shard_map/ppermute | solution.py:553
  29.2 3.3 %collective-permute-start.1 = (bf16[192,512]{1,0:T(8,128)(2,1)}, bf16[192,512]{1,0:T(8,128)(2,1)S(1)}, u32[]{:S(2)}, u32[]{:S(2)}) collective-permute-start(bf16[192,512]{1,0:T(8,128)(2,1)} %get-tuple-element.31), channel_id=1, source_target_pairs={{0,64},{32,96},{64,0},{96,32},{1,65},{33,97},{65,1},{97,33},{2,66}... | collective-permute-start | bytes 589832 | tf_op jit(solution)/shard_map/ppermute | solution.py:553
  32.6 0.7 collective-permute-start.2
  33.3 0.1 dynamic_slice.7
  33.4 0.1 constant_dynamic-slice_fusion
  33.5 0.1 broadcast_select_fusion
  33.5 0.1 reshape.116
  33.6 1.0 copy-done.5
  34.6 5.9 %tables.1 = (bf16[8,2,528,512]{3,2,1,0:T(8,128)(2,1)}, bf16[4,2,512,512]{3,2,1,0:T(8,128)(2,1)S(1)}) custom-call(f32[2,2,33,512]{3,2,1,0:T(8,128)S(1)} %copy-done.5, f32[2,2,16,512]{3,2,1,0:T(8,128)S(1)} %copy-done.8), custom_call_target="tpu_custom_call" | custom-call | flops 4325376 | bytes 15728640 | tf_op jit(solution)/shard_map/tables/pallas_call | solution.py:243
  40.5 2.0 %copy-done.10 = bf16[4,2,512,512]{3,2,1,0:T(8,128)(2,1)} copy-done((bf16[4,2,512,512]{3,2,1,0:T(8,128)(2,1)}, bf16[4,2,512,512]{3,2,1,0:T(8,128)(2,1)S(1)}, u32[]{:S(2)}) %copy-start.10) | copy-done | bytes 4194328
  42.6 0.1 dynamic-slice_bitcast_fusion
  42.6 0.1 compare_select_fusion
  42.7 0.1 maximum_bitcast_fusion
  42.8 2.6 %all-to-all-done.got_ref = bf16[32,64,384]{2,1,0:T(8,128)(2,1)} async-done(((bf16[32,64,384]{2,1,0:T(8,128)(2,1)}), bf16[32,64,384]{2,1,0:T(8,128)(2,1)}, u32[]{:S(2)}, u32[]{:S(2)}) %all-to-all-start) | async-done | bytes 1572896 | tf_op jit(solution)/shard_map/all_to_all | solution.py:549
  45.5 14.6 %grid.1 = bf16[128,16,384]{2,1,0:T(8,128)(2,1)S(1)} custom-call(bf16[32,64,384]{2,1,0:T(8,128)(2,1)} %all-to-all-done.got_ref, bf16[8,2,528,512]{3,2,1,0:T(8,128)(2,1)} %get-tuple-element.26.tab_hbm, bf16[4,2,512,512]{3,2,1,0:T(8,128)(2,1)} %copy-done.10, f32[3,128]{1,0:T(4,128)S(1)} %pad_maximum_fusion.rows_ref), custom_call_target="tpu_custom_call" | custom-call | flops 5813305344 | bytes 17825792 | tf_op jit(solution)/shard_map/grid/pallas_call | solution.py:347
  60.1 31.2 %all_to_all.15.y_ref = bf16[128,16,384]{2,1,0:T(8,128)(2,1)} all-to-all(bf16[128,16,384]{2,1,0:T(8,128)(2,1)S(1)} %grid.1), channel_id=1, replica_groups=mesh['node'=4,'band_0'=4,'band_1'=4,'band_2'=2] {'node','band_0','band_1..., dimensions={0} | all-to-all | bytes 3145728 | tf_op jit(solution)/shard_map/all_to_all | solution.py:549
  91.3 6.7 %analysis.1 = (bf16[192,512]{1,0:T(8,128)(2,1)}, bf16[192,512]{1,0:T(8,128)(2,1)}, bf16[192,512]{1,0:T(8,128)(2,1)}, bf16[192,512]{1,0:T(8,128)(2,1)}, f32[1,128]{1,0:T(1,128)}) custom-call(s32[1]{0:T(128)} %bitcast.id_ref, f32[4,4]{1,0:T(4,128)} %quad_ref.2, bf16[128,16,384]{2,1,0:T(8,128)(2,1)} %all_to_all.15.y_ref, bf16[16,2,512,512]{3,2,1,0:T(8,128)(2,1)} %bitcast.37, ...), custom_call_target="tpu_custom_call" | custom-call | flops 402653184 | bytes 10485760 | tf_op jit(solution)/shard_map/analysis/pallas_call | solution.py:468
  98.0 0.6 collective-permute-start.3
  98.6 1.7 %collective-permute-start.4 = (bf16[192,512]{1,0:T(8,128)(2,1)}, bf16[192,512]{1,0:T(8,128)(2,1)S(1)}, u32[]{:S(2)}, u32[]{:S(2)}) collective-permute-start(bf16[192,512]{1,0:T(8,128)(2,1)} %get-tuple-element.41), channel_id=1, source_target_pairs={{0,64},{32,96},{64,0},{96,32},{1,65},{33,97},{65,1},{97,33},{2,66}... | collective-permute-start | bytes 589832 | tf_op jit(solution)/shard_map/ppermute | solution.py:553
  100.4 1.3 %broadcast_in_dim.16 = f32[128,1,128]{2,1,0:T(1,128)} broadcast(f32[128]{0:T(128)} %bitcast.42), dimensions={2} | broadcast | bytes 66048 | tf_op jit(solution)/shard_map/broadcast_in_dim | solution.py:595
  101.6 7.0 %all-to-all-start.2 = ((f32[128,1,128]{2,1,0:T(1,128)}), f32[128,1,128]{2,1,0:T(1,128)S(1)}, u32[]{:S(2)}, u32[]{:S(2)}) async-start(f32[128,1,128]{2,1,0:T(1,128)} %broadcast_in_dim.16), calls=%async_computation.2 | async-start | bytes 131072 | tf_op jit(solution)/shard_map/all_to_all | solution.py:549
  108.7 1.8 %collective-permute-done.5.mixed3_ref = bf16[192,512]{1,0:T(8,128)(2,1)S(1)} collective-permute-done((bf16[192,512]{1,0:T(8,128)(2,1)}, bf16[192,512]{1,0:T(8,128)(2,1)S(1)}, u32[]{:S(2)}, u32[]{:S(2)}) %collective-permute-start.5) | collective-permute-done | bytes 196640 | tf_op jit(solution)/shard_map/ppermute | solution.py:553
  110.6 0.9 copy-done.7
  111.5 2.4 %update.1 = f32[2,2,8,2,3,4,512]{6,5,4,3,2,1,0:T(4,128)} custom-call(s32[1]{0:T(128)} %bitcast.id_ref, bf16[192,512]{1,0:T(8,128)(2,1)S(1)} %copy-done.7, bf16[192,512]{1,0:T(8,128)(2,1)S(1)} %collective-permute-done.3.mixed1_ref, bf16[192,512]{1,0:T(8,128)(2,1)S(1)} %collective-permute-done.4.mixed2_ref, ...), custom_call_target="tpu_custom_call" | custom-call | flops 1572864 | bytes 5242880 | tf_op jit(solution)/shard_map/update/pallas_call | solution.py:530
  113.8 4.4 %all-to-all-done.2 = f32[128,1,128]{2,1,0:T(1,128)S(1)} async-done(((f32[128,1,128]{2,1,0:T(1,128)}), f32[128,1,128]{2,1,0:T(1,128)S(1)}, u32[]{:S(2)}, u32[]{:S(2)}) %all-to-all-start.2) | async-done | bytes 65568 | tf_op jit(solution)/shard_map/all_to_all | solution.py:549
  118.3 0.2 reduce_sum.9
  118.4 0.6 fusion
  (35 shorter events, 0.1 us)
Async XLA Ops:
  0.6 22.1 %copy-start.4 = (f32[32,3,512]{2,0,1:T(8,128)S(1)}, f32[32,3,512]{2,0,1:T(8,128)}, u32[]{:S(2)}) copy-start(f32[32,3,512]{2,0,1:T(8,128)} %param.14) | copy-start | bytes 589828
  13.8 9.0 %copy-start = (f32[1,2,32,4,3,512]{5,3,4,2,1,0:T(4,128)S(1)}, f32[1,2,32,4,3,512]{5,3,4,2,1,0:T(4,128)}, u32[]{:S(2)}) copy-start(f32[1,2,32,4,3,512]{5,3,4,2,1,0:T(4,128)} %param.10) | copy-start | bytes 4718596
  13.8 9.0 %copy-start.1 = (f32[2,32,4,3,512]{4,2,3,1,0:T(4,128)S(1)}, f32[2,32,4,3,512]{4,2,3,1,0:T(4,128)}, u32[]{:S(2)}) copy-start(f32[2,32,4,3,512]{4,2,3,1,0:T(4,128)} %param.9) | copy-start | bytes 4718596
  13.8 9.0 %copy-start.9 = (f32[4,4]{1,0:T(4,128)S(1)}, f32[4,4]{1,0:T(4,128)}, u32[]{:S(2)}) copy-start(f32[4,4]{1,0:T(4,128)} %quad_ref.2) | copy-start | bytes 196
  13.8 31.7 %all-to-all-start = ((bf16[32,64,384]{2,1,0:T(8,128)(2,1)}), bf16[32,64,384]{2,1,0:T(8,128)(2,1)}, u32[]{:S(2)}, u32[]{:S(2)}) async-start(bf16[32,64,384]{2,1,0:T(8,128)(2,1)} %synthesis.1), calls=%async_computation | async-start | bytes 3145728 | tf_op jit(solution)/shard_map/all_to_all | solution.py:549
  22.8 10.5 %copy-start.15 = (f32[512]{0:T(512)S(1)}, f32[512]{0:T(512)}, u32[]{:S(2)}) copy-start(f32[512]{0:T(512)} %param.12) | copy-start | bytes 6148
  22.8 10.6 %copy-start.14 = (f32[2,512]{1,0:T(2,128)S(1)}, f32[2,512]{1,0:T(2,128)}, u32[]{:S(2)}) copy-start(f32[2,512]{1,0:T(2,128)} %param.13) | copy-start | bytes 12292
  22.8 10.8 %copy-start.8 = (f32[2,2,16,512]{3,2,1,0:T(8,128)S(1)}, f32[2,2,16,512]{3,2,1,0:T(8,128)}, u32[]{:S(2)}) copy-start(f32[2,2,16,512]{3,2,1,0:T(8,128)} %constant.56.clone.row2_ref) | copy-start | bytes 393220
  25.8 1.2 copy-start.2
  26.9 0.7 copy-start.6
  27.6 15.2 %collective-permute-start = (bf16[192,512]{1,0:T(8,128)(2,1)}, bf16[192,512]{1,0:T(8,128)(2,1)S(1)}, u32[]{:S(2)}, u32[]{:S(2)}) collective-permute-start(bf16[192,512]{1,0:T(8,128)(2,1)} %get-tuple-element.30), channel_id=1, source_target_pairs={{0,32},{32,64},{64,96},{96,0},{1,33},{33,65},{65,97},{97,1},{2,34}... | collective-permute-start | bytes 589832 | tf_op jit(solution)/shard_map/ppermute | solution.py:553
  29.2 13.6 %collective-permute-start.1 = (bf16[192,512]{1,0:T(8,128)(2,1)}, bf16[192,512]{1,0:T(8,128)(2,1)S(1)}, u32[]{:S(2)}, u32[]{:S(2)}) collective-permute-start(bf16[192,512]{1,0:T(8,128)(2,1)} %get-tuple-element.31), channel_id=1, source_target_pairs={{0,64},{32,96},{64,0},{96,32},{1,65},{33,97},{65,1},{97,33},{2,66}... | collective-permute-start | bytes 589832 | tf_op jit(solution)/shard_map/ppermute | solution.py:553
  32.6 10.3 %collective-permute-start.2 = (bf16[192,512]{1,0:T(8,128)(2,1)}, bf16[192,512]{1,0:T(8,128)(2,1)S(1)}, u32[]{:S(2)}, u32[]{:S(2)}) collective-permute-start(bf16[192,512]{1,0:T(8,128)(2,1)} %get-tuple-element.32), channel_id=1, source_target_pairs={{0,96},{32,0},{64,32},{96,64},{1,97},{33,1},{65,33},{97,65},{2,98}... | collective-permute-start | bytes 589832 | tf_op jit(solution)/shard_map/ppermute | solution.py:553
  33.6 1.0 copy-start.5
  40.5 2.0 %copy-start.10 = (bf16[4,2,512,512]{3,2,1,0:T(8,128)(2,1)}, bf16[4,2,512,512]{3,2,1,0:T(8,128)(2,1)S(1)}, u32[]{:S(2)}) copy-start(bf16[4,2,512,512]{3,2,1,0:T(8,128)(2,1)S(1)} %get-tuple-element.27.back_hbm) | copy-start | bytes 12582916
  42.8 17.2 %copy-start.11 = (bf16[192,512]{1,0:T(8,128)(2,1)}, bf16[192,512]{1,0:T(8,128)(2,1)S(1)}, u32[]{:S(2)}) copy-start(bf16[192,512]{1,0:T(8,128)(2,1)S(1)} %collective-permute-done) | copy-start | bytes 589828
  42.8 17.2 %copy-start.12 = (bf16[192,512]{1,0:T(8,128)(2,1)}, bf16[192,512]{1,0:T(8,128)(2,1)S(1)}, u32[]{:S(2)}) copy-start(bf16[192,512]{1,0:T(8,128)(2,1)S(1)} %collective-permute-done.1) | copy-start | bytes 589828
  42.8 17.2 %copy-start.13 = (bf16[192,512]{1,0:T(8,128)(2,1)}, bf16[192,512]{1,0:T(8,128)(2,1)S(1)}, u32[]{:S(2)}) copy-start(bf16[192,512]{1,0:T(8,128)(2,1)S(1)} %collective-permute-done.2) | copy-start | bytes 589828
  91.3 19.3 %copy-start.3 = (f32[2,2,8,2,3,4,512]{6,5,4,3,2,1,0:T(4,128)S(1)}, f32[2,2,8,2,3,4,512]{6,5,4,3,2,1,0:T(4,128)}, u32[]{:S(2)}) copy-start(f32[2,2,8,2,3,4,512]{6,5,4,3,2,1,0:T(4,128)} %copy-done.2) | copy-start | bytes 4718596
  98.0 10.7 %collective-permute-start.3 = (bf16[192,512]{1,0:T(8,128)(2,1)}, bf16[192,512]{1,0:T(8,128)(2,1)S(1)}, u32[]{:S(2)}, u32[]{:S(2)}) collective-permute-start(bf16[192,512]{1,0:T(8,128)(2,1)} %get-tuple-element.40), channel_id=1, source_target_pairs={{0,96},{32,0},{64,32},{96,64},{1,97},{33,1},{65,33},{97,65},{2,98}... | collective-permute-start | bytes 589832 | tf_op jit(solution)/shard_map/ppermute | solution.py:553
  98.6 10.1 %collective-permute-start.4 = (bf16[192,512]{1,0:T(8,128)(2,1)}, bf16[192,512]{1,0:T(8,128)(2,1)S(1)}, u32[]{:S(2)}, u32[]{:S(2)}) collective-permute-start(bf16[192,512]{1,0:T(8,128)(2,1)} %get-tuple-element.41), channel_id=1, source_target_pairs={{0,64},{32,96},{64,0},{96,32},{1,65},{33,97},{65,1},{97,33},{2,66}... | collective-permute-start | bytes 589832 | tf_op jit(solution)/shard_map/ppermute | solution.py:553
  100.4 10.2 %collective-permute-start.5 = (bf16[192,512]{1,0:T(8,128)(2,1)}, bf16[192,512]{1,0:T(8,128)(2,1)S(1)}, u32[]{:S(2)}, u32[]{:S(2)}) collective-permute-start(bf16[192,512]{1,0:T(8,128)(2,1)} %get-tuple-element.42), channel_id=1, source_target_pairs={{0,32},{32,64},{64,96},{96,0},{1,33},{33,65},{65,97},{97,1},{2,34}... | collective-permute-start | bytes 589832 | tf_op jit(solution)/shard_map/ppermute | solution.py:553
  101.6 16.6 %all-to-all-start.2 = ((f32[128,1,128]{2,1,0:T(1,128)}), f32[128,1,128]{2,1,0:T(1,128)S(1)}, u32[]{:S(2)}, u32[]{:S(2)}) async-start(f32[128,1,128]{2,1,0:T(1,128)} %broadcast_in_dim.16), calls=%async_computation.2 | async-start | bytes 131072 | tf_op jit(solution)/shard_map/all_to_all | solution.py:549
  110.6 0.9 copy-start.7

commit v4 on v3

--- a/solution.py
+++ b/solution.py
@@ -11,7 +11,8 @@
 from jax.sharding import PartitionSpec as P
 
 BAND = ("band_0", "band_1", "band_2")
-NODE_BAND = ("node",) + BAND
+SEND = ("band_2", "band_1", "band_0")
+SEND_NODE = SEND + ("node",)
 MODES = 1024
 POINTS = 2 * MODES
 HALF = MODES // 2
@@ -37,7 +38,7 @@
 STREAMS = 16
 
 
-def synthesis_kernel(it_hbm, leg_hbm, out_ref, it_ref, leg_ref, sems, coef_ref, wide_ref):
+def synthesis_kernel(it_hbm, leg_hbm, out_ref, it_ref, leg_ref, sems, coef_ref, turn_ref, wide_ref):
     def stream(j):
         return pltpu.make_async_copy(
             leg_hbm.at[pl.ds(j % 8 * 2, 2), j // 8], leg_ref.at[j], sems.at[j]
@@ -50,32 +51,54 @@
     coefficients.wait()
     low = lax.broadcasted_iota(jnp.int32, (COLS, 128), 1) < 64
 
-    def pair(j, _):
-        stream(j).wait()
-        par = j // 8
-        for k in range(2):
-            i = j % 8 * 2 + k
+    left = lax.broadcasted_iota(jnp.int32, (LATS, 128), 1) < 64
+
+    def place(at, t, north, south):
+        south = pltpu.roll(south, 64, 1)
+        rows = pl.ds(at, COLS, stride=2 * PAIRS)
+        wide_ref[2 * t, rows, :] = jnp.where(low, north, south)
+        wide_ref[2 * t + 1, rows, :] = jnp.where(low, south, north)
+
+    def four(j, _):
+        stream(2 * j).wait()
+        stream(2 * j + 1).wait()
+        par, first = j // 4, j % 4 * 4
+        at = par * PAIRS + first
+        for k in range(4):
             for c in range(2):
                 for f in range(3):
                     row = (c * 3 + f) * 4
-                    coef_ref[k, row : row + 4, :] = it_ref[c, i, par, f]
+                    value = it_ref[c, first + k, par, f]
+                    if k < 2:
+                        coef_ref[k, row : row + 4, :] = value
+                    else:
+                        row += 64 * (k - 2)
+                        turn_ref[row : row + 4, :] = value
+                        turn_ref[row + 32 : row + 36, :256] = value[:, :256]
+                        turn_ref[row + 32 : row + 36, 256:] = -value[:, 256:]
+        turned = jnp.transpose(turn_ref[...]).astype(jnp.bfloat16)
+        both = jnp.where(
+            left, mm(leg_ref[2 * j + 1, 0], turned), mm(leg_ref[2 * j + 1, 1], turned)
+        )
+        for k in range(2):
             coeff = coef_ref[k].astype(jnp.bfloat16)
             even = lax.dot_general(
-                coeff[:, :256], leg_ref[j, k, :, :256], NT, preferred_element_type=jnp.float32
+                coeff[:, :256], leg_ref[2 * j, k, :, :256], NT, preferred_element_type=jnp.float32
             )
             odd = lax.dot_general(
-                coeff[:, 256:], leg_ref[j, k, :, 256:], NT, preferred_element_type=jnp.float32
+                coeff[:, 256:], leg_ref[2 * j, k, :, 256:], NT, preferred_element_type=jnp.float32
             )
             for t in range(4):
                 cut = slice(128 * t, 128 * (t + 1))
-                north = even[:, cut] + odd[:, cut]
-                south = pltpu.roll(even[:, cut] - odd[:, cut], 64, 1)
-                rows = pl.ds(par * PAIRS + i, COLS, stride=2 * PAIRS)
-                wide_ref[2 * t, rows, :] = jnp.where(low, north, south)
-                wide_ref[2 * t + 1, rows, :] = jnp.where(low, south, north)
+                place(at + k, t, even[:, cut] + odd[:, cut], even[:, cut] - odd[:, cut])
+        for t in range(4):
+            block = jnp.transpose(both[128 * t : 128 * (t + 1)])
+            for k in range(2):
+                north = block[64 * k : 64 * k + COLS]
+                place(at + 2 + k, t, north, block[64 * k + 32 : 64 * k + 32 + COLS])
         return 0
 
-    lax.fori_loop(0, STREAMS, pair, 0)
+    lax.fori_loop(0, STREAMS // 2, four, 0)
     for p in range(2):
         for c in range(2):
             for f in range(3):
@@ -98,6 +121,7 @@
             pltpu.VMEM((STREAMS, 2, LATS, DEGREES), jnp.bfloat16),
             pltpu.SemaphoreType.DMA((STREAMS + 1,)),
             pltpu.VMEM((2, COLS, DEGREES), jnp.float32),
+            pltpu.VMEM((128, DEGREES), jnp.float32),
             pltpu.VMEM((8, COLS * 2 * PAIRS, 128), jnp.float32),
         ],
         compiler_params=pltpu.CompilerParams(vmem_limit_bytes=56 * MIB),
@@ -187,13 +211,11 @@
     return high, (x - high.astype(jnp.float32)).astype(jnp.bfloat16)
 
 
-def table_kernel(row1_ref, row2_ref, tab_ref, back_ref, keep_ref):
+def table_kernel(row1_ref, row2_ref, wave_ref, tab_ref, back_ref, keep_ref):
     first = lax.broadcasted_iota(jnp.int32, (1, 128), 1) == 0
     halve = jnp.where(first, 0.5, 1.0)
     for par in range(2):
-        wave = (
-            2 * lax.broadcasted_iota(jnp.int32, (1, HALF), 1) + par
-        ).astype(jnp.float32) * (1.0 / MODES)
+        wave = wave_ref[par]
 
         def rows(j, _, par=par, wave=wave):
             lead_c = row1_ref[par, 0, pl.ds(j, 1), :]
@@ -226,9 +248,12 @@
 def small_tables():
     scale = 1.0 / math.sqrt(MODES)
     step = 2.0 * math.pi / POINTS
-    rows1, rows2 = [], []
+    rows1, rows2, waves = [], [], []
+    place = np.arange(NBAND)
+    block = place % 4 * 8 + place // 4 % 4 * 2 + place // 16
+    pairs = (block[:, None] * PAIRS + np.arange(PAIRS)).reshape(-1)
     for par in range(2):
-        m = 2 * np.arange(HALF) + par
+        m = 2 * pairs + par
 
         def pair(k, factor):
             angle = ((k[:, None] * m[None, :]) % POINTS) * step
@@ -236,7 +261,8 @@
 
         rows1.append(pair(16 * np.arange(ROWS // 16), 1.0))
         rows2.append(pair(np.arange(16), scale))
-    return [np.stack(x).astype(np.float32) for x in (rows1, rows2)]
+        waves.append(m[None, :] / MODES)
+    return [np.stack(x).astype(np.float32) for x in (rows1, rows2, waves)]
 
 
 def tables(parts):
@@ -258,24 +284,22 @@
 def grid_kernel(
     got_ref, tab_hbm, back_hbm, rows_ref,
     out_ref,
-    tab_ref, back_ref, sems, x_ref, wave_ref, high_ref, low_ref, edge_ref,
+    tab_ref, back_ref, sems, x_ref, wave_ref, fold_ref, edge_ref,
 ):
     copies = [
         pltpu.make_async_copy(tab_hbm.at[t], tab_ref.at[t], sems.at[t]) for t in range(8)
     ] + [
         pltpu.make_async_copy(back_hbm.at[i], back_ref.at[i], sems.at[8 + i]) for i in range(4)
     ]
-    for copy in copies[:3]:
+    for copy in copies:
         copy.start()
     for i in range(4):
         x_ref[i] = got_ref[:, i * PAIRS : (i + 1) * PAIRS, :].reshape(HALF, LANES)
     which = (0, 1, 1, 0, 2, 3, 3, 2)
     for t in range(8):
         copies[t].wait()
-        copies[t + 3].start()
         x = x_ref[which[t]]
         wave_ref[t] = mm(tab_ref[t, 0], x) + mm(tab_ref[t, 1], x)
-    copies[11].start()
     cor = rows_ref[0:1, :]
 
     def quads(base, at, lanes):
@@ -306,8 +330,8 @@
         for f, folded in enumerate(tendency(at)):
             for i, value in enumerate(folded):
                 high, low = split(value)
-                high_ref[i, at, pl.ds(128 * f, 128)] = high
-                low_ref[i, at, pl.ds(128 * f, 128)] = low
+                fold_ref[i, at, pl.ds(128 * f, 128)] = high
+                fold_ref[i, at, pl.ds(LANES + 128 * f, 128)] = low
         return 0
 
     lax.fori_loop(0, QUARTER // 16, block, 0)
@@ -324,8 +348,9 @@
         for c in range(2):
             i = 2 * par + c
             copies[8 + i].wait()
-            out = mm(back_ref[i, 0], high_ref[i]) + mm(back_ref[i, 1], high_ref[i])
-            out = out + mm(back_ref[i, 0], low_ref[i])
+            both_parts = mm(back_ref[i, 0], fold_ref[i])
+            out = both_parts[:, :LANES] + both_parts[:, LANES:]
+            out = out + mm(back_ref[i, 1], fold_ref[i, :, :LANES])
             if i == 0:
                 out = out + sign * edge_ref[0, 0:1, :]
             if i == 3:
@@ -339,8 +364,7 @@
                 parts.append(part.reshape(NBAND, 2, 8, 128))
             joined = jnp.concatenate(parts, axis=2).astype(jnp.bfloat16)
             for h in range(2):
-                z = 2 * par + h
-                out_ref[z * NBAND : (z + 1) * NBAND, :, 128 * f : 128 * (f + 1)] = joined[:, h]
+                out_ref[:, 2 * par + h, :, 128 * f : 128 * (f + 1)] = joined[:, h]
 
 
 def grid_stage(got, tab, back, rows):
@@ -352,15 +376,14 @@
             pl.BlockSpec(memory_space=pl.ANY),
             pl.BlockSpec(memory_space=pltpu.VMEM),
         ],
-        out_shape=jax.ShapeDtypeStruct((4 * NBAND, 16, LANES), jnp.bfloat16),
+        out_shape=jax.ShapeDtypeStruct((NBAND, 4, 16, LANES), jnp.bfloat16),
         scratch_shapes=[
             pltpu.VMEM((8, 2, ROWS, HALF), jnp.bfloat16),
             pltpu.VMEM((4, 2, HALF, QUARTER), jnp.bfloat16),
             pltpu.SemaphoreType.DMA((12,)),
             pltpu.VMEM((4, HALF, LANES), jnp.bfloat16),
             pltpu.VMEM((8, ROWS, LANES), jnp.float32),
-            pltpu.VMEM((4, QUARTER, LANES), jnp.bfloat16),
-            pltpu.VMEM((4, QUARTER, LANES), jnp.bfloat16),
+            pltpu.VMEM((4, QUARTER, 2 * LANES), jnp.bfloat16),
             pltpu.VMEM((2, 16, LANES), jnp.float32),
         ],
         compiler_params=pltpu.CompilerParams(vmem_limit_bytes=48 * MIB),
@@ -390,7 +413,7 @@
                     for t in range(4):
                         first, second = (
                             y_ref[
-                                order[s] * NBAND + 8 * e + 2 * t + g, :, 128 * f : 128 * (f + 1)
+                                (8 * e + 2 * t + g) * 4 + order[s], :, 128 * f : 128 * (f + 1)
                             ].astype(jnp.float32)
                             for g in range(2)
                         )
@@ -460,7 +483,7 @@
             for f in range(3):
                 value = jnp.sum(jnp.where(field == f, per_row, 0.0), axis=0, keepdims=True)
                 sums = sums + jnp.where(lane == 3 * s + f, value, 0.0)
-        sums_ref[...] = sums
+        sums_ref[...] = jnp.broadcast_to(sums[None], sums_ref.shape)
 
 
 def analysis(ids, quad, y, leg4, moves, st6, damp):
@@ -485,7 +508,7 @@
             ],
             out_specs=(
                 *[spec((MB * COLS, DEGREES), lambda i, s: (i, 0))] * 4,
-                spec((1, 128), lambda i, s: (0, 0)),
+                spec((4 * NBAND, 1, 128), lambda i, s: (0, 0, 0)),
             ),
             scratch_shapes=[
                 pltpu.VMEM((2, 4, 4 * COLS * 8, 128), jnp.float32),
@@ -497,7 +520,7 @@
         ),
         out_shape=(
             *[jax.ShapeDtypeStruct((8 * COLS, DEGREES), jnp.bfloat16)] * 4,
-            jax.ShapeDtypeStruct((1, 128), jnp.float32),
+            jax.ShapeDtypeStruct((4 * NBAND, 1, 128), jnp.float32),
         ),
         compiler_params=pltpu.CompilerParams(vmem_limit_bytes=56 * MIB),
         cost_estimate=pl.CostEstimate(
@@ -553,9 +576,9 @@
     return lax.ppermute(x, axis, [(i, (i + by) % 4) for i in range(4)])
 
 
-def latitude_rows(band, coriolis, lat_weight):
+def latitude_rows(place, coriolis, lat_weight):
     count = LATS // 8
-    group = band % 8
+    group = place % 8
     cor = lax.dynamic_slice_in_dim(coriolis, group * count, count, 1)
     weight = lax.dynamic_slice_in_dim(lat_weight, group * count, count, 0)
     swapped = group % 2 == 1
@@ -568,7 +591,7 @@
 
 def body(state0, iterate, legendre, lat_weight, coriolis, damping, quadrature):
     node = lax.axis_index("node")
-    band = lax.axis_index(BAND)
+    place = lax.axis_index(SEND)
     spec = iterate[0].transpose(0, 1, 3, 2, 4)
     base = state0.transpose(0, 1, 3, 2, 4)
     it6 = spec.reshape(2, PAIRS, 2, 3, 4, DEGREES)
@@ -579,20 +602,21 @@
 
     shape7 = (2, 2, 8, 2, 3, 4, DEGREES)
     sent = synthesis(it6, leg4)
-    got = exchange(sent, BAND)
+    got = exchange(sent, SEND)
     parts = [jnp.asarray(x) for x in small_tables()]
     late, _ = lax.optimization_barrier(((parts, quadrature), sent))
     parts, quad = late
     *moves, settled = prepare(ids, quad, base.reshape(shape7), spec.reshape(shape7), damp)
     moves = [moves[0]] + [shift(moves[s], "node", s) for s in (1, 2, 3)]
     tab, back = tables(parts)
-    rows = latitude_rows(band, coriolis, lat_weight)
+    rows = latitude_rows(place, coriolis, lat_weight)
     rows, moves = lax.optimization_barrier((rows, moves))
     moves = [x.reshape(4, 2 * COLS, DEGREES) for x in moves]
-    spectra = exchange(grid_stage(got, tab, back, rows), NODE_BAND)
+    columns = grid_stage(got, tab, back, rows)
+    spectra = exchange(columns.reshape(4 * NBAND, 16, LANES), SEND_NODE)
     *mixed, sums = analysis(ids, quadrature, spectra, leg4, moves, st6, damp)
     mixed = [mixed[0]] + [shift(mixed[s], "node", -s) for s in (1, 2, 3)]
-    sums = exchange(jnp.broadcast_to(sums[None], (4 * NBAND, 1, 128)), NODE_BAND)
+    sums = exchange(sums, SEND_NODE)
     out = update(ids, mixed, settled)
     sums, out = lax.optimization_barrier((sums, out))
     total = jnp.sum(sums, axis=(0, 1))

time: 119 us -> 117 us (0.983)
  starting transfers between devices: 23.9 us -> 26.3 us
  Pallas kernels: 45.7 us -> 44.1 us
  local copies, waits for them, and re-layouts: 7.44 us -> 6.14 us
    all_to_all x2, waiting for transfers between devices: 7.08 us -> 5.6 us  [exchange(): return lax.all_to_all(x, axes, split_axis=0, concat_axis=0, tiled=True)]
    all_to_all x2, starting transfers between devices: 16 us -> 17.4 us  [exchange(): return lax.all_to_all(x, axes, split_axis=0, concat_axis=0, tiled=True)]
    broadcast_in_dim x1 -> x0, local copies, waits for them, and re-layouts: 1.29 us -> none  [body(): jnp.broadcast_to(sums[None], (4 * NBAND, 1, 128))]
    unnamed x32 -> x34, local copies, waits for them, and re-layouts: 5.82 us -> 5.81 us
  transfers between devices with their start and end apart: 8 -> 8, of which waited for: 3 -> 3; matrix products, arithmetic and copies ran while one was open for 2% -> 0% of each run, Pallas kernels for 9% -> 10%
where the time goes in v4:
time: 117 us
  Pallas kernels  44.1 us (38%)
  blocking collectives  30.1 us (26%)
  starting transfers between devices  26.3 us (22%)
  waiting for transfers between devices  8.6 us (7%)
  local copies, waits for them, and re-layouts  6.14 us (5%)
    all_to_all x1, blocking collectives, exchange(): return lax.all_to_all(x, axes, split_axis=0, concat_axis=0, tiled=True)  30.1 us
    all_to_all x2, starting transfers between devices, exchange(): return lax.all_to_all(x, axes, split_axis=0, concat_axis=0, tiled=True)  17.4 us
    pallas_call x1, Pallas kernels, grid_stage(): pl.pallas_call(grid_kernel, in_specs=[pl.BlockSpec(memory_space=pltpu.VME...  13.9 us
    pallas_call x1, Pallas kernels, synthesis(): pl.pallas_call(synthesis_kernel, in_specs=[pl.BlockSpec(memory_space=pl.A...  12.2 us
    ppermute x6, starting transfers between devices, shift(): return lax.ppermute(x, axis, [(i, (i + by) % 4) for i in range(4)])  8.87 us
    pallas_call x1, Pallas kernels, analysis(): pl.pallas_call(analysis_kernel, grid_spec=pltpu.PrefetchScalarGridSpec(nu...  6.77 us
    pallas_call x1, Pallas kernels, tables(): pl.pallas_call(table_kernel, out_shape=(jax.ShapeDtypeStruct((8, 2, ROWS,...  5.94 us
    unnamed x34, local copies, waits for them, and re-layouts  5.81 us
  transfers between devices with their start and end apart: 8, of which 3 were waited for; matrix products, arithmetic and copies ran while one was open for 0% of the time, Pallas kernels for 10%

profile of v4, /device:TPU:1, one launch (start us, length us, event | category | flops | bytes accessed | tf_op | source)
XLA Modules:
  0.0 117.1 jit_solution(15129702359983300417)
XLA Ops:
  0.6 12.2 %synthesis.1 = bf16[32,64,384]{2,1,0:T(8,128)(2,1)} custom-call(f32[2,16,2,3,4,512]{5,4,3,2,1,0:T(4,128)} %bitcast.29, bf16[16,2,512,512]{3,2,1,0:T(8,128)(2,1)} %bitcast.37), custom_call_target="tpu_custom_call" | custom-call | flops 402653184 | bytes 20971520 | tf_op jit(solution)/shard_map/synthesis/pallas_call | solution.py:115
  12.9 8.9 %all-to-all-start = ((bf16[32,64,384]{2,1,0:T(8,128)(2,1)}), bf16[32,64,384]{2,1,0:T(8,128)(2,1)}, u32[]{:S(2)}, u32[]{:S(2)}) async-start(bf16[32,64,384]{2,1,0:T(8,128)(2,1)} %synthesis.1), calls=%async_computation | async-start | bytes 3145728 | tf_op jit(solution)/shard_map/all_to_all | solution.py:572
  21.9 3.0 %prepare.1 = (bf16[192,512]{1,0:T(8,128)(2,1)S(1)}, bf16[192,512]{1,0:T(8,128)(2,1)}, bf16[192,512]{1,0:T(8,128)(2,1)}, bf16[192,512]{1,0:T(8,128)(2,1)}, f32[2,2,8,2,3,4,512]{6,5,4,3,2,1,0:T(4,128)S(1)}) custom-call(s32[1]{0:T(128)} %bitcast.id_ref, f32[4,4]{1,0:T(4,128)S(1)} %copy-done.9, f32[2,2,8,2,3,4,512]{6,5,4,3,2,1,0:T(4,128)S(1)} %bitcast.32, ...), custom_call_target="tpu_custom_call" | custom-call | flops 3145728 | bytes 6291456 | tf_op jit(solution)/shard_map/prepare/pallas_call | solution.py:185
  24.9 1.2 copy-done.2
  26.0 0.7 copy-done.6
  26.7 1.6 %collective-permute-start = (bf16[192,512]{1,0:T(8,128)(2,1)}, bf16[192,512]{1,0:T(8,128)(2,1)S(1)}, u32[]{:S(2)}, u32[]{:S(2)}) collective-permute-start(bf16[192,512]{1,0:T(8,128)(2,1)} %get-tuple-element.32), channel_id=1, source_target_pairs={{0,32},{32,64},{64,96},{96,0},{1,33},{33,65},{65,97},{97,1},{2,34}... | collective-permute-start | bytes 589832 | tf_op jit(solution)/shard_map/ppermute | solution.py:576
  28.3 3.3 %collective-permute-start.1 = (bf16[192,512]{1,0:T(8,128)(2,1)}, bf16[192,512]{1,0:T(8,128)(2,1)S(1)}, u32[]{:S(2)}, u32[]{:S(2)}) collective-permute-start(bf16[192,512]{1,0:T(8,128)(2,1)} %get-tuple-element.33), channel_id=1, source_target_pairs={{0,64},{32,96},{64,0},{96,32},{1,65},{33,97},{65,1},{97,33},{2,66}... | collective-permute-start | bytes 589832 | tf_op jit(solution)/shard_map/ppermute | solution.py:576
  31.6 0.7 collective-permute-start.2
  32.3 0.1 dynamic_slice.7
  32.4 0.1 constant_dynamic-slice_fusion
  32.5 0.1 broadcast_select_fusion
  32.6 0.1 reshape.116
  32.7 1.0 copy-done.5
  33.7 5.9 %tables.1 = (bf16[8,2,528,512]{3,2,1,0:T(8,128)(2,1)}, bf16[4,2,512,512]{3,2,1,0:T(8,128)(2,1)S(1)}) custom-call(f32[2,2,33,512]{3,2,1,0:T(8,128)S(1)} %copy-done.5, f32[2,2,16,512]{3,2,1,0:T(8,128)S(1)} %copy-done.8, f32[2,1,512]{2,1,0:T(1,128)S(1)} %copy-done.10), custom_call_target="tpu_custom_call" | custom-call | flops 4325376 | bytes 15728640 | tf_op jit(solution)/shard_map/tables/pallas_call | solution.py:269
  39.6 2.0 %copy-done.11 = bf16[4,2,512,512]{3,2,1,0:T(8,128)(2,1)} copy-done((bf16[4,2,512,512]{3,2,1,0:T(8,128)(2,1)}, bf16[4,2,512,512]{3,2,1,0:T(8,128)(2,1)S(1)}, u32[]{:S(2)}) %copy-start.11) | copy-done | bytes 4194328
  41.6 0.1 dynamic-slice_bitcast_fusion
  41.7 0.1 compare_select_fusion
  41.8 0.1 maximum_bitcast_fusion
  41.9 2.6 %all-to-all-done.got_ref = bf16[32,64,384]{2,1,0:T(8,128)(2,1)} async-done(((bf16[32,64,384]{2,1,0:T(8,128)(2,1)}), bf16[32,64,384]{2,1,0:T(8,128)(2,1)}, u32[]{:S(2)}, u32[]{:S(2)}) %all-to-all-start) | async-done | bytes 1572896 | tf_op jit(solution)/shard_map/all_to_all | solution.py:572
  44.5 13.9 %grid.1 = bf16[32,4,16,384]{3,2,1,0:T(8,128)(2,1)S(1)} custom-call(bf16[32,64,384]{2,1,0:T(8,128)(2,1)} %all-to-all-done.got_ref, bf16[8,2,528,512]{3,2,1,0:T(8,128)(2,1)} %get-tuple-element.28.tab_hbm, bf16[4,2,512,512]{3,2,1,0:T(8,128)(2,1)} %copy-done.11, f32[3,128]{1,0:T(4,128)S(1)} %pad_maximum_fusion.rows_ref), custom_call_target="tpu_custom_call" | custom-call | flops 5813305344 | bytes 17825792 | tf_op jit(solution)/shard_map/grid/pallas_call | solution.py:371
  58.4 30.1 %all_to_all.15.y_ref = bf16[128,16,384]{2,1,0:T(8,128)(2,1)} all-to-all(bf16[128,16,384]{2,1,0:T(8,128)(2,1)S(1)} %bitcast.33), channel_id=1, replica_groups=mesh['node'=4,'band_0'=4,'band_1'=4,'band_2'=2] {'band_2','band_1','band..., dimensions={0} | all-to-all | bytes 3145728 | tf_op jit(solution)/shard_map/all_to_all | solution.py:572
  88.5 6.8 %analysis.1 = (bf16[192,512]{1,0:T(8,128)(2,1)}, bf16[192,512]{1,0:T(8,128)(2,1)}, bf16[192,512]{1,0:T(8,128)(2,1)}, bf16[192,512]{1,0:T(8,128)(2,1)}, f32[128,1,128]{2,1,0:T(1,128)}) custom-call(s32[1]{0:T(128)} %bitcast.id_ref, f32[4,4]{1,0:T(4,128)} %quad_ref.2, bf16[128,16,384]{2,1,0:T(8,128)(2,1)} %all_to_all.15.y_ref, ...), custom_call_target="tpu_custom_call" | custom-call | flops 402653184 | bytes 10485760 | tf_op jit(solution)/shard_map/analysis/pallas_call | solution.py:491
  95.3 2.0 %collective-permute-start.3 = (bf16[192,512]{1,0:T(8,128)(2,1)}, bf16[192,512]{1,0:T(8,128)(2,1)S(1)}, u32[]{:S(2)}, u32[]{:S(2)}) collective-permute-start(bf16[192,512]{1,0:T(8,128)(2,1)} %get-tuple-element.42), channel_id=1, source_target_pairs={{0,96},{32,0},{64,32},{96,64},{1,97},{33,1},{65,33},{97,65},{2,98}... | collective-permute-start | bytes 589832 | tf_op jit(solution)/shard_map/ppermute | solution.py:576
  97.2 0.9 collective-permute-start.4
  98.2 0.3 collective-permute-start.5
  98.5 8.5 %all-to-all-start.2 = ((f32[128,1,128]{2,1,0:T(1,128)}), f32[128,1,128]{2,1,0:T(1,128)S(1)}, u32[]{:S(2)}, u32[]{:S(2)}) async-start(f32[128,1,128]{2,1,0:T(1,128)} %get-tuple-element.40), calls=%async_computation.2 | async-start | bytes 131072 | tf_op jit(solution)/shard_map/all_to_all | solution.py:572
  107.0 3.0 %collective-permute-done.5.mixed3_ref = bf16[192,512]{1,0:T(8,128)(2,1)S(1)} collective-permute-done((bf16[192,512]{1,0:T(8,128)(2,1)}, bf16[192,512]{1,0:T(8,128)(2,1)S(1)}, u32[]{:S(2)}, u32[]{:S(2)}) %collective-permute-start.5) | collective-permute-done | bytes 196640 | tf_op jit(solution)/shard_map/ppermute | solution.py:576
  110.0 0.9 copy-done.7
  110.9 2.4 %update.1 = f32[2,2,8,2,3,4,512]{6,5,4,3,2,1,0:T(4,128)} custom-call(s32[1]{0:T(128)} %bitcast.id_ref, bf16[192,512]{1,0:T(8,128)(2,1)S(1)} %copy-done.7, bf16[192,512]{1,0:T(8,128)(2,1)S(1)} %collective-permute-done.3.mixed1_ref, bf16[192,512]{1,0:T(8,128)(2,1)S(1)} %collective-permute-done.4.mixed2_ref, ...), custom_call_target="tpu_custom_call" | custom-call | flops 1572864 | bytes 5242880 | tf_op jit(solution)/shard_map/update/pallas_call | solution.py:553
  113.3 3.0 %all-to-all-done.2 = f32[128,1,128]{2,1,0:T(1,128)S(1)} async-done(((f32[128,1,128]{2,1,0:T(1,128)}), f32[128,1,128]{2,1,0:T(1,128)S(1)}, u32[]{:S(2)}, u32[]{:S(2)}) %all-to-all-start.2) | async-done | bytes 65568 | tf_op jit(solution)/shard_map/all_to_all | solution.py:572
  116.3 0.2 reduce_sum.9
  116.5 0.6 fusion
  (36 shorter events, 0.1 us)
Async XLA Ops:
  0.6 21.2 %copy-start.4 = (f32[32,3,512]{2,0,1:T(8,128)S(1)}, f32[32,3,512]{2,0,1:T(8,128)}, u32[]{:S(2)}) copy-start(f32[32,3,512]{2,0,1:T(8,128)} %param.15) | copy-start | bytes 589828
  12.8 9.0 %copy-start = (f32[1,2,32,4,3,512]{5,3,4,2,1,0:T(4,128)S(1)}, f32[1,2,32,4,3,512]{5,3,4,2,1,0:T(4,128)}, u32[]{:S(2)}) copy-start(f32[1,2,32,4,3,512]{5,3,4,2,1,0:T(4,128)} %param.11) | copy-start | bytes 4718596
  12.9 9.0 %copy-start.1 = (f32[2,32,4,3,512]{4,2,3,1,0:T(4,128)S(1)}, f32[2,32,4,3,512]{4,2,3,1,0:T(4,128)}, u32[]{:S(2)}) copy-start(f32[2,32,4,3,512]{4,2,3,1,0:T(4,128)} %param.10) | copy-start | bytes 4718596
  12.9 9.0 %copy-start.9 = (f32[4,4]{1,0:T(4,128)S(1)}, f32[4,4]{1,0:T(4,128)}, u32[]{:S(2)}) copy-start(f32[4,4]{1,0:T(4,128)} %quad_ref.2) | copy-start | bytes 196
  12.9 31.6 %all-to-all-start = ((bf16[32,64,384]{2,1,0:T(8,128)(2,1)}), bf16[32,64,384]{2,1,0:T(8,128)(2,1)}, u32[]{:S(2)}, u32[]{:S(2)}) async-start(bf16[32,64,384]{2,1,0:T(8,128)(2,1)} %synthesis.1), calls=%async_computation | async-start | bytes 3145728 | tf_op jit(solution)/shard_map/all_to_all | solution.py:572
  21.9 10.5 %copy-start.16 = (f32[512]{0:T(512)S(1)}, f32[512]{0:T(512)}, u32[]{:S(2)}) copy-start(f32[512]{0:T(512)} %param.13) | copy-start | bytes 6148
  21.9 10.6 %copy-start.15 = (f32[2,512]{1,0:T(2,128)S(1)}, f32[2,512]{1,0:T(2,128)}, u32[]{:S(2)}) copy-start(f32[2,512]{1,0:T(2,128)} %param.14) | copy-start | bytes 12292
  21.9 10.8 %copy-start.8 = (f32[2,2,16,512]{3,2,1,0:T(8,128)S(1)}, f32[2,2,16,512]{3,2,1,0:T(8,128)}, u32[]{:S(2)}) copy-start(f32[2,2,16,512]{3,2,1,0:T(8,128)} %constant.62.clone.row2_ref) | copy-start | bytes 393220
  21.9 10.8 %copy-start.10 = (f32[2,1,512]{2,1,0:T(1,128)S(1)}, f32[2,1,512]{2,1,0:T(1,128)}, u32[]{:S(2)}) copy-start(f32[2,1,512]{2,1,0:T(1,128)} %constant.63.clone.wave_ref) | copy-start | bytes 12292
  24.9 1.2 copy-start.2
  26.0 0.7 copy-start.6
  26.7 15.2 %collective-permute-start = (bf16[192,512]{1,0:T(8,128)(2,1)}, bf16[192,512]{1,0:T(8,128)(2,1)S(1)}, u32[]{:S(2)}, u32[]{:S(2)}) collective-permute-start(bf16[192,512]{1,0:T(8,128)(2,1)} %get-tuple-element.32), channel_id=1, source_target_pairs={{0,32},{32,64},{64,96},{96,0},{1,33},{33,65},{65,97},{97,1},{2,34}... | collective-permute-start | bytes 589832 | tf_op jit(solution)/shard_map/ppermute | solution.py:576
  28.3 13.6 %collective-permute-start.1 = (bf16[192,512]{1,0:T(8,128)(2,1)}, bf16[192,512]{1,0:T(8,128)(2,1)S(1)}, u32[]{:S(2)}, u32[]{:S(2)}) collective-permute-start(bf16[192,512]{1,0:T(8,128)(2,1)} %get-tuple-element.33), channel_id=1, source_target_pairs={{0,64},{32,96},{64,0},{96,32},{1,65},{33,97},{65,1},{97,33},{2,66}... | collective-permute-start | bytes 589832 | tf_op jit(solution)/shard_map/ppermute | solution.py:576
  31.6 10.3 %collective-permute-start.2 = (bf16[192,512]{1,0:T(8,128)(2,1)}, bf16[192,512]{1,0:T(8,128)(2,1)S(1)}, u32[]{:S(2)}, u32[]{:S(2)}) collective-permute-start(bf16[192,512]{1,0:T(8,128)(2,1)} %get-tuple-element.34), channel_id=1, source_target_pairs={{0,96},{32,0},{64,32},{96,64},{1,97},{33,1},{65,33},{97,65},{2,98}... | collective-permute-start | bytes 589832 | tf_op jit(solution)/shard_map/ppermute | solution.py:576
  32.7 1.0 copy-start.5
  39.6 2.0 %copy-start.11 = (bf16[4,2,512,512]{3,2,1,0:T(8,128)(2,1)}, bf16[4,2,512,512]{3,2,1,0:T(8,128)(2,1)S(1)}, u32[]{:S(2)}) copy-start(bf16[4,2,512,512]{3,2,1,0:T(8,128)(2,1)S(1)} %get-tuple-element.29.back_hbm) | copy-start | bytes 12582916
  41.9 16.5 %copy-start.12 = (bf16[192,512]{1,0:T(8,128)(2,1)}, bf16[192,512]{1,0:T(8,128)(2,1)S(1)}, u32[]{:S(2)}) copy-start(bf16[192,512]{1,0:T(8,128)(2,1)S(1)} %collective-permute-done) | copy-start | bytes 589828
  41.9 16.5 %copy-start.13 = (bf16[192,512]{1,0:T(8,128)(2,1)}, bf16[192,512]{1,0:T(8,128)(2,1)S(1)}, u32[]{:S(2)}) copy-start(bf16[192,512]{1,0:T(8,128)(2,1)S(1)} %collective-permute-done.1) | copy-start | bytes 589828
  41.9 16.5 %copy-start.14 = (bf16[192,512]{1,0:T(8,128)(2,1)}, bf16[192,512]{1,0:T(8,128)(2,1)S(1)}, u32[]{:S(2)}) copy-start(bf16[192,512]{1,0:T(8,128)(2,1)S(1)} %collective-permute-done.2) | copy-start | bytes 589828
  88.5 21.5 %copy-start.3 = (f32[2,2,8,2,3,4,512]{6,5,4,3,2,1,0:T(4,128)S(1)}, f32[2,2,8,2,3,4,512]{6,5,4,3,2,1,0:T(4,128)}, u32[]{:S(2)}) copy-start(f32[2,2,8,2,3,4,512]{6,5,4,3,2,1,0:T(4,128)} %copy-done.2) | copy-start | bytes 4718596
  95.3 11.7 %collective-permute-start.3 = (bf16[192,512]{1,0:T(8,128)(2,1)}, bf16[192,512]{1,0:T(8,128)(2,1)S(1)}, u32[]{:S(2)}, u32[]{:S(2)}) collective-permute-start(bf16[192,512]{1,0:T(8,128)(2,1)} %get-tuple-element.42), channel_id=1, source_target_pairs={{0,96},{32,0},{64,32},{96,64},{1,97},{33,1},{65,33},{97,65},{2,98}... | collective-permute-start | bytes 589832 | tf_op jit(solution)/shard_map/ppermute | solution.py:576
  97.2 9.8 %collective-permute-start.4 = (bf16[192,512]{1,0:T(8,128)(2,1)}, bf16[192,512]{1,0:T(8,128)(2,1)S(1)}, u32[]{:S(2)}, u32[]{:S(2)}) collective-permute-start(bf16[192,512]{1,0:T(8,128)(2,1)} %get-tuple-element.43), channel_id=1, source_target_pairs={{0,64},{32,96},{64,0},{96,32},{1,65},{33,97},{65,1},{97,33},{2,66}... | collective-permute-start | bytes 589832 | tf_op jit(solution)/shard_map/ppermute | solution.py:576
  98.2 11.8 %collective-permute-start.5 = (bf16[192,512]{1,0:T(8,128)(2,1)}, bf16[192,512]{1,0:T(8,128)(2,1)S(1)}, u32[]{:S(2)}, u32[]{:S(2)}) collective-permute-start(bf16[192,512]{1,0:T(8,128)(2,1)} %get-tuple-element.44), channel_id=1, source_target_pairs={{0,32},{32,64},{64,96},{96,0},{1,33},{33,65},{65,97},{97,1},{2,34}... | collective-permute-start | bytes 589832 | tf_op jit(solution)/shard_map/ppermute | solution.py:576
  98.5 17.8 %all-to-all-start.2 = ((f32[128,1,128]{2,1,0:T(1,128)}), f32[128,1,128]{2,1,0:T(1,128)S(1)}, u32[]{:S(2)}, u32[]{:S(2)}) async-start(f32[128,1,128]{2,1,0:T(1,128)} %get-tuple-element.40), calls=%async_computation.2 | async-start | bytes 131072 | tf_op jit(solution)/shard_map/all_to_all | solution.py:572
  110.0 0.9 copy-start.7

commit v5 on v4

--- a/solution.py
+++ b/solution.py
@@ -198,7 +198,7 @@
         ),
         out_shape=[jax.ShapeDtypeStruct((8 * COLS, DEGREES), jnp.bfloat16)] * 4
         + [jax.ShapeDtypeStruct(it7.shape, jnp.float32)],
-        compiler_params=pltpu.CompilerParams(vmem_limit_bytes=32 * MIB),
+        compiler_params=pltpu.CompilerParams(vmem_limit_bytes=60 * MIB),
         cost_estimate=pl.CostEstimate(
             flops=8 * 32 * COLS * DEGREES, bytes_accessed=6 * MIB, transcendentals=0
         ),
@@ -214,35 +214,34 @@
 def table_kernel(row1_ref, row2_ref, wave_ref, tab_ref, back_ref, keep_ref):
     first = lax.broadcasted_iota(jnp.int32, (1, 128), 1) == 0
     halve = jnp.where(first, 0.5, 1.0)
-    for par in range(2):
-        wave = wave_ref[par]
-
-        def rows(j, _, par=par, wave=wave):
-            lead_c = row1_ref[par, 0, pl.ds(j, 1), :]
-            lead_s = row1_ref[par, 1, pl.ds(j, 1), :]
-            cosine = lead_c * row2_ref[par, 0] - lead_s * row2_ref[par, 1]
-            sine = lead_s * row2_ref[par, 0] + lead_c * row2_ref[par, 1]
-            at = pl.ds(pl.multiple_of(16 * j, 16), 16)
-            keep_ref[0, at, :] = cosine
-            keep_ref[1, at, :] = sine
-            for t, value in enumerate((cosine, sine, -wave * cosine, wave * sine)):
-                high, low = split(value)
-                tab_ref[4 * par + t, 0, at, :] = high
-                tab_ref[4 * par + t, 1, at, :] = low
-            return 0
-
-        lax.fori_loop(0, ROWS // 16, rows, 0)
-        for t in range(2):
-            for block in range(4):
-                cut = slice(128 * block, 128 * (block + 1))
-                value = jnp.transpose(keep_ref[t, cut, :])
-                if t == 1:
-                    value = -value
-                if block == 0:
-                    value = value * halve
-                high, low = split(value)
-                back_ref[2 * par + t, 0, :, cut] = high
-                back_ref[2 * par + t, 1, :, cut] = low
+    wave = wave_ref[...]
+
+    def rows(j, _):
+        lead_c = row1_ref[0, pl.ds(j, 1), :]
+        lead_s = row1_ref[1, pl.ds(j, 1), :]
+        cosine = lead_c * row2_ref[0] - lead_s * row2_ref[1]
+        sine = lead_s * row2_ref[0] + lead_c * row2_ref[1]
+        at = pl.ds(pl.multiple_of(16 * j, 16), 16)
+        keep_ref[0, at, :] = cosine
+        keep_ref[1, at, :] = sine
+        for t, value in enumerate((cosine, sine, -wave * cosine, wave * sine)):
+            high, low = split(value)
+            tab_ref[t, 0, at, :] = high
+            tab_ref[t, 1, at, :] = low
+        return 0
+
+    lax.fori_loop(0, ROWS // 16, rows, 0)
+    for t in range(2):
+        for block in range(4):
+            cut = slice(128 * block, 128 * (block + 1))
+            value = jnp.transpose(keep_ref[t, cut, :])
+            if t == 1:
+                value = -value
+            if block == 0:
+                value = value * halve
+            high, low = split(value)
+            back_ref[t, 0, :, cut] = high
+            back_ref[t, 1, :, cut] = low
 
 
 def small_tables():
@@ -266,14 +265,23 @@
 
 
 def tables(parts):
+    spec = pl.BlockSpec
     return pl.pallas_call(
         table_kernel,
+        grid=(2,),
+        in_specs=[
+            spec((None,) + x.shape[1:], lambda i, n=x.ndim: (i,) + (0,) * (n - 1)) for x in parts
+        ],
+        out_specs=(
+            spec((4, 2, ROWS, HALF), lambda i: (i, 0, 0, 0)),
+            spec((2, 2, HALF, QUARTER), lambda i: (i, 0, 0, 0)),
+        ),
         out_shape=(
             jax.ShapeDtypeStruct((8, 2, ROWS, HALF), jnp.bfloat16),
             jax.ShapeDtypeStruct((4, 2, HALF, QUARTER), jnp.bfloat16),
         ),
         scratch_shapes=[pltpu.VMEM((2, ROWS, HALF), jnp.float32)],
-        compiler_params=pltpu.CompilerParams(vmem_limit_bytes=48 * MIB),
+        compiler_params=pltpu.CompilerParams(vmem_limit_bytes=60 * MIB),
         cost_estimate=pl.CostEstimate(
             flops=16 * ROWS * HALF, bytes_accessed=15 * MIB, transcendentals=0
         ),

time: 117 us -> 116 us (level)
  local copies, waits for them, and re-layouts: 6.14 us -> 1.29 us
  waiting for transfers between devices: 8.6 us -> 11.1 us
    unnamed x34 -> x14, local copies, waits for them, and re-layouts: 5.81 us -> 0.96 us
    pallas_call x1, Pallas kernels: 2.96 us -> 4.8 us  [prepare(): pl.pallas_call(prepare_kernel, grid_spec=pltpu.PrefetchScalarGridSpec(num...]
    pallas_call x1, Pallas kernels: 13.9 us -> 12.5 us  [grid_stage(): pl.pallas_call(grid_kernel, in_specs=[pl.BlockSpec(memory_space=pltpu.VME...]
    ppermute x6, waiting for transfers between devices: 3 us -> 4.34 us  [shift(): return lax.ppermute(x, axis, [(i, (i + by) % 4) for i in range(4)])]
  transfers between devices with their start and end apart: 8 -> 8, of which waited for: 3 -> 4; matrix products, arithmetic and copies ran while one was open for 0% -> 0% of each run, Pallas kernels for 10% -> 12%
where the time goes in v5:
time: 116 us; the launch traced here: 115 us
  Pallas kernels  45.1 us (39%)
  blocking collectives  30.1 us (26%)
  starting transfers between devices  25.9 us (22%)
  waiting for transfers between devices  11.1 us (10%)
  local copies, waits for them, and re-layouts  1.29 us (1%)
    all_to_all x1, blocking collectives, exchange(): return lax.all_to_all(x, axes, split_axis=0, concat_axis=0, tiled=True)  30.1 us
    all_to_all x2, starting transfers between devices, exchange(): return lax.all_to_all(x, axes, split_axis=0, concat_axis=0, tiled=True)  17.1 us
    pallas_call x1, Pallas kernels, grid_stage(): pl.pallas_call(grid_kernel, in_specs=[pl.BlockSpec(memory_space=pltpu.VME...  12.5 us
    pallas_call x1, Pallas kernels, synthesis(): pl.pallas_call(synthesis_kernel, in_specs=[pl.BlockSpec(memory_space=pl.A...  12.2 us
    ppermute x6, starting transfers between devices, shift(): return lax.ppermute(x, axis, [(i, (i + by) % 4) for i in range(4)])  8.83 us
    pallas_call x1, Pallas kernels, analysis(): pl.pallas_call(analysis_kernel, grid_spec=pltpu.PrefetchScalarGridSpec(nu...  6.77 us
    all_to_all x2, waiting for transfers between devices, exchange(): return lax.all_to_all(x, axes, split_axis=0, concat_axis=0, tiled=True)  6.71 us
    pallas_call x1, Pallas kernels, tables(): pl.pallas_call(table_kernel, grid=(2,), in_specs=[spec((None,) + x.shape[...  6.56 us
  transfers between devices with their start and end apart: 8, of which 4 were waited for; matrix products, arithmetic and copies ran while one was open for 0% of the time, Pallas kernels for 12%

profile of v5, /device:TPU:1, one launch (start us, length us, event | category | flops | bytes accessed | tf_op | source)
XLA Modules:
  0.0 115.2 jit_solution(6478646754732170290)
XLA Ops:
  0.6 12.2 %synthesis.1 = bf16[32,64,384]{2,1,0:T(8,128)(2,1)} custom-call(f32[2,16,2,3,4,512]{5,4,3,2,1,0:T(4,128)} %bitcast.32, bf16[16,2,512,512]{3,2,1,0:T(8,128)(2,1)} %bitcast.30), custom_call_target="tpu_custom_call" | custom-call | flops 402653184 | bytes 20971520 | tf_op jit(solution)/shard_map/synthesis/pallas_call | solution.py:115
  12.8 8.6 %all-to-all-start = ((bf16[32,64,384]{2,1,0:T(8,128)(2,1)}), bf16[32,64,384]{2,1,0:T(8,128)(2,1)S(1)}, u32[]{:S(2)}, u32[]{:S(2)}) async-start(bf16[32,64,384]{2,1,0:T(8,128)(2,1)} %synthesis.1), calls=%async_computation | async-start | bytes 3145728 | tf_op jit(solution)/shard_map/all_to_all | solution.py:580
  21.4 0.0 copy-start.6
  21.4 0.0 copy-start.5
  21.4 4.8 %prepare.1 = (bf16[192,512]{1,0:T(8,128)(2,1)}, bf16[192,512]{1,0:T(8,128)(2,1)}, bf16[192,512]{1,0:T(8,128)(2,1)}, bf16[192,512]{1,0:T(8,128)(2,1)}, f32[2,2,8,2,3,4,512]{6,5,4,3,2,1,0:T(4,128)}) custom-call(s32[1]{0:T(128)} %bitcast.id_ref, f32[4,4]{1,0:T(4,128)} %quad_ref.2, f32[2,2,8,2,3,4,512]{6,5,4,3,2,1,0:T(4,128)} %bitcast.34, ...), custom_call_target="tpu_custom_call" | custom-call | flops 3145728 | bytes 6291456 | tf_op jit(solution)/shard_map/prepare/pallas_call | solution.py:185
  26.2 1.6 %collective-permute-start = (bf16[192,512]{1,0:T(8,128)(2,1)}, bf16[192,512]{1,0:T(8,128)(2,1)S(1)}, u32[]{:S(2)}, u32[]{:S(2)}) collective-permute-start(bf16[192,512]{1,0:T(8,128)(2,1)} %get-tuple-element.32), channel_id=1, source_target_pairs={{0,32},{32,64},{64,96},{96,0},{1,33},{33,65},{65,97},{97,1},{2,34}... | collective-permute-start | bytes 589832 | tf_op jit(solution)/shard_map/ppermute | solution.py:584
  27.8 3.3 %collective-permute-start.1 = (bf16[192,512]{1,0:T(8,128)(2,1)}, bf16[192,512]{1,0:T(8,128)(2,1)S(1)}, u32[]{:S(2)}, u32[]{:S(2)}) collective-permute-start(bf16[192,512]{1,0:T(8,128)(2,1)} %get-tuple-element.33), channel_id=1, source_target_pairs={{0,64},{32,96},{64,0},{96,32},{1,65},{33,97},{65,1},{97,33},{2,66}... | collective-permute-start | bytes 589832 | tf_op jit(solution)/shard_map/ppermute | solution.py:584
  31.1 0.7 collective-permute-start.2
  31.9 0.1 dynamic_slice.7
  31.9 0.1 constant_dynamic-slice_fusion
  32.0 0.1 broadcast_select_fusion
  32.1 0.1 reshape.116
  32.2 6.6 %tables.1 = (bf16[8,2,528,512]{3,2,1,0:T(8,128)(2,1)}, bf16[4,2,512,512]{3,2,1,0:T(8,128)(2,1)}) custom-call(f32[2,2,33,512]{3,2,1,0:T(8,128)} %constant.61.clone.row1_ref, f32[2,2,16,512]{3,2,1,0:T(8,128)} %constant.62.clone.row2_ref, f32[2,1,512]{2,1,0:T(1,128)} %constant.63.clone.wave_ref), custom_call_target="tpu_custom_call" | custom-call | flops 4325376 | bytes 15728640 | tf_op jit(solution)/shard_map/tables/pallas_call | solution.py:269
  38.8 0.1 dynamic-slice_bitcast_fusion
  38.8 0.1 compare_select_fusion
  38.9 0.1 maximum_bitcast_fusion
  39.0 0.0 collective-permute-done
  39.0 1.3 %collective-permute-done.1 = bf16[192,512]{1,0:T(8,128)(2,1)S(1)} collective-permute-done((bf16[192,512]{1,0:T(8,128)(2,1)}, bf16[192,512]{1,0:T(8,128)(2,1)S(1)}, u32[]{:S(2)}, u32[]{:S(2)}) %collective-permute-start.1) | collective-permute-done | bytes 196640 | tf_op jit(solution)/shard_map/ppermute | solution.py:584
  40.4 3.7 %all-to-all-done.got_ref = bf16[32,64,384]{2,1,0:T(8,128)(2,1)S(1)} async-done(((bf16[32,64,384]{2,1,0:T(8,128)(2,1)}), bf16[32,64,384]{2,1,0:T(8,128)(2,1)S(1)}, u32[]{:S(2)}, u32[]{:S(2)}) %all-to-all-start) | async-done | bytes 1572896 | tf_op jit(solution)/shard_map/all_to_all | solution.py:580
  44.0 12.5 %grid.1 = bf16[32,4,16,384]{3,2,1,0:T(8,128)(2,1)S(1)} custom-call(bf16[32,64,384]{2,1,0:T(8,128)(2,1)S(1)} %all-to-all-done.got_ref, bf16[8,2,528,512]{3,2,1,0:T(8,128)(2,1)} %get-tuple-element.28.tab_hbm, bf16[4,2,512,512]{3,2,1,0:T(8,128)(2,1)} %get-tuple-element.29.back_hbm, f32[3,128]{1,0:T(4,128)S(1)} %pad_maximum_fusion.rows_ref), custom_call_target="tpu_custom_call" | custom-call | flops 5813305344 | bytes 17825792 | tf_op jit(solution)/shard_map/grid/pallas_call | solution.py:379
  56.6 30.1 %all_to_all.15.y_ref = bf16[128,16,384]{2,1,0:T(8,128)(2,1)} all-to-all(bf16[128,16,384]{2,1,0:T(8,128)(2,1)S(1)} %bitcast.29), channel_id=1, replica_groups=mesh['node'=4,'band_0'=4,'band_1'=4,'band_2'=2] {'band_2','band_1','band..., dimensions={0} | all-to-all | bytes 3145728 | tf_op jit(solution)/shard_map/all_to_all | solution.py:580
  86.6 6.8 %analysis.1 = (bf16[192,512]{1,0:T(8,128)(2,1)}, bf16[192,512]{1,0:T(8,128)(2,1)}, bf16[192,512]{1,0:T(8,128)(2,1)}, bf16[192,512]{1,0:T(8,128)(2,1)}, f32[128,1,128]{2,1,0:T(1,128)}) custom-call(s32[1]{0:T(128)} %bitcast.id_ref, f32[4,4]{1,0:T(4,128)} %quad_ref.2, bf16[128,16,384]{2,1,0:T(8,128)(2,1)} %all_to_all.15.y_ref, ...), custom_call_target="tpu_custom_call" | custom-call | flops 402653184 | bytes 10485760 | tf_op jit(solution)/shard_map/analysis/pallas_call | solution.py:499
  93.4 2.0 %collective-permute-start.3 = (bf16[192,512]{1,0:T(8,128)(2,1)}, bf16[192,512]{1,0:T(8,128)(2,1)S(1)}, u32[]{:S(2)}, u32[]{:S(2)}) collective-permute-start(bf16[192,512]{1,0:T(8,128)(2,1)} %get-tuple-element.42), channel_id=1, source_target_pairs={{0,96},{32,0},{64,32},{96,64},{1,97},{33,1},{65,33},{97,65},{2,98}... | collective-permute-start | bytes 589832 | tf_op jit(solution)/shard_map/ppermute | solution.py:584
  95.4 0.9 collective-permute-start.4
  96.3 0.3 collective-permute-start.5
  96.6 8.5 %all-to-all-start.2 = ((f32[128,1,128]{2,1,0:T(1,128)}), f32[128,1,128]{2,1,0:T(1,128)S(1)}, u32[]{:S(2)}, u32[]{:S(2)}) async-start(f32[128,1,128]{2,1,0:T(1,128)} %get-tuple-element.40), calls=%async_computation.2 | async-start | bytes 131072 | tf_op jit(solution)/shard_map/all_to_all | solution.py:580
  105.1 3.0 %collective-permute-done.5.mixed3_ref = bf16[192,512]{1,0:T(8,128)(2,1)S(1)} collective-permute-done((bf16[192,512]{1,0:T(8,128)(2,1)}, bf16[192,512]{1,0:T(8,128)(2,1)S(1)}, u32[]{:S(2)}, u32[]{:S(2)}) %collective-permute-start.5) | collective-permute-done | bytes 196640 | tf_op jit(solution)/shard_map/ppermute | solution.py:584
  108.1 0.9 copy-done.1
  109.1 2.4 %update.1 = f32[2,2,8,2,3,4,512]{6,5,4,3,2,1,0:T(4,128)} custom-call(s32[1]{0:T(128)} %bitcast.id_ref, bf16[192,512]{1,0:T(8,128)(2,1)S(1)} %copy-done.1, bf16[192,512]{1,0:T(8,128)(2,1)S(1)} %collective-permute-done.3.mixed1_ref, bf16[192,512]{1,0:T(8,128)(2,1)S(1)} %collective-permute-done.4.mixed2_ref, ...), custom_call_target="tpu_custom_call" | custom-call | flops 1572864 | bytes 5242880 | tf_op jit(solution)/shard_map/update/pallas_call | solution.py:561
  111.4 3.0 %all-to-all-done.2 = f32[128,1,128]{2,1,0:T(1,128)S(1)} async-done(((f32[128,1,128]{2,1,0:T(1,128)}), f32[128,1,128]{2,1,0:T(1,128)S(1)}, u32[]{:S(2)}, u32[]{:S(2)}) %all-to-all-start.2) | async-done | bytes 65568 | tf_op jit(solution)/shard_map/all_to_all | solution.py:580
  114.4 0.2 reduce_sum.9
  114.6 0.6 fusion
  (16 shorter events, 0.1 us)
Async XLA Ops:
  12.8 31.3 %all-to-all-start = ((bf16[32,64,384]{2,1,0:T(8,128)(2,1)}), bf16[32,64,384]{2,1,0:T(8,128)(2,1)S(1)}, u32[]{:S(2)}, u32[]{:S(2)}) async-start(bf16[32,64,384]{2,1,0:T(8,128)(2,1)} %synthesis.1), calls=%async_computation | async-start | bytes 3145728 | tf_op jit(solution)/shard_map/all_to_all | solution.py:580
  21.4 10.4 %copy-start.6 = (f32[512]{0:T(512)S(1)}, f32[512]{0:T(512)}, u32[]{:S(2)}) copy-start(f32[512]{0:T(512)} %param.13) | copy-start | bytes 6148
  21.4 10.5 %copy-start.5 = (f32[2,512]{1,0:T(2,128)S(1)}, f32[2,512]{1,0:T(2,128)}, u32[]{:S(2)}) copy-start(f32[2,512]{1,0:T(2,128)} %param.14) | copy-start | bytes 12292
  26.2 12.8 %collective-permute-start = (bf16[192,512]{1,0:T(8,128)(2,1)}, bf16[192,512]{1,0:T(8,128)(2,1)S(1)}, u32[]{:S(2)}, u32[]{:S(2)}) collective-permute-start(bf16[192,512]{1,0:T(8,128)(2,1)} %get-tuple-element.32), channel_id=1, source_target_pairs={{0,32},{32,64},{64,96},{96,0},{1,33},{33,65},{65,97},{97,1},{2,34}... | collective-permute-start | bytes 589832 | tf_op jit(solution)/shard_map/ppermute | solution.py:584
  27.8 12.5 %collective-permute-start.1 = (bf16[192,512]{1,0:T(8,128)(2,1)}, bf16[192,512]{1,0:T(8,128)(2,1)S(1)}, u32[]{:S(2)}, u32[]{:S(2)}) collective-permute-start(bf16[192,512]{1,0:T(8,128)(2,1)} %get-tuple-element.33), channel_id=1, source_target_pairs={{0,64},{32,96},{64,0},{96,32},{1,65},{33,97},{65,1},{97,33},{2,66}... | collective-permute-start | bytes 589832 | tf_op jit(solution)/shard_map/ppermute | solution.py:584
  31.1 9.2 %collective-permute-start.2 = (bf16[192,512]{1,0:T(8,128)(2,1)}, bf16[192,512]{1,0:T(8,128)(2,1)S(1)}, u32[]{:S(2)}, u32[]{:S(2)}) collective-permute-start(bf16[192,512]{1,0:T(8,128)(2,1)} %get-tuple-element.34), channel_id=1, source_target_pairs={{0,96},{32,0},{64,32},{96,64},{1,97},{33,1},{65,33},{97,65},{2,98}... | collective-permute-start | bytes 589832 | tf_op jit(solution)/shard_map/ppermute | solution.py:584
  39.0 17.5 %copy-start.2 = (bf16[192,512]{1,0:T(8,128)(2,1)}, bf16[192,512]{1,0:T(8,128)(2,1)S(1)}, u32[]{:S(2)}) copy-start(bf16[192,512]{1,0:T(8,128)(2,1)S(1)} %collective-permute-done) | copy-start | bytes 589828
  40.4 16.2 %copy-start.3 = (bf16[192,512]{1,0:T(8,128)(2,1)}, bf16[192,512]{1,0:T(8,128)(2,1)S(1)}, u32[]{:S(2)}) copy-start(bf16[192,512]{1,0:T(8,128)(2,1)S(1)} %collective-permute-done.1) | copy-start | bytes 589828
  40.4 16.2 %copy-start.4 = (bf16[192,512]{1,0:T(8,128)(2,1)}, bf16[192,512]{1,0:T(8,128)(2,1)S(1)}, u32[]{:S(2)}) copy-start(bf16[192,512]{1,0:T(8,128)(2,1)S(1)} %collective-permute-done.2) | copy-start | bytes 589828
  86.6 21.5 %copy-start = (f32[2,2,8,2,3,4,512]{6,5,4,3,2,1,0:T(4,128)S(1)}, f32[2,2,8,2,3,4,512]{6,5,4,3,2,1,0:T(4,128)}, u32[]{:S(2)}) copy-start(f32[2,2,8,2,3,4,512]{6,5,4,3,2,1,0:T(4,128)} %get-tuple-element.45.base_ref) | copy-start | bytes 4718596
  93.4 11.7 %collective-permute-start.3 = (bf16[192,512]{1,0:T(8,128)(2,1)}, bf16[192,512]{1,0:T(8,128)(2,1)S(1)}, u32[]{:S(2)}, u32[]{:S(2)}) collective-permute-start(bf16[192,512]{1,0:T(8,128)(2,1)} %get-tuple-element.42), channel_id=1, source_target_pairs={{0,96},{32,0},{64,32},{96,64},{1,97},{33,1},{65,33},{97,65},{2,98}... | collective-permute-start | bytes 589832 | tf_op jit(solution)/shard_map/ppermute | solution.py:584
  95.4 9.8 %collective-permute-start.4 = (bf16[192,512]{1,0:T(8,128)(2,1)}, bf16[192,512]{1,0:T(8,128)(2,1)S(1)}, u32[]{:S(2)}, u32[]{:S(2)}) collective-permute-start(bf16[192,512]{1,0:T(8,128)(2,1)} %get-tuple-element.43), channel_id=1, source_target_pairs={{0,64},{32,96},{64,0},{96,32},{1,65},{33,97},{65,1},{97,33},{2,66}... | collective-permute-start | bytes 589832 | tf_op jit(solution)/shard_map/ppermute | solution.py:584
  96.3 11.8 %collective-permute-start.5 = (bf16[192,512]{1,0:T(8,128)(2,1)}, bf16[192,512]{1,0:T(8,128)(2,1)S(1)}, u32[]{:S(2)}, u32[]{:S(2)}) collective-permute-start(bf16[192,512]{1,0:T(8,128)(2,1)} %get-tuple-element.44), channel_id=1, source_target_pairs={{0,32},{32,64},{64,96},{96,0},{1,33},{33,65},{65,97},{97,1},{2,34}... | collective-permute-start | bytes 589832 | tf_op jit(solution)/shard_map/ppermute | solution.py:584
  96.6 17.8 %all-to-all-start.2 = ((f32[128,1,128]{2,1,0:T(1,128)}), f32[128,1,128]{2,1,0:T(1,128)S(1)}, u32[]{:S(2)}, u32[]{:S(2)}) async-start(f32[128,1,128]{2,1,0:T(1,128)} %get-tuple-element.40), calls=%async_computation.2 | async-start | bytes 131072 | tf_op jit(solution)/shard_map/all_to_all | solution.py:580
  108.1 0.9 copy-start.1

commit v6 on v5

--- a/solution.py
+++ b/solution.py
@@ -211,10 +211,9 @@
     return high, (x - high.astype(jnp.float32)).astype(jnp.bfloat16)
 
 
-def table_kernel(row1_ref, row2_ref, wave_ref, tab_ref, back_ref, keep_ref):
+def table_kernel(row1_ref, row2_ref, tab_ref, back_ref, keep_ref):
     first = lax.broadcasted_iota(jnp.int32, (1, 128), 1) == 0
     halve = jnp.where(first, 0.5, 1.0)
-    wave = wave_ref[...]
 
     def rows(j, _):
         lead_c = row1_ref[0, pl.ds(j, 1), :]
@@ -224,7 +223,7 @@
         at = pl.ds(pl.multiple_of(16 * j, 16), 16)
         keep_ref[0, at, :] = cosine
         keep_ref[1, at, :] = sine
-        for t, value in enumerate((cosine, sine, -wave * cosine, wave * sine)):
+        for t, value in enumerate((cosine, sine)):
             high, low = split(value)
             tab_ref[t, 0, at, :] = high
             tab_ref[t, 1, at, :] = low
@@ -247,7 +246,7 @@
 def small_tables():
     scale = 1.0 / math.sqrt(MODES)
     step = 2.0 * math.pi / POINTS
-    rows1, rows2, waves = [], [], []
+    rows1, rows2 = [], []
     place = np.arange(NBAND)
     block = place % 4 * 8 + place // 4 % 4 * 2 + place // 16
     pairs = (block[:, None] * PAIRS + np.arange(PAIRS)).reshape(-1)
@@ -260,8 +259,7 @@
 
         rows1.append(pair(16 * np.arange(ROWS // 16), 1.0))
         rows2.append(pair(np.arange(16), scale))
-        waves.append(m[None, :] / MODES)
-    return [np.stack(x).astype(np.float32) for x in (rows1, rows2, waves)]
+    return [np.stack(x).astype(np.float32) for x in (rows1, rows2)]
 
 
 def tables(parts):
@@ -273,17 +271,17 @@
             spec((None,) + x.shape[1:], lambda i, n=x.ndim: (i,) + (0,) * (n - 1)) for x in parts
         ],
         out_specs=(
-            spec((4, 2, ROWS, HALF), lambda i: (i, 0, 0, 0)),
+            spec((2, 2, ROWS, HALF), lambda i: (i, 0, 0, 0)),
             spec((2, 2, HALF, QUARTER), lambda i: (i, 0, 0, 0)),
         ),
         out_shape=(
-            jax.ShapeDtypeStruct((8, 2, ROWS, HALF), jnp.bfloat16),
+            jax.ShapeDtypeStruct((4, 2, ROWS, HALF), jnp.bfloat16),
             jax.ShapeDtypeStruct((4, 2, HALF, QUARTER), jnp.bfloat16),
         ),
         scratch_shapes=[pltpu.VMEM((2, ROWS, HALF), jnp.float32)],
         compiler_params=pltpu.CompilerParams(vmem_limit_bytes=60 * MIB),
         cost_estimate=pl.CostEstimate(
-            flops=16 * ROWS * HALF, bytes_accessed=15 * MIB, transcendentals=0
+            flops=16 * ROWS * HALF, bytes_accessed=9 * MIB, transcendentals=0
         ),
         name="tables",
     )(*parts)
@@ -292,34 +290,42 @@
 def grid_kernel(
     got_ref, tab_hbm, back_hbm, rows_ref,
     out_ref,
-    tab_ref, back_ref, sems, x_ref, wave_ref, fold_ref, edge_ref,
+    tab_ref, back_ref, sems, x_ref, rest_ref, wave_ref, fold_ref, edge_ref,
 ):
     copies = [
-        pltpu.make_async_copy(tab_hbm.at[t], tab_ref.at[t], sems.at[t]) for t in range(8)
+        pltpu.make_async_copy(tab_hbm.at[i], tab_ref.at[i], sems.at[i]) for i in range(4)
     ] + [
-        pltpu.make_async_copy(back_hbm.at[i], back_ref.at[i], sems.at[8 + i]) for i in range(4)
+        pltpu.make_async_copy(back_hbm.at[i], back_ref.at[i], sems.at[4 + i]) for i in range(4)
     ]
     for copy in copies:
         copy.start()
+    index = lax.broadcasted_iota(jnp.int32, (HALF, 1), 0)
+    place = index >> 4
+    first = ((place & 3) * 8 + (place >> 2 & 3) * 2 + (place >> 4)) * PAIRS + (index & 15)
+    for par in range(2):
+        ratio = (2 * first + par).astype(jnp.float32) * (1.0 / MODES)
+        for c in range(2):
+            at = (2 * par + c) * PAIRS
+            value = got_ref[:, at : at + PAIRS, :].reshape(HALF, LANES)
+            scaled = value.astype(jnp.float32) * (ratio if c == 0 else -ratio)
+            high, low = split(scaled)
+            x_ref[2 * par + c, :, :LANES] = value
+            x_ref[2 * par + 1 - c, :, LANES:] = high
+            rest_ref[2 * par + 1 - c] = low
     for i in range(4):
-        x_ref[i] = got_ref[:, i * PAIRS : (i + 1) * PAIRS, :].reshape(HALF, LANES)
-    which = (0, 1, 1, 0, 2, 3, 3, 2)
-    for t in range(8):
-        copies[t].wait()
-        x = x_ref[which[t]]
-        wave_ref[t] = mm(tab_ref[t, 0], x) + mm(tab_ref[t, 1], x)
+        copies[i].wait()
+        wave_ref[i] = mm(tab_ref[i, 0], x_ref[i]) + mm(tab_ref[i, 1], x_ref[i])
+        wave_ref[i, :, LANES:] += mm(tab_ref[i, 0], rest_ref[i])
     cor = rows_ref[0:1, :]
 
     def quads(base, at, lanes):
-        ce, se = wave_ref[base, at, lanes], wave_ref[base + 1, at, lanes]
-        co, so = wave_ref[base + 4, at, lanes], wave_ref[base + 5, at, lanes]
+        ce, se, co, so = (wave_ref[i, at, base + lanes : base + lanes + 128] for i in range(4))
         a, b, s, d = ce + co, ce - co, se + so, se - so
         return a - s, b + d, b - d, a + s
 
     def tendency(at):
-        cuts = [pl.ds(128 * f, 128) for f in range(3)]
-        values = [quads(0, at, cut) for cut in cuts]
-        slopes = [quads(2, at, cut) for cut in cuts]
+        values = [quads(0, at, 128 * f) for f in range(3)]
+        slopes = [quads(LANES, at, 128 * f) for f in range(3)]
         out = [[], [], []]
         for q in range(4):
             u, v, h = (values[f][q] for f in range(3))
@@ -355,7 +361,7 @@
         both = []
         for c in range(2):
             i = 2 * par + c
-            copies[8 + i].wait()
+            copies[4 + i].wait()
             both_parts = mm(back_ref[i, 0], fold_ref[i])
             out = both_parts[:, :LANES] + both_parts[:, LANES:]
             out = out + mm(back_ref[i, 1], fold_ref[i, :, :LANES])
@@ -386,11 +392,12 @@
         ],
         out_shape=jax.ShapeDtypeStruct((NBAND, 4, 16, LANES), jnp.bfloat16),
         scratch_shapes=[
-            pltpu.VMEM((8, 2, ROWS, HALF), jnp.bfloat16),
+            pltpu.VMEM((4, 2, ROWS, HALF), jnp.bfloat16),
             pltpu.VMEM((4, 2, HALF, QUARTER), jnp.bfloat16),
-            pltpu.SemaphoreType.DMA((12,)),
+            pltpu.SemaphoreType.DMA((8,)),
+            pltpu.VMEM((4, HALF, 2 * LANES), jnp.bfloat16),
             pltpu.VMEM((4, HALF, LANES), jnp.bfloat16),
-            pltpu.VMEM((8, ROWS, LANES), jnp.float32),
+            pltpu.VMEM((4, ROWS, 2 * LANES), jnp.float32),
             pltpu.VMEM((4, QUARTER, 2 * LANES), jnp.bfloat16),
             pltpu.VMEM((2, 16, LANES), jnp.float32),
         ],
@@ -530,7 +537,7 @@
             *[jax.ShapeDtypeStruct((8 * COLS, DEGREES), jnp.bfloat16)] * 4,
             jax.ShapeDtypeStruct((4 * NBAND, 1, 128), jnp.float32),
         ),
-        compiler_params=pltpu.CompilerParams(vmem_limit_bytes=56 * MIB),
+        compiler_params=pltpu.CompilerParams(vmem_limit_bytes=46 * MIB),
         cost_estimate=pl.CostEstimate(
             flops=2 * 32 * COLS * LATS * DEGREES, bytes_accessed=10 * MIB, transcendentals=0
         ),

time: 116 us -> 114 us (0.983)
  Pallas kernels: 45.1 us -> 41.9 us
  waiting for transfers between devices: 11.1 us -> 13.7 us
    pallas_call x1, Pallas kernels: 6.56 us -> 4.87 us  [tables(): pl.pallas_call(table_kernel, grid=(2,), in_specs=[spec((None,) + x.shape[...]
    ppermute x6, waiting for transfers between devices: 4.34 us -> 5.9 us  [shift(): return lax.ppermute(x, axis, [(i, (i + by) % 4) for i in range(4)])]
  transfers between devices with their start and end apart: 8 -> 8, of which waited for: 4 -> 4; matrix products, arithmetic and copies ran while one was open for 0% -> 1% of each run, Pallas kernels for 12% -> 11%
where the time goes in v6:
time: 114 us
  Pallas kernels  41.9 us (37%)
  blocking collectives  30 us (26%)
  starting transfers between devices  25.8 us (23%)
  waiting for transfers between devices  13.7 us (12%)
    all_to_all x1, blocking collectives, exchange(): return lax.all_to_all(x, axes, split_axis=0, concat_axis=0, tiled=True)  30 us
    all_to_all x2, starting transfers between devices, exchange(): return lax.all_to_all(x, axes, split_axis=0, concat_axis=0, tiled=True)  17.1 us
    pallas_call x1, Pallas kernels, synthesis(): pl.pallas_call(synthesis_kernel, in_specs=[pl.BlockSpec(memory_space=pl.A...  12.2 us
    pallas_call x1, Pallas kernels, grid_stage(): pl.pallas_call(grid_kernel, in_specs=[pl.BlockSpec(memory_space=pltpu.VME...  11.8 us
    ppermute x6, starting transfers between devices, shift(): return lax.ppermute(x, axis, [(i, (i + by) % 4) for i in range(4)])  8.74 us
    all_to_all x2, waiting for transfers between devices, exchange(): return lax.all_to_all(x, axes, split_axis=0, concat_axis=0, tiled=True)  7.85 us
    pallas_call x1, Pallas kernels, analysis(): pl.pallas_call(analysis_kernel, grid_spec=pltpu.PrefetchScalarGridSpec(nu...  5.95 us
    ppermute x6, waiting for transfers between devices, shift(): return lax.ppermute(x, axis, [(i, (i + by) % 4) for i in range(4)])  5.9 us
  transfers between devices with their start and end apart: 8, of which 4 were waited for; matrix products, arithmetic and copies ran while one was open for 1% of the time, Pallas kernels for 11%

profile of v6, /device:TPU:1, one launch (start us, length us, event | category | flops | bytes accessed | tf_op | source)
XLA Modules:
  0.0 113.6 jit_solution(6224365722404007626)
XLA Ops:
  0.6 12.2 %synthesis.1 = bf16[32,64,384]{2,1,0:T(8,128)(2,1)} custom-call(f32[2,16,2,3,4,512]{5,4,3,2,1,0:T(4,128)} %bitcast.40, bf16[16,2,512,512]{3,2,1,0:T(8,128)(2,1)} %bitcast.38), custom_call_target="tpu_custom_call" | custom-call | flops 402653184 | bytes 20971520 | tf_op jit(solution)/shard_map/synthesis/pallas_call | solution.py:115
  12.8 8.6 %all-to-all-start = ((bf16[32,64,384]{2,1,0:T(8,128)(2,1)}), bf16[32,64,384]{2,1,0:T(8,128)(2,1)S(1)}, u32[]{:S(2)}, u32[]{:S(2)}) async-start(bf16[32,64,384]{2,1,0:T(8,128)(2,1)} %synthesis.1), calls=%async_computation | async-start | bytes 3145728 | tf_op jit(solution)/shard_map/all_to_all | solution.py:587
  21.4 0.0 copy-start.6
  21.4 0.0 copy-start.5
  21.4 4.8 %prepare.1 = (bf16[192,512]{1,0:T(8,128)(2,1)}, bf16[192,512]{1,0:T(8,128)(2,1)}, bf16[192,512]{1,0:T(8,128)(2,1)}, bf16[192,512]{1,0:T(8,128)(2,1)}, f32[2,2,8,2,3,4,512]{6,5,4,3,2,1,0:T(4,128)}) custom-call(s32[1]{0:T(128)} %bitcast.id_ref, f32[4,4]{1,0:T(4,128)} %quad_ref.2, f32[2,2,8,2,3,4,512]{6,5,4,3,2,1,0:T(4,128)} %bitcast.29, ...), custom_call_target="tpu_custom_call" | custom-call | flops 3145728 | bytes 6291456 | tf_op jit(solution)/shard_map/prepare/pallas_call | solution.py:185
  26.2 1.6 %collective-permute-start = (bf16[192,512]{1,0:T(8,128)(2,1)}, bf16[192,512]{1,0:T(8,128)(2,1)S(1)}, u32[]{:S(2)}, u32[]{:S(2)}) collective-permute-start(bf16[192,512]{1,0:T(8,128)(2,1)} %get-tuple-element.30), channel_id=1, source_target_pairs={{0,32},{32,64},{64,96},{96,0},{1,33},{33,65},{65,97},{97,1},{2,34}... | collective-permute-start | bytes 589832 | tf_op jit(solution)/shard_map/ppermute | solution.py:591
  27.8 3.3 %collective-permute-start.1 = (bf16[192,512]{1,0:T(8,128)(2,1)}, bf16[192,512]{1,0:T(8,128)(2,1)S(1)}, u32[]{:S(2)}, u32[]{:S(2)}) collective-permute-start(bf16[192,512]{1,0:T(8,128)(2,1)} %get-tuple-element.31), channel_id=1, source_target_pairs={{0,64},{32,96},{64,0},{96,32},{1,65},{33,97},{65,1},{97,33},{2,66}... | collective-permute-start | bytes 589832 | tf_op jit(solution)/shard_map/ppermute | solution.py:591
  31.1 0.7 collective-permute-start.2
  31.8 0.1 dynamic_slice.7
  31.9 0.1 constant_dynamic-slice_fusion
  32.0 0.1 broadcast_select_fusion
  32.1 0.1 reshape.116
  32.2 4.9 %tables.1 = (bf16[4,2,528,512]{3,2,1,0:T(8,128)(2,1)}, bf16[4,2,512,512]{3,2,1,0:T(8,128)(2,1)}) custom-call(f32[2,2,33,512]{3,2,1,0:T(8,128)} %constant.59.clone.row1_ref, f32[2,2,16,512]{3,2,1,0:T(8,128)} %constant.60.clone.row2_ref), custom_call_target="tpu_custom_call" | custom-call | flops 4325376 | bytes 9437184 | tf_op jit(solution)/shard_map/tables/pallas_call | solution.py:267
  37.0 0.1 dynamic-slice_bitcast_fusion
  37.1 0.1 compare_select_fusion
  37.2 0.1 maximum_bitcast_fusion
  37.3 3.1 %collective-permute-done.1 = bf16[192,512]{1,0:T(8,128)(2,1)S(1)} collective-permute-done((bf16[192,512]{1,0:T(8,128)(2,1)}, bf16[192,512]{1,0:T(8,128)(2,1)S(1)}, u32[]{:S(2)}, u32[]{:S(2)}) %collective-permute-start.1) | collective-permute-done | bytes 196640 | tf_op jit(solution)/shard_map/ppermute | solution.py:591
  40.4 3.7 %all-to-all-done.got_ref = bf16[32,64,384]{2,1,0:T(8,128)(2,1)S(1)} async-done(((bf16[32,64,384]{2,1,0:T(8,128)(2,1)}), bf16[32,64,384]{2,1,0:T(8,128)(2,1)S(1)}, u32[]{:S(2)}, u32[]{:S(2)}) %all-to-all-start) | async-done | bytes 1572896 | tf_op jit(solution)/shard_map/all_to_all | solution.py:587
  44.0 11.8 %grid.1 = bf16[32,4,16,384]{3,2,1,0:T(8,128)(2,1)S(1)} custom-call(bf16[32,64,384]{2,1,0:T(8,128)(2,1)S(1)} %all-to-all-done.got_ref, bf16[4,2,528,512]{3,2,1,0:T(8,128)(2,1)} %get-tuple-element.26.tab_hbm, bf16[4,2,512,512]{3,2,1,0:T(8,128)(2,1)} %get-tuple-element.27.back_hbm, f32[3,128]{1,0:T(4,128)S(1)} %pad_maximum_fusion.rows_ref), custom_call_target="tpu_custom_call" | custom-call | flops 5813305344 | bytes 17825792 | tf_op jit(solution)/shard_map/grid/pallas_call | solution.py:385
  55.9 0.0 copy-start.2
  55.9 0.0 copy-start.4
  55.9 30.0 %all_to_all.15.y_ref = bf16[128,16,384]{2,1,0:T(8,128)(2,1)S(1)} all-to-all(bf16[128,16,384]{2,1,0:T(8,128)(2,1)S(1)} %bitcast.31), channel_id=1, replica_groups=mesh['node'=4,'band_0'=4,'band_1'=4,'band_2'=2] {'band_2','band_1','band..., dimensions={0} | all-to-all | bytes 3145728 | tf_op jit(solution)/shard_map/all_to_all | solution.py:587
  85.9 5.9 %analysis.1 = (bf16[192,512]{1,0:T(8,128)(2,1)S(1)}, bf16[192,512]{1,0:T(8,128)(2,1)S(1)}, bf16[192,512]{1,0:T(8,128)(2,1)S(1)}, bf16[192,512]{1,0:T(8,128)(2,1)S(1)}, f32[128,1,128]{2,1,0:T(1,128)}) custom-call(s32[1]{0:T(128)} %bitcast.id_ref, f32[4,4]{1,0:T(4,128)S(1)} %copy-done.4, bf16[128,16,384]{2,1,0:T(8,128)(2,1)S(1)} %all_to_all.15.y_ref, ...), custom_call_target="tpu_custom_call" | custom-call | flops 402653184 | bytes 10485760 | tf_op jit(solution)/shard_map/analysis/pallas_call | solution.py:506
  91.9 1.9 %collective-permute-start.3 = (bf16[192,512]{1,0:T(8,128)(2,1)S(1)}, bf16[192,512]{1,0:T(8,128)(2,1)S(1)}, u32[]{:S(2)}, u32[]{:S(2)}) collective-permute-start(bf16[192,512]{1,0:T(8,128)(2,1)S(1)} %get-tuple-element.40), channel_id=1, source_target_pairs={{0,96},{32,0},{64,32},{96,64},{1,97},{33,1},{65,33},{97,65},{2,98}... | collective-permute-start | bytes 589832 | tf_op jit(solution)/shard_map/ppermute | solution.py:591
  93.8 0.9 collective-permute-start.4
  94.7 0.3 collective-permute-start.5
  95.0 8.5 %all-to-all-start.2 = ((f32[128,1,128]{2,1,0:T(1,128)}), f32[128,1,128]{2,1,0:T(1,128)S(1)}, u32[]{:S(2)}, u32[]{:S(2)}) async-start(f32[128,1,128]{2,1,0:T(1,128)} %get-tuple-element.38), calls=%async_computation.2 | async-start | bytes 131072 | tf_op jit(solution)/shard_map/all_to_all | solution.py:587
  103.5 2.8 %collective-permute-done.5.mixed3_ref = bf16[192,512]{1,0:T(8,128)(2,1)S(1)} collective-permute-done((bf16[192,512]{1,0:T(8,128)(2,1)S(1)}, bf16[192,512]{1,0:T(8,128)(2,1)S(1)}, u32[]{:S(2)}, u32[]{:S(2)}) %collective-permute-start.5) | collective-permute-done | bytes 196640 | tf_op jit(solution)/shard_map/ppermute | solution.py:591
  106.3 2.4 %update.1 = f32[2,2,8,2,3,4,512]{6,5,4,3,2,1,0:T(4,128)} custom-call(s32[1]{0:T(128)} %bitcast.id_ref, bf16[192,512]{1,0:T(8,128)(2,1)S(1)} %get-tuple-element.39.mixed0_ref, bf16[192,512]{1,0:T(8,128)(2,1)S(1)} %collective-permute-done.3.mixed1_ref, bf16[192,512]{1,0:T(8,128)(2,1)S(1)} %collective-permute-done.4.mixed2_ref, ...), custom_call_target="tpu_custom_call" | custom-call | flops 1572864 | bytes 5242880 | tf_op jit(solution)/shard_map/update/pallas_call | solution.py:568
  108.7 4.2 %all-to-all-done.2 = f32[128,1,128]{2,1,0:T(1,128)S(1)} async-done(((f32[128,1,128]{2,1,0:T(1,128)}), f32[128,1,128]{2,1,0:T(1,128)S(1)}, u32[]{:S(2)}, u32[]{:S(2)}) %all-to-all-start.2) | async-done | bytes 65568 | tf_op jit(solution)/shard_map/all_to_all | solution.py:587
  112.9 0.2 reduce_sum.9
  113.0 0.6 fusion
  (16 shorter events, 0.1 us)
Async XLA Ops:
  12.8 31.3 %all-to-all-start = ((bf16[32,64,384]{2,1,0:T(8,128)(2,1)}), bf16[32,64,384]{2,1,0:T(8,128)(2,1)S(1)}, u32[]{:S(2)}, u32[]{:S(2)}) async-start(bf16[32,64,384]{2,1,0:T(8,128)(2,1)} %synthesis.1), calls=%async_computation | async-start | bytes 3145728 | tf_op jit(solution)/shard_map/all_to_all | solution.py:587
  21.4 10.4 %copy-start.6 = (f32[512]{0:T(512)S(1)}, f32[512]{0:T(512)}, u32[]{:S(2)}) copy-start(f32[512]{0:T(512)} %param.12) | copy-start | bytes 6148
  21.4 10.5 %copy-start.5 = (f32[2,512]{1,0:T(2,128)S(1)}, f32[2,512]{1,0:T(2,128)}, u32[]{:S(2)}) copy-start(f32[2,512]{1,0:T(2,128)} %param.13) | copy-start | bytes 12292
  26.2 11.1 %collective-permute-start = (bf16[192,512]{1,0:T(8,128)(2,1)}, bf16[192,512]{1,0:T(8,128)(2,1)S(1)}, u32[]{:S(2)}, u32[]{:S(2)}) collective-permute-start(bf16[192,512]{1,0:T(8,128)(2,1)} %get-tuple-element.30), channel_id=1, source_target_pairs={{0,32},{32,64},{64,96},{96,0},{1,33},{33,65},{65,97},{97,1},{2,34}... | collective-permute-start | bytes 589832 | tf_op jit(solution)/shard_map/ppermute | solution.py:591
  27.8 12.5 %collective-permute-start.1 = (bf16[192,512]{1,0:T(8,128)(2,1)}, bf16[192,512]{1,0:T(8,128)(2,1)S(1)}, u32[]{:S(2)}, u32[]{:S(2)}) collective-permute-start(bf16[192,512]{1,0:T(8,128)(2,1)} %get-tuple-element.31), channel_id=1, source_target_pairs={{0,64},{32,96},{64,0},{96,32},{1,65},{33,97},{65,1},{97,33},{2,66}... | collective-permute-start | bytes 589832 | tf_op jit(solution)/shard_map/ppermute | solution.py:591
  31.1 9.2 %collective-permute-start.2 = (bf16[192,512]{1,0:T(8,128)(2,1)}, bf16[192,512]{1,0:T(8,128)(2,1)S(1)}, u32[]{:S(2)}, u32[]{:S(2)}) collective-permute-start(bf16[192,512]{1,0:T(8,128)(2,1)} %get-tuple-element.32), channel_id=1, source_target_pairs={{0,96},{32,0},{64,32},{96,64},{1,97},{33,1},{65,33},{97,65},{2,98}... | collective-permute-start | bytes 589832 | tf_op jit(solution)/shard_map/ppermute | solution.py:591
  55.9 30.0 %copy-start = (f32[2,32,4,3,512]{4,2,3,1,0:T(4,128)S(1)}, f32[2,32,4,3,512]{4,2,3,1,0:T(4,128)}, u32[]{:S(2)}) copy-start(f32[2,32,4,3,512]{4,2,3,1,0:T(4,128)} %param.9) | copy-start | bytes 4718596
  55.9 30.0 %copy-start.2 = (f32[32,3,512]{2,0,1:T(8,128)S(1)}, f32[32,3,512]{2,0,1:T(8,128)}, u32[]{:S(2)}) copy-start(f32[32,3,512]{2,0,1:T(8,128)} %param.14) | copy-start | bytes 589828
  55.9 30.0 %copy-start.3 = (bf16[192,512]{1,0:T(8,128)(2,1)S(1)}, bf16[192,512]{1,0:T(8,128)(2,1)}, u32[]{:S(2)}) copy-start(bf16[192,512]{1,0:T(8,128)(2,1)} %get-tuple-element.34) | copy-start | bytes 589828
  55.9 30.0 %copy-start.4 = (f32[4,4]{1,0:T(4,128)S(1)}, f32[4,4]{1,0:T(4,128)}, u32[]{:S(2)}) copy-start(f32[4,4]{1,0:T(4,128)} %quad_ref.2) | copy-start | bytes 196
  85.9 20.4 %copy-start.1 = (f32[2,2,8,2,3,4,512]{6,5,4,3,2,1,0:T(4,128)S(1)}, f32[2,2,8,2,3,4,512]{6,5,4,3,2,1,0:T(4,128)}, u32[]{:S(2)}) copy-start(f32[2,2,8,2,3,4,512]{6,5,4,3,2,1,0:T(4,128)} %get-tuple-element.43.base_ref) | copy-start | bytes 4718596
  91.9 11.6 %collective-permute-start.3 = (bf16[192,512]{1,0:T(8,128)(2,1)S(1)}, bf16[192,512]{1,0:T(8,128)(2,1)S(1)}, u32[]{:S(2)}, u32[]{:S(2)}) collective-permute-start(bf16[192,512]{1,0:T(8,128)(2,1)S(1)} %get-tuple-element.40), channel_id=1, source_target_pairs={{0,96},{32,0},{64,32},{96,64},{1,97},{33,1},{65,33},{97,65},{2,98}... | collective-permute-start | bytes 589832 | tf_op jit(solution)/shard_map/ppermute | solution.py:591
  93.8 9.7 %collective-permute-start.4 = (bf16[192,512]{1,0:T(8,128)(2,1)S(1)}, bf16[192,512]{1,0:T(8,128)(2,1)S(1)}, u32[]{:S(2)}, u32[]{:S(2)}) collective-permute-start(bf16[192,512]{1,0:T(8,128)(2,1)S(1)} %get-tuple-element.41), channel_id=1, source_target_pairs={{0,64},{32,96},{64,0},{96,32},{1,65},{33,97},{65,1},{97,33},{2,66}... | collective-permute-start | bytes 589832 | tf_op jit(solution)/shard_map/ppermute | solution.py:591
  94.7 11.6 %collective-permute-start.5 = (bf16[192,512]{1,0:T(8,128)(2,1)S(1)}, bf16[192,512]{1,0:T(8,128)(2,1)S(1)}, u32[]{:S(2)}, u32[]{:S(2)}) collective-permute-start(bf16[192,512]{1,0:T(8,128)(2,1)S(1)} %get-tuple-element.42), channel_id=1, source_target_pairs={{0,32},{32,64},{64,96},{96,0},{1,33},{33,65},{65,97},{97,1},{2,34}... | collective-permute-start | bytes 589832 | tf_op jit(solution)/shard_map/ppermute | solution.py:591
  95.0 17.8 %all-to-all-start.2 = ((f32[128,1,128]{2,1,0:T(1,128)}), f32[128,1,128]{2,1,0:T(1,128)S(1)}, u32[]{:S(2)}, u32[]{:S(2)}) async-start(f32[128,1,128]{2,1,0:T(1,128)} %get-tuple-element.38), calls=%async_computation.2 | async-start | bytes 131072 | tf_op jit(solution)/shard_map/all_to_all | solution.py:587

commit v7 on v6

--- a/solution.py
+++ b/solution.py
@@ -523,7 +523,7 @@
             ],
             out_specs=(
                 *[spec((MB * COLS, DEGREES), lambda i, s: (i, 0))] * 4,
-                spec((4 * NBAND, 1, 128), lambda i, s: (0, 0, 0)),
+                spec((NBAND, 1, 128), lambda i, s: (0, 0, 0)),
             ),
             scratch_shapes=[
                 pltpu.VMEM((2, 4, 4 * COLS * 8, 128), jnp.float32),
@@ -535,7 +535,7 @@
         ),
         out_shape=(
             *[jax.ShapeDtypeStruct((8 * COLS, DEGREES), jnp.bfloat16)] * 4,
-            jax.ShapeDtypeStruct((4 * NBAND, 1, 128), jnp.float32),
+            jax.ShapeDtypeStruct((NBAND, 1, 128), jnp.float32),
         ),
         compiler_params=pltpu.CompilerParams(vmem_limit_bytes=46 * MIB),
         cost_estimate=pl.CostEstimate(
@@ -631,7 +631,8 @@
     spectra = exchange(columns.reshape(4 * NBAND, 16, LANES), SEND_NODE)
     *mixed, sums = analysis(ids, quadrature, spectra, leg4, moves, st6, damp)
     mixed = [mixed[0]] + [shift(mixed[s], "node", -s) for s in (1, 2, 3)]
-    sums = exchange(sums, SEND_NODE)
+    near = shift(sums, "node", 1) + shift(sums, "node", -1)
+    sums = exchange((sums + shift(sums, "node", 2)) + near, SEND)
     out = update(ids, mixed, settled)
     sums, out = lax.optimization_barrier((sums, out))
     total = jnp.sum(sums, axis=(0, 1))

time: 114 us -> 114 us (level)
  waiting for transfers between devices: 13.7 us -> 11.1 us
  starting transfers between devices: 25.8 us -> 28.2 us
    ppermute x6 -> x9, starting transfers between devices: 8.74 us -> 12.7 us  [shift(): return lax.ppermute(x, axis, [(i, (i + by) % 4) for i in range(4)])]
    all_to_all x2, waiting for transfers between devices: 7.85 us -> 6.13 us  [exchange(): return lax.all_to_all(x, axes, split_axis=0, concat_axis=0, tiled=True)]
    all_to_all x2, starting transfers between devices: 17.1 us -> 15.5 us  [exchange(): return lax.all_to_all(x, axes, split_axis=0, concat_axis=0, tiled=True)]
    ppermute x6 -> x9, waiting for transfers between devices: 5.9 us -> 4.94 us  [shift(): return lax.ppermute(x, axis, [(i, (i + by) % 4) for i in range(4)])]
  transfers between devices with their start and end apart: 8 -> 11, of which waited for: 4 -> 4; matrix products, arithmetic and copies ran while one was open for 1% -> 1% of each run, Pallas kernels for 11% -> 11%
where the time goes in v7:
time: 114 us; the launch traced here: 113 us
  Pallas kernels  41.3 us (36%)
  blocking collectives  30 us (26%)
  starting transfers between devices  28.2 us (25%)
  waiting for transfers between devices  11.1 us (10%)
  other arithmetic  1.5 us (1%)
    all_to_all x1, blocking collectives, exchange(): return lax.all_to_all(x, axes, split_axis=0, concat_axis=0, tiled=True)  30 us
    all_to_all x2, starting transfers between devices, exchange(): return lax.all_to_all(x, axes, split_axis=0, concat_axis=0, tiled=True)  15.5 us
    ppermute x9, starting transfers between devices, shift(): return lax.ppermute(x, axis, [(i, (i + by) % 4) for i in range(4)])  12.7 us
    pallas_call x1, Pallas kernels, synthesis(): pl.pallas_call(synthesis_kernel, in_specs=[pl.BlockSpec(memory_space=pl.A...  12.2 us
    pallas_call x1, Pallas kernels, grid_stage(): pl.pallas_call(grid_kernel, in_specs=[pl.BlockSpec(memory_space=pltpu.VME...  11.8 us
    all_to_all x2, waiting for transfers between devices, exchange(): return lax.all_to_all(x, axes, split_axis=0, concat_axis=0, tiled=True)  6.13 us
    pallas_call x1, Pallas kernels, analysis(): pl.pallas_call(analysis_kernel, grid_spec=pltpu.PrefetchScalarGridSpec(nu...  5.32 us
    ppermute x9, waiting for transfers between devices, shift(): return lax.ppermute(x, axis, [(i, (i + by) % 4) for i in range(4)])  4.94 us
  transfers between devices with their start and end apart: 11, of which 4 were waited for; matrix products, arithmetic and copies ran while one was open for 1% of the time, Pallas kernels for 11%

profile of v7, /device:TPU:1, one launch (start us, length us, event | category | flops | bytes accessed | tf_op | source)
XLA Modules:
  0.0 113.2 jit_solution(2856196333676971786)
XLA Ops:
  0.6 12.2 %synthesis.1 = bf16[32,64,384]{2,1,0:T(8,128)(2,1)} custom-call(f32[2,16,2,3,4,512]{5,4,3,2,1,0:T(4,128)} %bitcast.46, bf16[16,2,512,512]{3,2,1,0:T(8,128)(2,1)} %bitcast.44), custom_call_target="tpu_custom_call" | custom-call | flops 402653184 | bytes 20971520 | tf_op jit(solution)/shard_map/synthesis/pallas_call | solution.py:115
  12.8 8.6 %all-to-all-start = ((bf16[32,64,384]{2,1,0:T(8,128)(2,1)}), bf16[32,64,384]{2,1,0:T(8,128)(2,1)S(1)}, u32[]{:S(2)}, u32[]{:S(2)}) async-start(bf16[32,64,384]{2,1,0:T(8,128)(2,1)} %synthesis.1), calls=%async_computation | async-start | bytes 3145728 | tf_op jit(solution)/shard_map/all_to_all | solution.py:587
  21.4 4.7 %prepare.1 = (bf16[192,512]{1,0:T(8,128)(2,1)}, bf16[192,512]{1,0:T(8,128)(2,1)}, bf16[192,512]{1,0:T(8,128)(2,1)}, bf16[192,512]{1,0:T(8,128)(2,1)}, f32[2,2,8,2,3,4,512]{6,5,4,3,2,1,0:T(4,128)}) custom-call(s32[1]{0:T(128)} %bitcast.id_ref, f32[4,4]{1,0:T(4,128)} %quad_ref.2, f32[2,2,8,2,3,4,512]{6,5,4,3,2,1,0:T(4,128)} %bitcast.34, ...), custom_call_target="tpu_custom_call" | custom-call | flops 3145728 | bytes 6291456 | tf_op jit(solution)/shard_map/prepare/pallas_call | solution.py:185
  26.2 1.7 %collective-permute-start = (bf16[192,512]{1,0:T(8,128)(2,1)}, bf16[192,512]{1,0:T(8,128)(2,1)S(1)}, u32[]{:S(2)}, u32[]{:S(2)}) collective-permute-start(bf16[192,512]{1,0:T(8,128)(2,1)} %get-tuple-element.30), channel_id=1, source_target_pairs={{0,32},{32,64},{64,96},{96,0},{1,33},{33,65},{65,97},{97,1},{2,34}... | collective-permute-start | bytes 589832 | tf_op jit(solution)/shard_map/ppermute | solution.py:591
  27.8 3.3 %collective-permute-start.1 = (bf16[192,512]{1,0:T(8,128)(2,1)}, bf16[192,512]{1,0:T(8,128)(2,1)S(1)}, u32[]{:S(2)}, u32[]{:S(2)}) collective-permute-start(bf16[192,512]{1,0:T(8,128)(2,1)} %get-tuple-element.31), channel_id=1, source_target_pairs={{0,64},{32,96},{64,0},{96,32},{1,65},{33,97},{65,1},{97,33},{2,66}... | collective-permute-start | bytes 589832 | tf_op jit(solution)/shard_map/ppermute | solution.py:591
  31.1 0.7 collective-permute-start.2
  31.8 0.1 dynamic_slice.7
  31.9 0.1 constant_dynamic-slice_fusion
  32.0 0.1 broadcast_select_fusion
  32.1 0.1 reshape.116
  32.2 4.9 %tables.1 = (bf16[4,2,528,512]{3,2,1,0:T(8,128)(2,1)}, bf16[4,2,512,512]{3,2,1,0:T(8,128)(2,1)}) custom-call(f32[2,2,33,512]{3,2,1,0:T(8,128)} %constant.59.clone.row1_ref, f32[2,2,16,512]{3,2,1,0:T(8,128)} %constant.60.clone.row2_ref), custom_call_target="tpu_custom_call" | custom-call | flops 4325376 | bytes 9437184 | tf_op jit(solution)/shard_map/tables/pallas_call | solution.py:267
  37.1 0.1 dynamic-slice_bitcast_fusion
  37.1 0.1 compare_select_fusion
  37.2 0.1 maximum_bitcast_fusion
  37.3 3.0 %collective-permute-done.1 = bf16[192,512]{1,0:T(8,128)(2,1)S(1)} collective-permute-done((bf16[192,512]{1,0:T(8,128)(2,1)}, bf16[192,512]{1,0:T(8,128)(2,1)S(1)}, u32[]{:S(2)}, u32[]{:S(2)}) %collective-permute-start.1) | collective-permute-done | bytes 196640 | tf_op jit(solution)/shard_map/ppermute | solution.py:591
  40.3 3.7 %all-to-all-done.got_ref = bf16[32,64,384]{2,1,0:T(8,128)(2,1)S(1)} async-done(((bf16[32,64,384]{2,1,0:T(8,128)(2,1)}), bf16[32,64,384]{2,1,0:T(8,128)(2,1)S(1)}, u32[]{:S(2)}, u32[]{:S(2)}) %all-to-all-start) | async-done | bytes 1572896 | tf_op jit(solution)/shard_map/all_to_all | solution.py:587
  44.0 11.8 %grid.1 = bf16[32,4,16,384]{3,2,1,0:T(8,128)(2,1)S(1)} custom-call(bf16[32,64,384]{2,1,0:T(8,128)(2,1)S(1)} %all-to-all-done.got_ref, bf16[4,2,528,512]{3,2,1,0:T(8,128)(2,1)} %get-tuple-element.26.tab_hbm, bf16[4,2,512,512]{3,2,1,0:T(8,128)(2,1)} %get-tuple-element.27.back_hbm, f32[3,128]{1,0:T(4,128)S(1)} %pad_maximum_fusion.rows_ref), custom_call_target="tpu_custom_call" | custom-call | flops 5813305344 | bytes 17825792 | tf_op jit(solution)/shard_map/grid/pallas_call | solution.py:385
  55.9 0.0 copy-start.2
  55.9 0.0 copy-start.4
  55.9 30.0 %all_to_all.15.y_ref = bf16[128,16,384]{2,1,0:T(8,128)(2,1)S(1)} all-to-all(bf16[128,16,384]{2,1,0:T(8,128)(2,1)S(1)} %bitcast.36), channel_id=1, replica_groups=mesh['node'=4,'band_0'=4,'band_1'=4,'band_2'=2] {'band_2','band_1','band..., dimensions={0} | all-to-all | bytes 3145728 | tf_op jit(solution)/shard_map/all_to_all | solution.py:587
  85.9 5.3 %analysis.1 = (bf16[192,512]{1,0:T(8,128)(2,1)S(1)}, bf16[192,512]{1,0:T(8,128)(2,1)S(1)}, bf16[192,512]{1,0:T(8,128)(2,1)S(1)}, bf16[192,512]{1,0:T(8,128)(2,1)S(1)}, f32[32,1,128]{2,1,0:T(1,128)S(1)}) custom-call(s32[1]{0:T(128)} %bitcast.id_ref, f32[4,4]{1,0:T(4,128)S(1)} %copy-done.4, bf16[128,16,384]{2,1,0:T(8,128)(2,1)S(1)} %all_to_all.15.y_ref, ...), custom_call_target="tpu_custom_call" | custom-call | flops 402653184 | bytes 10485760 | tf_op jit(solution)/shard_map/analysis/pallas_call | solution.py:506
  91.2 2.0 %collective-permute-start.5 = (f32[32,1,128]{2,1,0:T(1,128)S(1)}, f32[32,1,128]{2,1,0:T(1,128)S(1)}, u32[]{:S(2)}, u32[]{:S(2)}) collective-permute-start(f32[32,1,128]{2,1,0:T(1,128)S(1)} %get-tuple-element.38), channel_id=1, source_target_pairs={{0,96},{32,0},{64,32},{96,64},{1,97},{33,1},{65,33},{97,65},{2,98}... | collective-permute-start | bytes 49160 | tf_op jit(solution)/shard_map/ppermute | solution.py:591
  93.2 1.8 %collective-permute-start.3 = (f32[32,1,128]{2,1,0:T(1,128)S(1)}, f32[32,1,128]{2,1,0:T(1,128)S(1)}, u32[]{:S(2)}, u32[]{:S(2)}) collective-permute-start(f32[32,1,128]{2,1,0:T(1,128)S(1)} %get-tuple-element.38), channel_id=1, source_target_pairs={{0,64},{32,96},{64,0},{96,32},{1,65},{33,97},{65,1},{97,33},{2,66}... | collective-permute-start | bytes 49160 | tf_op jit(solution)/shard_map/ppermute | solution.py:591
  95.1 1.2 %collective-permute-start.6 = (bf16[192,512]{1,0:T(8,128)(2,1)S(1)}, bf16[192,512]{1,0:T(8,128)(2,1)S(1)}, u32[]{:S(2)}, u32[]{:S(2)}) collective-permute-start(bf16[192,512]{1,0:T(8,128)(2,1)S(1)} %get-tuple-element.40), channel_id=1, source_target_pairs={{0,96},{32,0},{64,32},{96,64},{1,97},{33,1},{65,33},{97,65},{2,98}... | collective-permute-start | bytes 589832 | tf_op jit(solution)/shard_map/ppermute | solution.py:591
  96.2 2.0 %collective-permute-start.7 = (bf16[192,512]{1,0:T(8,128)(2,1)S(1)}, bf16[192,512]{1,0:T(8,128)(2,1)S(1)}, u32[]{:S(2)}, u32[]{:S(2)}) collective-permute-start(bf16[192,512]{1,0:T(8,128)(2,1)S(1)} %get-tuple-element.41), channel_id=1, source_target_pairs={{0,64},{32,96},{64,0},{96,32},{1,65},{33,97},{65,1},{97,33},{2,66}... | collective-permute-start | bytes 589832 | tf_op jit(solution)/shard_map/ppermute | solution.py:591
  98.3 0.6 add_add_fusion
  98.9 6.9 %all-to-all-start.2 = ((f32[32,1,128]{2,1,0:T(1,128)}), f32[32,1,128]{2,1,0:T(1,128)S(1)}, u32[]{:S(2)}, u32[]{:S(2)}) async-start(f32[32,1,128]{2,1,0:T(1,128)} %bitcast.33), calls=%async_computation.2 | async-start | bytes 32768 | tf_op jit(solution)/shard_map/all_to_all | solution.py:587
  105.8 1.9 %collective-permute-done.8.mixed3_ref = bf16[192,512]{1,0:T(8,128)(2,1)S(1)} collective-permute-done((bf16[192,512]{1,0:T(8,128)(2,1)S(1)}, bf16[192,512]{1,0:T(8,128)(2,1)S(1)}, u32[]{:S(2)}, u32[]{:S(2)}) %collective-permute-start.8) | collective-permute-done | bytes 196640 | tf_op jit(solution)/shard_map/ppermute | solution.py:591
  107.7 2.4 %update.1 = f32[2,2,8,2,3,4,512]{6,5,4,3,2,1,0:T(4,128)} custom-call(s32[1]{0:T(128)} %bitcast.id_ref, bf16[192,512]{1,0:T(8,128)(2,1)S(1)} %get-tuple-element.39.mixed0_ref, bf16[192,512]{1,0:T(8,128)(2,1)S(1)} %collective-permute-done.6.mixed1_ref, bf16[192,512]{1,0:T(8,128)(2,1)S(1)} %collective-permute-done.7.mixed2_ref, ...), custom_call_target="tpu_custom_call" | custom-call | flops 1572864 | bytes 5242880 | tf_op jit(solution)/shard_map/update/pallas_call | solution.py:568
  110.1 2.4 %all-to-all-done.2 = f32[32,1,128]{2,1,0:T(1,128)S(1)} async-done(((f32[32,1,128]{2,1,0:T(1,128)}), f32[32,1,128]{2,1,0:T(1,128)S(1)}, u32[]{:S(2)}, u32[]{:S(2)}) %all-to-all-start.2) | async-done | bytes 16416 | tf_op jit(solution)/shard_map/all_to_all | solution.py:587
  112.5 0.1 reduce_sum.9
  112.6 0.6 fusion
  (23 shorter events, 0.1 us)
Async XLA Ops:
  12.8 31.3 %all-to-all-start = ((bf16[32,64,384]{2,1,0:T(8,128)(2,1)}), bf16[32,64,384]{2,1,0:T(8,128)(2,1)S(1)}, u32[]{:S(2)}, u32[]{:S(2)}) async-start(bf16[32,64,384]{2,1,0:T(8,128)(2,1)} %synthesis.1), calls=%async_computation | async-start | bytes 3145728 | tf_op jit(solution)/shard_map/all_to_all | solution.py:587
  21.4 10.4 %copy-start.6 = (f32[512]{0:T(512)S(1)}, f32[512]{0:T(512)}, u32[]{:S(2)}) copy-start(f32[512]{0:T(512)} %param.12) | copy-start | bytes 6148
  21.4 10.5 %copy-start.5 = (f32[2,512]{1,0:T(2,128)S(1)}, f32[2,512]{1,0:T(2,128)}, u32[]{:S(2)}) copy-start(f32[2,512]{1,0:T(2,128)} %param.13) | copy-start | bytes 12292
  26.2 11.1 %collective-permute-start = (bf16[192,512]{1,0:T(8,128)(2,1)}, bf16[192,512]{1,0:T(8,128)(2,1)S(1)}, u32[]{:S(2)}, u32[]{:S(2)}) collective-permute-start(bf16[192,512]{1,0:T(8,128)(2,1)} %get-tuple-element.30), channel_id=1, source_target_pairs={{0,32},{32,64},{64,96},{96,0},{1,33},{33,65},{65,97},{97,1},{2,34}... | collective-permute-start | bytes 589832 | tf_op jit(solution)/shard_map/ppermute | solution.py:591
  27.8 12.5 %collective-permute-start.1 = (bf16[192,512]{1,0:T(8,128)(2,1)}, bf16[192,512]{1,0:T(8,128)(2,1)S(1)}, u32[]{:S(2)}, u32[]{:S(2)}) collective-permute-start(bf16[192,512]{1,0:T(8,128)(2,1)} %get-tuple-element.31), channel_id=1, source_target_pairs={{0,64},{32,96},{64,0},{96,32},{1,65},{33,97},{65,1},{97,33},{2,66}... | collective-permute-start | bytes 589832 | tf_op jit(solution)/shard_map/ppermute | solution.py:591
  31.1 9.2 %collective-permute-start.2 = (bf16[192,512]{1,0:T(8,128)(2,1)}, bf16[192,512]{1,0:T(8,128)(2,1)S(1)}, u32[]{:S(2)}, u32[]{:S(2)}) collective-permute-start(bf16[192,512]{1,0:T(8,128)(2,1)} %get-tuple-element.32), channel_id=1, source_target_pairs={{0,96},{32,0},{64,32},{96,64},{1,97},{33,1},{65,33},{97,65},{2,98}... | collective-permute-start | bytes 589832 | tf_op jit(solution)/shard_map/ppermute | solution.py:591
  55.9 30.0 %copy-start = (f32[2,32,4,3,512]{4,2,3,1,0:T(4,128)S(1)}, f32[2,32,4,3,512]{4,2,3,1,0:T(4,128)}, u32[]{:S(2)}) copy-start(f32[2,32,4,3,512]{4,2,3,1,0:T(4,128)} %param.9) | copy-start | bytes 4718596
  55.9 30.0 %copy-start.2 = (f32[32,3,512]{2,0,1:T(8,128)S(1)}, f32[32,3,512]{2,0,1:T(8,128)}, u32[]{:S(2)}) copy-start(f32[32,3,512]{2,0,1:T(8,128)} %param.14) | copy-start | bytes 589828
  55.9 30.0 %copy-start.3 = (bf16[192,512]{1,0:T(8,128)(2,1)S(1)}, bf16[192,512]{1,0:T(8,128)(2,1)}, u32[]{:S(2)}) copy-start(bf16[192,512]{1,0:T(8,128)(2,1)} %get-tuple-element.34) | copy-start | bytes 589828
  55.9 30.0 %copy-start.4 = (f32[4,4]{1,0:T(4,128)S(1)}, f32[4,4]{1,0:T(4,128)}, u32[]{:S(2)}) copy-start(f32[4,4]{1,0:T(4,128)} %quad_ref.2) | copy-start | bytes 196
  85.9 21.8 %copy-start.1 = (f32[2,2,8,2,3,4,512]{6,5,4,3,2,1,0:T(4,128)S(1)}, f32[2,2,8,2,3,4,512]{6,5,4,3,2,1,0:T(4,128)}, u32[]{:S(2)}) copy-start(f32[2,2,8,2,3,4,512]{6,5,4,3,2,1,0:T(4,128)} %get-tuple-element.43.base_ref) | copy-start | bytes 4718596
  91.2 7.0 %collective-permute-start.5 = (f32[32,1,128]{2,1,0:T(1,128)S(1)}, f32[32,1,128]{2,1,0:T(1,128)S(1)}, u32[]{:S(2)}, u32[]{:S(2)}) collective-permute-start(f32[32,1,128]{2,1,0:T(1,128)S(1)} %get-tuple-element.38), channel_id=1, source_target_pairs={{0,96},{32,0},{64,32},{96,64},{1,97},{33,1},{65,33},{97,65},{2,98}... | collective-permute-start | bytes 49160 | tf_op jit(solution)/shard_map/ppermute | solution.py:591
  93.2 5.1 %collective-permute-start.4 = (f32[32,1,128]{2,1,0:T(1,128)S(1)}, f32[32,1,128]{2,1,0:T(1,128)S(1)}, u32[]{:S(2)}, u32[]{:S(2)}) collective-permute-start(f32[32,1,128]{2,1,0:T(1,128)S(1)} %get-tuple-element.38), channel_id=1, source_target_pairs={{0,32},{32,64},{64,96},{96,0},{1,33},{33,65},{65,97},{97,1},{2,34}... | collective-permute-start | bytes 49160 | tf_op jit(solution)/shard_map/ppermute | solution.py:591
  93.2 5.1 %collective-permute-start.3 = (f32[32,1,128]{2,1,0:T(1,128)S(1)}, f32[32,1,128]{2,1,0:T(1,128)S(1)}, u32[]{:S(2)}, u32[]{:S(2)}) collective-permute-start(f32[32,1,128]{2,1,0:T(1,128)S(1)} %get-tuple-element.38), channel_id=1, source_target_pairs={{0,64},{32,96},{64,0},{96,32},{1,65},{33,97},{65,1},{97,33},{2,66}... | collective-permute-start | bytes 49160 | tf_op jit(solution)/shard_map/ppermute | solution.py:591
  95.1 10.8 %collective-permute-start.6 = (bf16[192,512]{1,0:T(8,128)(2,1)S(1)}, bf16[192,512]{1,0:T(8,128)(2,1)S(1)}, u32[]{:S(2)}, u32[]{:S(2)}) collective-permute-start(bf16[192,512]{1,0:T(8,128)(2,1)S(1)} %get-tuple-element.40), channel_id=1, source_target_pairs={{0,96},{32,0},{64,32},{96,64},{1,97},{33,1},{65,33},{97,65},{2,98}... | collective-permute-start | bytes 589832 | tf_op jit(solution)/shard_map/ppermute | solution.py:591
  96.2 9.6 %collective-permute-start.7 = (bf16[192,512]{1,0:T(8,128)(2,1)S(1)}, bf16[192,512]{1,0:T(8,128)(2,1)S(1)}, u32[]{:S(2)}, u32[]{:S(2)}) collective-permute-start(bf16[192,512]{1,0:T(8,128)(2,1)S(1)} %get-tuple-element.41), channel_id=1, source_target_pairs={{0,64},{32,96},{64,0},{96,32},{1,65},{33,97},{65,1},{97,33},{2,66}... | collective-permute-start | bytes 589832 | tf_op jit(solution)/shard_map/ppermute | solution.py:591
  98.3 9.5 %collective-permute-start.8 = (bf16[192,512]{1,0:T(8,128)(2,1)S(1)}, bf16[192,512]{1,0:T(8,128)(2,1)S(1)}, u32[]{:S(2)}, u32[]{:S(2)}) collective-permute-start(bf16[192,512]{1,0:T(8,128)(2,1)S(1)} %get-tuple-element.42), channel_id=1, source_target_pairs={{0,32},{32,64},{64,96},{96,0},{1,33},{33,65},{65,97},{97,1},{2,34}... | collective-permute-start | bytes 589832 | tf_op jit(solution)/shard_map/ppermute | solution.py:591
  98.9 13.6 %all-to-all-start.2 = ((f32[32,1,128]{2,1,0:T(1,128)}), f32[32,1,128]{2,1,0:T(1,128)S(1)}, u32[]{:S(2)}, u32[]{:S(2)}) async-start(f32[32,1,128]{2,1,0:T(1,128)} %bitcast.33), calls=%async_computation.2 | async-start | bytes 32768 | tf_op jit(solution)/shard_map/all_to_all | solution.py:587

commit v8 on v6

--- a/solution.py
+++ b/solution.py
@@ -523,7 +523,7 @@
             ],
             out_specs=(
                 *[spec((MB * COLS, DEGREES), lambda i, s: (i, 0))] * 4,
-                spec((4 * NBAND, 1, 128), lambda i, s: (0, 0, 0)),
+                spec((NBAND // 2, 8, 128), lambda i, s: (0, 0, 0)),
             ),
             scratch_shapes=[
                 pltpu.VMEM((2, 4, 4 * COLS * 8, 128), jnp.float32),
@@ -535,7 +535,7 @@
         ),
         out_shape=(
             *[jax.ShapeDtypeStruct((8 * COLS, DEGREES), jnp.bfloat16)] * 4,
-            jax.ShapeDtypeStruct((4 * NBAND, 1, 128), jnp.float32),
+            jax.ShapeDtypeStruct((NBAND // 2, 8, 128), jnp.float32),
         ),
         compiler_params=pltpu.CompilerParams(vmem_limit_bytes=46 * MIB),
         cost_estimate=pl.CostEstimate(
@@ -631,7 +631,7 @@
     spectra = exchange(columns.reshape(4 * NBAND, 16, LANES), SEND_NODE)
     *mixed, sums = analysis(ids, quadrature, spectra, leg4, moves, st6, damp)
     mixed = [mixed[0]] + [shift(mixed[s], "node", -s) for s in (1, 2, 3)]
-    sums = exchange(sums, SEND_NODE)
+    sums = exchange(sums.reshape(4 * NBAND, 1, 128), SEND_NODE)
     out = update(ids, mixed, settled)
     sums, out = lax.optimization_barrier((sums, out))
     total = jnp.sum(sums, axis=(0, 1))

time: 114 us -> 114 us (level)
  no operation moved by 1% of the time
where the time goes in v8:
time: 114 us
  Pallas kernels  41.9 us (37%)
  blocking collectives  30 us (26%)
  starting transfers between devices  25.8 us (23%)
  waiting for transfers between devices  13.7 us (12%)
    all_to_all x1, blocking collectives, exchange(): return lax.all_to_all(x, axes, split_axis=0, concat_axis=0, tiled=True)  30 us
    all_to_all x2, starting transfers between devices, exchange(): return lax.all_to_all(x, axes, split_axis=0, concat_axis=0, tiled=True)  17.1 us
    pallas_call x1, Pallas kernels, synthesis(): pl.pallas_call(synthesis_kernel, in_specs=[pl.BlockSpec(memory_space=pl.A...  12.2 us
    pallas_call x1, Pallas kernels, grid_stage(): pl.pallas_call(grid_kernel, in_specs=[pl.BlockSpec(memory_space=pltpu.VME...  11.8 us
    ppermute x6, starting transfers between devices, shift(): return lax.ppermute(x, axis, [(i, (i + by) % 4) for i in range(4)])  8.74 us
    all_to_all x2, waiting for transfers between devices, exchange(): return lax.all_to_all(x, axes, split_axis=0, concat_axis=0, tiled=True)  7.85 us
    pallas_call x1, Pallas kernels, analysis(): pl.pallas_call(analysis_kernel, grid_spec=pltpu.PrefetchScalarGridSpec(nu...  5.92 us
    ppermute x6, waiting for transfers between devices, shift(): return lax.ppermute(x, axis, [(i, (i + by) % 4) for i in range(4)])  5.9 us
  transfers between devices with their start and end apart: 8, of which 4 were waited for; matrix products, arithmetic and copies ran while one was open for 1% of the time, Pallas kernels for 11%

profile of v8, /device:TPU:1, one launch (start us, length us, event | category | flops | bytes accessed | tf_op | source)
XLA Modules:
  0.0 113.6 jit_solution(15281131665261847157)
XLA Ops:
  0.6 12.2 %synthesis.1 = bf16[32,64,384]{2,1,0:T(8,128)(2,1)} custom-call(f32[2,16,2,3,4,512]{5,4,3,2,1,0:T(4,128)} %bitcast.43, bf16[16,2,512,512]{3,2,1,0:T(8,128)(2,1)} %bitcast.41), custom_call_target="tpu_custom_call" | custom-call | flops 402653184 | bytes 20971520 | tf_op jit(solution)/shard_map/synthesis/pallas_call | solution.py:115
  12.8 8.6 %all-to-all-start = ((bf16[32,64,384]{2,1,0:T(8,128)(2,1)}), bf16[32,64,384]{2,1,0:T(8,128)(2,1)S(1)}, u32[]{:S(2)}, u32[]{:S(2)}) async-start(bf16[32,64,384]{2,1,0:T(8,128)(2,1)} %synthesis.1), calls=%async_computation | async-start | bytes 3145728 | tf_op jit(solution)/shard_map/all_to_all | solution.py:587
  21.4 0.0 copy-start.6
  21.4 0.0 copy-start.5
  21.4 4.8 %prepare.1 = (bf16[192,512]{1,0:T(8,128)(2,1)}, bf16[192,512]{1,0:T(8,128)(2,1)}, bf16[192,512]{1,0:T(8,128)(2,1)}, bf16[192,512]{1,0:T(8,128)(2,1)}, f32[2,2,8,2,3,4,512]{6,5,4,3,2,1,0:T(4,128)}) custom-call(s32[1]{0:T(128)} %bitcast.id_ref, f32[4,4]{1,0:T(4,128)} %quad_ref.2, f32[2,2,8,2,3,4,512]{6,5,4,3,2,1,0:T(4,128)} %bitcast.32, ...), custom_call_target="tpu_custom_call" | custom-call | flops 3145728 | bytes 6291456 | tf_op jit(solution)/shard_map/prepare/pallas_call | solution.py:185
  26.2 1.6 %collective-permute-start = (bf16[192,512]{1,0:T(8,128)(2,1)}, bf16[192,512]{1,0:T(8,128)(2,1)S(1)}, u32[]{:S(2)}, u32[]{:S(2)}) collective-permute-start(bf16[192,512]{1,0:T(8,128)(2,1)} %get-tuple-element.30), channel_id=1, source_target_pairs={{0,32},{32,64},{64,96},{96,0},{1,33},{33,65},{65,97},{97,1},{2,34}... | collective-permute-start | bytes 589832 | tf_op jit(solution)/shard_map/ppermute | solution.py:591
  27.8 3.3 %collective-permute-start.1 = (bf16[192,512]{1,0:T(8,128)(2,1)}, bf16[192,512]{1,0:T(8,128)(2,1)S(1)}, u32[]{:S(2)}, u32[]{:S(2)}) collective-permute-start(bf16[192,512]{1,0:T(8,128)(2,1)} %get-tuple-element.31), channel_id=1, source_target_pairs={{0,64},{32,96},{64,0},{96,32},{1,65},{33,97},{65,1},{97,33},{2,66}... | collective-permute-start | bytes 589832 | tf_op jit(solution)/shard_map/ppermute | solution.py:591
  31.1 0.7 collective-permute-start.2
  31.8 0.1 dynamic_slice.7
  31.9 0.1 constant_dynamic-slice_fusion
  32.0 0.1 broadcast_select_fusion
  32.1 0.1 reshape.119
  32.2 4.9 %tables.1 = (bf16[4,2,528,512]{3,2,1,0:T(8,128)(2,1)}, bf16[4,2,512,512]{3,2,1,0:T(8,128)(2,1)}) custom-call(f32[2,2,33,512]{3,2,1,0:T(8,128)} %constant.59.clone.row1_ref, f32[2,2,16,512]{3,2,1,0:T(8,128)} %constant.60.clone.row2_ref), custom_call_target="tpu_custom_call" | custom-call | flops 4325376 | bytes 9437184 | tf_op jit(solution)/shard_map/tables/pallas_call | solution.py:267
  37.0 0.1 dynamic-slice_bitcast_fusion
  37.1 0.1 compare_select_fusion
  37.2 0.1 maximum_bitcast_fusion
  37.3 3.1 %collective-permute-done.1 = bf16[192,512]{1,0:T(8,128)(2,1)S(1)} collective-permute-done((bf16[192,512]{1,0:T(8,128)(2,1)}, bf16[192,512]{1,0:T(8,128)(2,1)S(1)}, u32[]{:S(2)}, u32[]{:S(2)}) %collective-permute-start.1) | collective-permute-done | bytes 196640 | tf_op jit(solution)/shard_map/ppermute | solution.py:591
  40.4 3.7 %all-to-all-done.got_ref = bf16[32,64,384]{2,1,0:T(8,128)(2,1)S(1)} async-done(((bf16[32,64,384]{2,1,0:T(8,128)(2,1)}), bf16[32,64,384]{2,1,0:T(8,128)(2,1)S(1)}, u32[]{:S(2)}, u32[]{:S(2)}) %all-to-all-start) | async-done | bytes 1572896 | tf_op jit(solution)/shard_map/all_to_all | solution.py:587
  44.0 11.8 %grid.1 = bf16[32,4,16,384]{3,2,1,0:T(8,128)(2,1)S(1)} custom-call(bf16[32,64,384]{2,1,0:T(8,128)(2,1)S(1)} %all-to-all-done.got_ref, bf16[4,2,528,512]{3,2,1,0:T(8,128)(2,1)} %get-tuple-element.26.tab_hbm, bf16[4,2,512,512]{3,2,1,0:T(8,128)(2,1)} %get-tuple-element.27.back_hbm, f32[3,128]{1,0:T(4,128)S(1)} %pad_maximum_fusion.rows_ref), custom_call_target="tpu_custom_call" | custom-call | flops 5813305344 | bytes 17825792 | tf_op jit(solution)/shard_map/grid/pallas_call | solution.py:385
  55.9 0.0 copy-start.2
  55.9 0.0 copy-start.4
  55.9 30.0 %all_to_all.15.y_ref = bf16[128,16,384]{2,1,0:T(8,128)(2,1)S(1)} all-to-all(bf16[128,16,384]{2,1,0:T(8,128)(2,1)S(1)} %bitcast.34), channel_id=1, replica_groups=mesh['node'=4,'band_0'=4,'band_1'=4,'band_2'=2] {'band_2','band_1','band..., dimensions={0} | all-to-all | bytes 3145728 | tf_op jit(solution)/shard_map/all_to_all | solution.py:587
  85.9 5.9 %analysis.1 = (bf16[192,512]{1,0:T(8,128)(2,1)S(1)}, bf16[192,512]{1,0:T(8,128)(2,1)S(1)}, bf16[192,512]{1,0:T(8,128)(2,1)S(1)}, bf16[192,512]{1,0:T(8,128)(2,1)S(1)}, f32[16,8,128]{2,1,0:T(8,128)}) custom-call(s32[1]{0:T(128)} %bitcast.id_ref, f32[4,4]{1,0:T(4,128)S(1)} %copy-done.4, bf16[128,16,384]{2,1,0:T(8,128)(2,1)S(1)} %all_to_all.15.y_ref, ...), custom_call_target="tpu_custom_call" | custom-call | flops 402653184 | bytes 10485760 | tf_op jit(solution)/shard_map/analysis/pallas_call | solution.py:506
  91.8 1.9 %collective-permute-start.3 = (bf16[192,512]{1,0:T(8,128)(2,1)S(1)}, bf16[192,512]{1,0:T(8,128)(2,1)S(1)}, u32[]{:S(2)}, u32[]{:S(2)}) collective-permute-start(bf16[192,512]{1,0:T(8,128)(2,1)S(1)} %get-tuple-element.40), channel_id=1, source_target_pairs={{0,96},{32,0},{64,32},{96,64},{1,97},{33,1},{65,33},{97,65},{2,98}... | collective-permute-start | bytes 589832 | tf_op jit(solution)/shard_map/ppermute | solution.py:591
  93.7 0.9 collective-permute-start.4
  94.7 0.3 collective-permute-start.5
  95.0 8.5 %all-to-all-start.2 = ((f32[128,1,128]{2,1,0:T(1,128)}), f32[128,1,128]{2,1,0:T(1,128)S(1)}, u32[]{:S(2)}, u32[]{:S(2)}) async-start(f32[128,1,128]{2,1,0:T(1,128)} %bitcast.19), calls=%async_computation.2 | async-start | bytes 131072 | tf_op jit(solution)/shard_map/all_to_all | solution.py:587
  103.5 2.8 %collective-permute-done.5.mixed3_ref = bf16[192,512]{1,0:T(8,128)(2,1)S(1)} collective-permute-done((bf16[192,512]{1,0:T(8,128)(2,1)S(1)}, bf16[192,512]{1,0:T(8,128)(2,1)S(1)}, u32[]{:S(2)}, u32[]{:S(2)}) %collective-permute-start.5) | collective-permute-done | bytes 196640 | tf_op jit(solution)/shard_map/ppermute | solution.py:591
  106.3 2.4 %update.1 = f32[2,2,8,2,3,4,512]{6,5,4,3,2,1,0:T(4,128)} custom-call(s32[1]{0:T(128)} %bitcast.id_ref, bf16[192,512]{1,0:T(8,128)(2,1)S(1)} %get-tuple-element.39.mixed0_ref, bf16[192,512]{1,0:T(8,128)(2,1)S(1)} %collective-permute-done.3.mixed1_ref, bf16[192,512]{1,0:T(8,128)(2,1)S(1)} %collective-permute-done.4.mixed2_ref, ...), custom_call_target="tpu_custom_call" | custom-call | flops 1572864 | bytes 5242880 | tf_op jit(solution)/shard_map/update/pallas_call | solution.py:568
  108.6 4.2 %all-to-all-done.2 = f32[128,1,128]{2,1,0:T(1,128)S(1)} async-done(((f32[128,1,128]{2,1,0:T(1,128)}), f32[128,1,128]{2,1,0:T(1,128)S(1)}, u32[]{:S(2)}, u32[]{:S(2)}) %all-to-all-start.2) | async-done | bytes 65568 | tf_op jit(solution)/shard_map/all_to_all | solution.py:587
  112.8 0.2 reduce_sum.9
  113.0 0.6 fusion
  (16 shorter events, 0.1 us)
Async XLA Ops:
  12.8 31.3 %all-to-all-start = ((bf16[32,64,384]{2,1,0:T(8,128)(2,1)}), bf16[32,64,384]{2,1,0:T(8,128)(2,1)S(1)}, u32[]{:S(2)}, u32[]{:S(2)}) async-start(bf16[32,64,384]{2,1,0:T(8,128)(2,1)} %synthesis.1), calls=%async_computation | async-start | bytes 3145728 | tf_op jit(solution)/shard_map/all_to_all | solution.py:587
  21.4 10.4 %copy-start.6 = (f32[512]{0:T(512)S(1)}, f32[512]{0:T(512)}, u32[]{:S(2)}) copy-start(f32[512]{0:T(512)} %param.12) | copy-start | bytes 6148
  21.4 10.5 %copy-start.5 = (f32[2,512]{1,0:T(2,128)S(1)}, f32[2,512]{1,0:T(2,128)}, u32[]{:S(2)}) copy-start(f32[2,512]{1,0:T(2,128)} %param.13) | copy-start | bytes 12292
  26.2 11.1 %collective-permute-start = (bf16[192,512]{1,0:T(8,128)(2,1)}, bf16[192,512]{1,0:T(8,128)(2,1)S(1)}, u32[]{:S(2)}, u32[]{:S(2)}) collective-permute-start(bf16[192,512]{1,0:T(8,128)(2,1)} %get-tuple-element.30), channel_id=1, source_target_pairs={{0,32},{32,64},{64,96},{96,0},{1,33},{33,65},{65,97},{97,1},{2,34}... | collective-permute-start | bytes 589832 | tf_op jit(solution)/shard_map/ppermute | solution.py:591
  27.8 12.5 %collective-permute-start.1 = (bf16[192,512]{1,0:T(8,128)(2,1)}, bf16[192,512]{1,0:T(8,128)(2,1)S(1)}, u32[]{:S(2)}, u32[]{:S(2)}) collective-permute-start(bf16[192,512]{1,0:T(8,128)(2,1)} %get-tuple-element.31), channel_id=1, source_target_pairs={{0,64},{32,96},{64,0},{96,32},{1,65},{33,97},{65,1},{97,33},{2,66}... | collective-permute-start | bytes 589832 | tf_op jit(solution)/shard_map/ppermute | solution.py:591
  31.1 9.2 %collective-permute-start.2 = (bf16[192,512]{1,0:T(8,128)(2,1)}, bf16[192,512]{1,0:T(8,128)(2,1)S(1)}, u32[]{:S(2)}, u32[]{:S(2)}) collective-permute-start(bf16[192,512]{1,0:T(8,128)(2,1)} %get-tuple-element.32), channel_id=1, source_target_pairs={{0,96},{32,0},{64,32},{96,64},{1,97},{33,1},{65,33},{97,65},{2,98}... | collective-permute-start | bytes 589832 | tf_op jit(solution)/shard_map/ppermute | solution.py:591
  55.9 30.0 %copy-start = (f32[2,32,4,3,512]{4,2,3,1,0:T(4,128)S(1)}, f32[2,32,4,3,512]{4,2,3,1,0:T(4,128)}, u32[]{:S(2)}) copy-start(f32[2,32,4,3,512]{4,2,3,1,0:T(4,128)} %param.9) | copy-start | bytes 4718596
  55.9 30.0 %copy-start.2 = (f32[32,3,512]{2,0,1:T(8,128)S(1)}, f32[32,3,512]{2,0,1:T(8,128)}, u32[]{:S(2)}) copy-start(f32[32,3,512]{2,0,1:T(8,128)} %param.14) | copy-start | bytes 589828
  55.9 30.0 %copy-start.3 = (bf16[192,512]{1,0:T(8,128)(2,1)S(1)}, bf16[192,512]{1,0:T(8,128)(2,1)}, u32[]{:S(2)}) copy-start(bf16[192,512]{1,0:T(8,128)(2,1)} %get-tuple-element.34) | copy-start | bytes 589828
  55.9 30.0 %copy-start.4 = (f32[4,4]{1,0:T(4,128)S(1)}, f32[4,4]{1,0:T(4,128)}, u32[]{:S(2)}) copy-start(f32[4,4]{1,0:T(4,128)} %quad_ref.2) | copy-start | bytes 196
  85.9 20.4 %copy-start.1 = (f32[2,2,8,2,3,4,512]{6,5,4,3,2,1,0:T(4,128)S(1)}, f32[2,2,8,2,3,4,512]{6,5,4,3,2,1,0:T(4,128)}, u32[]{:S(2)}) copy-start(f32[2,2,8,2,3,4,512]{6,5,4,3,2,1,0:T(4,128)} %get-tuple-element.43.base_ref) | copy-start | bytes 4718596
  91.8 11.6 %collective-permute-start.3 = (bf16[192,512]{1,0:T(8,128)(2,1)S(1)}, bf16[192,512]{1,0:T(8,128)(2,1)S(1)}, u32[]{:S(2)}, u32[]{:S(2)}) collective-permute-start(bf16[192,512]{1,0:T(8,128)(2,1)S(1)} %get-tuple-element.40), channel_id=1, source_target_pairs={{0,96},{32,0},{64,32},{96,64},{1,97},{33,1},{65,33},{97,65},{2,98}... | collective-permute-start | bytes 589832 | tf_op jit(solution)/shard_map/ppermute | solution.py:591
  93.7 9.7 %collective-permute-start.4 = (bf16[192,512]{1,0:T(8,128)(2,1)S(1)}, bf16[192,512]{1,0:T(8,128)(2,1)S(1)}, u32[]{:S(2)}, u32[]{:S(2)}) collective-permute-start(bf16[192,512]{1,0:T(8,128)(2,1)S(1)} %get-tuple-element.41), channel_id=1, source_target_pairs={{0,64},{32,96},{64,0},{96,32},{1,65},{33,97},{65,1},{97,33},{2,66}... | collective-permute-start | bytes 589832 | tf_op jit(solution)/shard_map/ppermute | solution.py:591
  94.7 11.6 %collective-permute-start.5 = (bf16[192,512]{1,0:T(8,128)(2,1)S(1)}, bf16[192,512]{1,0:T(8,128)(2,1)S(1)}, u32[]{:S(2)}, u32[]{:S(2)}) collective-permute-start(bf16[192,512]{1,0:T(8,128)(2,1)S(1)} %get-tuple-element.42), channel_id=1, source_target_pairs={{0,32},{32,64},{64,96},{96,0},{1,33},{33,65},{65,97},{97,1},{2,34}... | collective-permute-start | bytes 589832 | tf_op jit(solution)/shard_map/ppermute | solution.py:591
  95.0 17.8 %all-to-all-start.2 = ((f32[128,1,128]{2,1,0:T(1,128)}), f32[128,1,128]{2,1,0:T(1,128)S(1)}, u32[]{:S(2)}, u32[]{:S(2)}) async-start(f32[128,1,128]{2,1,0:T(1,128)} %bitcast.19), calls=%async_computation.2 | async-start | bytes 131072 | tf_op jit(solution)/shard_map/all_to_all | solution.py:587

commit v9 on v8

--- a/solution.py
+++ b/solution.py
@@ -122,7 +122,7 @@
             pltpu.SemaphoreType.DMA((STREAMS + 1,)),
             pltpu.VMEM((2, COLS, DEGREES), jnp.float32),
             pltpu.VMEM((128, DEGREES), jnp.float32),
-            pltpu.VMEM((8, COLS * 2 * PAIRS, 128), jnp.float32),
+            pltpu.VMEM((8, (COLS + 1) * 2 * PAIRS, 128), jnp.float32),
         ],
         compiler_params=pltpu.CompilerParams(vmem_limit_bytes=56 * MIB),
         cost_estimate=pl.CostEstimate(
@@ -526,7 +526,7 @@
                 spec((NBAND // 2, 8, 128), lambda i, s: (0, 0, 0)),
             ),
             scratch_shapes=[
-                pltpu.VMEM((2, 4, 4 * COLS * 8, 128), jnp.float32),
+                pltpu.VMEM((2, 4, (4 * COLS + 1) * 8, 128), jnp.float32),
                 pltpu.VMEM((COLS, DEGREES), jnp.float32),
                 pltpu.VMEM((COLS, DEGREES), jnp.float32),
                 pltpu.VMEM((4, MB * COLS, DEGREES), jnp.float32),

time: 114 us -> 114 us (level)
  no operation moved by 1% of the time
where the time goes in v9:
time: 114 us; the launch traced here: 113 us
  Pallas kernels  41.7 us (37%)
  blocking collectives  30 us (26%)
  starting transfers between devices  25.8 us (23%)
  waiting for transfers between devices  13.7 us (12%)
    all_to_all x1, blocking collectives, exchange(): return lax.all_to_all(x, axes, split_axis=0, concat_axis=0, tiled=True)  30 us
    all_to_all x2, starting transfers between devices, exchange(): return lax.all_to_all(x, axes, split_axis=0, concat_axis=0, tiled=True)  17.1 us
    pallas_call x1, Pallas kernels, synthesis(): pl.pallas_call(synthesis_kernel, in_specs=[pl.BlockSpec(memory_space=pl.A...  12.1 us
    pallas_call x1, Pallas kernels, grid_stage(): pl.pallas_call(grid_kernel, in_specs=[pl.BlockSpec(memory_space=pltpu.VME...  11.8 us
    ppermute x6, starting transfers between devices, shift(): return lax.ppermute(x, axis, [(i, (i + by) % 4) for i in range(4)])  8.73 us
    all_to_all x2, waiting for transfers between devices, exchange(): return lax.all_to_all(x, axes, split_axis=0, concat_axis=0, tiled=True)  7.85 us
    ppermute x6, waiting for transfers between devices, shift(): return lax.ppermute(x, axis, [(i, (i + by) % 4) for i in range(4)])  5.9 us
    pallas_call x1, Pallas kernels, analysis(): pl.pallas_call(analysis_kernel, grid_spec=pltpu.PrefetchScalarGridSpec(nu...  5.8 us
  transfers between devices with their start and end apart: 8, of which 4 were waited for; matrix products, arithmetic and copies ran while one was open for 1% of the time, Pallas kernels for 11%

profile of v9, /device:TPU:1, one launch (start us, length us, event | category | flops | bytes accessed | tf_op | source)
XLA Modules:
  0.0 113.4 jit_solution(10218124036697838217)
XLA Ops:
  0.6 12.1 %synthesis.1 = bf16[32,64,384]{2,1,0:T(8,128)(2,1)} custom-call(f32[2,16,2,3,4,512]{5,4,3,2,1,0:T(4,128)} %bitcast.43, bf16[16,2,512,512]{3,2,1,0:T(8,128)(2,1)} %bitcast.41), custom_call_target="tpu_custom_call" | custom-call | flops 402653184 | bytes 20971520 | tf_op jit(solution)/shard_map/synthesis/pallas_call | solution.py:115
  12.7 8.6 %all-to-all-start = ((bf16[32,64,384]{2,1,0:T(8,128)(2,1)}), bf16[32,64,384]{2,1,0:T(8,128)(2,1)S(1)}, u32[]{:S(2)}, u32[]{:S(2)}) async-start(bf16[32,64,384]{2,1,0:T(8,128)(2,1)} %synthesis.1), calls=%async_computation | async-start | bytes 3145728 | tf_op jit(solution)/shard_map/all_to_all | solution.py:587
  21.3 0.0 copy-start.6
  21.4 0.0 copy-start.5
  21.4 4.8 %prepare.1 = (bf16[192,512]{1,0:T(8,128)(2,1)}, bf16[192,512]{1,0:T(8,128)(2,1)}, bf16[192,512]{1,0:T(8,128)(2,1)}, bf16[192,512]{1,0:T(8,128)(2,1)}, f32[2,2,8,2,3,4,512]{6,5,4,3,2,1,0:T(4,128)}) custom-call(s32[1]{0:T(128)} %bitcast.id_ref, f32[4,4]{1,0:T(4,128)} %quad_ref.2, f32[2,2,8,2,3,4,512]{6,5,4,3,2,1,0:T(4,128)} %bitcast.32, ...), custom_call_target="tpu_custom_call" | custom-call | flops 3145728 | bytes 6291456 | tf_op jit(solution)/shard_map/prepare/pallas_call | solution.py:185
  26.1 1.6 %collective-permute-start = (bf16[192,512]{1,0:T(8,128)(2,1)}, bf16[192,512]{1,0:T(8,128)(2,1)S(1)}, u32[]{:S(2)}, u32[]{:S(2)}) collective-permute-start(bf16[192,512]{1,0:T(8,128)(2,1)} %get-tuple-element.30), channel_id=1, source_target_pairs={{0,32},{32,64},{64,96},{96,0},{1,33},{33,65},{65,97},{97,1},{2,34}... | collective-permute-start | bytes 589832 | tf_op jit(solution)/shard_map/ppermute | solution.py:591
  27.8 3.3 %collective-permute-start.1 = (bf16[192,512]{1,0:T(8,128)(2,1)}, bf16[192,512]{1,0:T(8,128)(2,1)S(1)}, u32[]{:S(2)}, u32[]{:S(2)}) collective-permute-start(bf16[192,512]{1,0:T(8,128)(2,1)} %get-tuple-element.31), channel_id=1, source_target_pairs={{0,64},{32,96},{64,0},{96,32},{1,65},{33,97},{65,1},{97,33},{2,66}... | collective-permute-start | bytes 589832 | tf_op jit(solution)/shard_map/ppermute | solution.py:591
  31.1 0.7 collective-permute-start.2
  31.7 0.1 dynamic_slice.7
  31.8 0.1 constant_dynamic-slice_fusion
  31.9 0.1 broadcast_select_fusion
  32.0 0.1 reshape.119
  32.1 4.9 %tables.1 = (bf16[4,2,528,512]{3,2,1,0:T(8,128)(2,1)}, bf16[4,2,512,512]{3,2,1,0:T(8,128)(2,1)}) custom-call(f32[2,2,33,512]{3,2,1,0:T(8,128)} %constant.59.clone.row1_ref, f32[2,2,16,512]{3,2,1,0:T(8,128)} %constant.60.clone.row2_ref), custom_call_target="tpu_custom_call" | custom-call | flops 4325376 | bytes 9437184 | tf_op jit(solution)/shard_map/tables/pallas_call | solution.py:267
  37.0 0.1 dynamic-slice_bitcast_fusion
  37.0 0.1 compare_select_fusion
  37.1 0.1 maximum_bitcast_fusion
  37.2 3.1 %collective-permute-done.1 = bf16[192,512]{1,0:T(8,128)(2,1)S(1)} collective-permute-done((bf16[192,512]{1,0:T(8,128)(2,1)}, bf16[192,512]{1,0:T(8,128)(2,1)S(1)}, u32[]{:S(2)}, u32[]{:S(2)}) %collective-permute-start.1) | collective-permute-done | bytes 196640 | tf_op jit(solution)/shard_map/ppermute | solution.py:591
  40.3 3.7 %all-to-all-done.got_ref = bf16[32,64,384]{2,1,0:T(8,128)(2,1)S(1)} async-done(((bf16[32,64,384]{2,1,0:T(8,128)(2,1)}), bf16[32,64,384]{2,1,0:T(8,128)(2,1)S(1)}, u32[]{:S(2)}, u32[]{:S(2)}) %all-to-all-start) | async-done | bytes 1572896 | tf_op jit(solution)/shard_map/all_to_all | solution.py:587
  44.0 11.8 %grid.1 = bf16[32,4,16,384]{3,2,1,0:T(8,128)(2,1)S(1)} custom-call(bf16[32,64,384]{2,1,0:T(8,128)(2,1)S(1)} %all-to-all-done.got_ref, bf16[4,2,528,512]{3,2,1,0:T(8,128)(2,1)} %get-tuple-element.26.tab_hbm, bf16[4,2,512,512]{3,2,1,0:T(8,128)(2,1)} %get-tuple-element.27.back_hbm, f32[3,128]{1,0:T(4,128)S(1)} %pad_maximum_fusion.rows_ref), custom_call_target="tpu_custom_call" | custom-call | flops 5813305344 | bytes 17825792 | tf_op jit(solution)/shard_map/grid/pallas_call | solution.py:385
  55.8 0.0 copy-start
  55.8 0.0 copy-start.4
  55.9 30.0 %all_to_all.15.y_ref = bf16[128,16,384]{2,1,0:T(8,128)(2,1)S(1)} all-to-all(bf16[128,16,384]{2,1,0:T(8,128)(2,1)S(1)} %bitcast.34), channel_id=1, replica_groups=mesh['node'=4,'band_0'=4,'band_1'=4,'band_2'=2] {'band_2','band_1','band..., dimensions={0} | all-to-all | bytes 3145728 | tf_op jit(solution)/shard_map/all_to_all | solution.py:587
  85.8 5.8 %analysis.1 = (bf16[192,512]{1,0:T(8,128)(2,1)S(1)}, bf16[192,512]{1,0:T(8,128)(2,1)S(1)}, bf16[192,512]{1,0:T(8,128)(2,1)S(1)}, bf16[192,512]{1,0:T(8,128)(2,1)S(1)}, f32[16,8,128]{2,1,0:T(8,128)}) custom-call(s32[1]{0:T(128)} %bitcast.id_ref, f32[4,4]{1,0:T(4,128)S(1)} %copy-done.4, bf16[128,16,384]{2,1,0:T(8,128)(2,1)S(1)} %all_to_all.15.y_ref, ...), custom_call_target="tpu_custom_call" | custom-call | flops 402653184 | bytes 10485760 | tf_op jit(solution)/shard_map/analysis/pallas_call | solution.py:506
  91.7 1.9 %collective-permute-start.3 = (bf16[192,512]{1,0:T(8,128)(2,1)S(1)}, bf16[192,512]{1,0:T(8,128)(2,1)S(1)}, u32[]{:S(2)}, u32[]{:S(2)}) collective-permute-start(bf16[192,512]{1,0:T(8,128)(2,1)S(1)} %get-tuple-element.40), channel_id=1, source_target_pairs={{0,96},{32,0},{64,32},{96,64},{1,97},{33,1},{65,33},{97,65},{2,98}... | collective-permute-start | bytes 589832 | tf_op jit(solution)/shard_map/ppermute | solution.py:591
  93.6 0.9 collective-permute-start.4
  94.5 0.3 collective-permute-start.5
  94.8 8.5 %all-to-all-start.2 = ((f32[128,1,128]{2,1,0:T(1,128)}), f32[128,1,128]{2,1,0:T(1,128)S(1)}, u32[]{:S(2)}, u32[]{:S(2)}) async-start(f32[128,1,128]{2,1,0:T(1,128)} %bitcast.19), calls=%async_computation.2 | async-start | bytes 131072 | tf_op jit(solution)/shard_map/all_to_all | solution.py:587
  103.3 2.8 %collective-permute-done.5.mixed3_ref = bf16[192,512]{1,0:T(8,128)(2,1)S(1)} collective-permute-done((bf16[192,512]{1,0:T(8,128)(2,1)S(1)}, bf16[192,512]{1,0:T(8,128)(2,1)S(1)}, u32[]{:S(2)}, u32[]{:S(2)}) %collective-permute-start.5) | collective-permute-done | bytes 196640 | tf_op jit(solution)/shard_map/ppermute | solution.py:591
  106.1 2.4 %update.1 = f32[2,2,8,2,3,4,512]{6,5,4,3,2,1,0:T(4,128)} custom-call(s32[1]{0:T(128)} %bitcast.id_ref, bf16[192,512]{1,0:T(8,128)(2,1)S(1)} %get-tuple-element.39.mixed0_ref, bf16[192,512]{1,0:T(8,128)(2,1)S(1)} %collective-permute-done.3.mixed1_ref, bf16[192,512]{1,0:T(8,128)(2,1)S(1)} %collective-permute-done.4.mixed2_ref, ...), custom_call_target="tpu_custom_call" | custom-call | flops 1572864 | bytes 5242880 | tf_op jit(solution)/shard_map/update/pallas_call | solution.py:568
  108.5 4.2 %all-to-all-done.2 = f32[128,1,128]{2,1,0:T(1,128)S(1)} async-done(((f32[128,1,128]{2,1,0:T(1,128)}), f32[128,1,128]{2,1,0:T(1,128)S(1)}, u32[]{:S(2)}, u32[]{:S(2)}) %all-to-all-start.2) | async-done | bytes 65568 | tf_op jit(solution)/shard_map/all_to_all | solution.py:587
  112.6 0.2 reduce_sum.9
  112.8 0.6 fusion
  (16 shorter events, 0.1 us)
Async XLA Ops:
  12.7 31.3 %all-to-all-start = ((bf16[32,64,384]{2,1,0:T(8,128)(2,1)}), bf16[32,64,384]{2,1,0:T(8,128)(2,1)S(1)}, u32[]{:S(2)}, u32[]{:S(2)}) async-start(bf16[32,64,384]{2,1,0:T(8,128)(2,1)} %synthesis.1), calls=%async_computation | async-start | bytes 3145728 | tf_op jit(solution)/shard_map/all_to_all | solution.py:587
  21.3 10.4 %copy-start.6 = (f32[512]{0:T(512)S(1)}, f32[512]{0:T(512)}, u32[]{:S(2)}) copy-start(f32[512]{0:T(512)} %param.12) | copy-start | bytes 6148
  21.4 10.5 %copy-start.5 = (f32[2,512]{1,0:T(2,128)S(1)}, f32[2,512]{1,0:T(2,128)}, u32[]{:S(2)}) copy-start(f32[2,512]{1,0:T(2,128)} %param.13) | copy-start | bytes 12292
  26.1 11.1 %collective-permute-start = (bf16[192,512]{1,0:T(8,128)(2,1)}, bf16[192,512]{1,0:T(8,128)(2,1)S(1)}, u32[]{:S(2)}, u32[]{:S(2)}) collective-permute-start(bf16[192,512]{1,0:T(8,128)(2,1)} %get-tuple-element.30), channel_id=1, source_target_pairs={{0,32},{32,64},{64,96},{96,0},{1,33},{33,65},{65,97},{97,1},{2,34}... | collective-permute-start | bytes 589832 | tf_op jit(solution)/shard_map/ppermute | solution.py:591
  27.8 12.5 %collective-permute-start.1 = (bf16[192,512]{1,0:T(8,128)(2,1)}, bf16[192,512]{1,0:T(8,128)(2,1)S(1)}, u32[]{:S(2)}, u32[]{:S(2)}) collective-permute-start(bf16[192,512]{1,0:T(8,128)(2,1)} %get-tuple-element.31), channel_id=1, source_target_pairs={{0,64},{32,96},{64,0},{96,32},{1,65},{33,97},{65,1},{97,33},{2,66}... | collective-permute-start | bytes 589832 | tf_op jit(solution)/shard_map/ppermute | solution.py:591
  31.1 9.2 %collective-permute-start.2 = (bf16[192,512]{1,0:T(8,128)(2,1)}, bf16[192,512]{1,0:T(8,128)(2,1)S(1)}, u32[]{:S(2)}, u32[]{:S(2)}) collective-permute-start(bf16[192,512]{1,0:T(8,128)(2,1)} %get-tuple-element.32), channel_id=1, source_target_pairs={{0,96},{32,0},{64,32},{96,64},{1,97},{33,1},{65,33},{97,65},{2,98}... | collective-permute-start | bytes 589832 | tf_op jit(solution)/shard_map/ppermute | solution.py:591
  55.8 30.0 %copy-start = (f32[2,32,4,3,512]{4,2,3,1,0:T(4,128)S(1)}, f32[2,32,4,3,512]{4,2,3,1,0:T(4,128)}, u32[]{:S(2)}) copy-start(f32[2,32,4,3,512]{4,2,3,1,0:T(4,128)} %param.9) | copy-start | bytes 4718596
  55.8 30.0 %copy-start.2 = (f32[32,3,512]{2,0,1:T(8,128)S(1)}, f32[32,3,512]{2,0,1:T(8,128)}, u32[]{:S(2)}) copy-start(f32[32,3,512]{2,0,1:T(8,128)} %param.14) | copy-start | bytes 589828
  55.8 30.0 %copy-start.3 = (bf16[192,512]{1,0:T(8,128)(2,1)S(1)}, bf16[192,512]{1,0:T(8,128)(2,1)}, u32[]{:S(2)}) copy-start(bf16[192,512]{1,0:T(8,128)(2,1)} %get-tuple-element.34) | copy-start | bytes 589828
  55.8 30.0 %copy-start.4 = (f32[4,4]{1,0:T(4,128)S(1)}, f32[4,4]{1,0:T(4,128)}, u32[]{:S(2)}) copy-start(f32[4,4]{1,0:T(4,128)} %quad_ref.2) | copy-start | bytes 196
  85.8 20.3 %copy-start.1 = (f32[2,2,8,2,3,4,512]{6,5,4,3,2,1,0:T(4,128)S(1)}, f32[2,2,8,2,3,4,512]{6,5,4,3,2,1,0:T(4,128)}, u32[]{:S(2)}) copy-start(f32[2,2,8,2,3,4,512]{6,5,4,3,2,1,0:T(4,128)} %get-tuple-element.43.base_ref) | copy-start | bytes 4718596
  91.7 11.6 %collective-permute-start.3 = (bf16[192,512]{1,0:T(8,128)(2,1)S(1)}, bf16[192,512]{1,0:T(8,128)(2,1)S(1)}, u32[]{:S(2)}, u32[]{:S(2)}) collective-permute-start(bf16[192,512]{1,0:T(8,128)(2,1)S(1)} %get-tuple-element.40), channel_id=1, source_target_pairs={{0,96},{32,0},{64,32},{96,64},{1,97},{33,1},{65,33},{97,65},{2,98}... | collective-permute-start | bytes 589832 | tf_op jit(solution)/shard_map/ppermute | solution.py:591
  93.6 9.8 %collective-permute-start.4 = (bf16[192,512]{1,0:T(8,128)(2,1)S(1)}, bf16[192,512]{1,0:T(8,128)(2,1)S(1)}, u32[]{:S(2)}, u32[]{:S(2)}) collective-permute-start(bf16[192,512]{1,0:T(8,128)(2,1)S(1)} %get-tuple-element.41), channel_id=1, source_target_pairs={{0,64},{32,96},{64,0},{96,32},{1,65},{33,97},{65,1},{97,33},{2,66}... | collective-permute-start | bytes 589832 | tf_op jit(solution)/shard_map/ppermute | solution.py:591
  94.5 11.6 %collective-permute-start.5 = (bf16[192,512]{1,0:T(8,128)(2,1)S(1)}, bf16[192,512]{1,0:T(8,128)(2,1)S(1)}, u32[]{:S(2)}, u32[]{:S(2)}) collective-permute-start(bf16[192,512]{1,0:T(8,128)(2,1)S(1)} %get-tuple-element.42), channel_id=1, source_target_pairs={{0,32},{32,64},{64,96},{96,0},{1,33},{33,65},{65,97},{97,1},{2,34}... | collective-permute-start | bytes 589832 | tf_op jit(solution)/shard_map/ppermute | solution.py:591
  94.8 17.8 %all-to-all-start.2 = ((f32[128,1,128]{2,1,0:T(1,128)}), f32[128,1,128]{2,1,0:T(1,128)S(1)}, u32[]{:S(2)}, u32[]{:S(2)}) async-start(f32[128,1,128]{2,1,0:T(1,128)} %bitcast.19), calls=%async_computation.2 | async-start | bytes 131072 | tf_op jit(solution)/shard_map/all_to_all | solution.py:587

commit v10 on v9

--- a/solution.py
+++ b/solution.py
@@ -44,11 +44,14 @@
             leg_hbm.at[pl.ds(j % 8 * 2, 2), j // 8], leg_ref.at[j], sems.at[j]
         )
 
-    coefficients = pltpu.make_async_copy(it_hbm, it_ref, sems.at[STREAMS])
-    coefficients.start()
-    for j in range(STREAMS):
-        stream(j).start()
-    coefficients.wait()
+    coefficients = [
+        pltpu.make_async_copy(it_hbm.at[:, :, p], it_ref.at[:, :, p], sems.at[STREAMS + p])
+        for p in range(2)
+    ]
+    for p in range(2):
+        coefficients[p].start()
+        for j in range(8 * p, 8 * p + 8):
+            stream(j).start()
     low = lax.broadcasted_iota(jnp.int32, (COLS, 128), 1) < 64
 
     left = lax.broadcasted_iota(jnp.int32, (LATS, 128), 1) < 64
@@ -98,7 +101,9 @@
                 place(at + 2 + k, t, north, block[64 * k + 32 : 64 * k + 32 + COLS])
         return 0
 
-    lax.fori_loop(0, STREAMS // 2, four, 0)
+    for p in range(2):
+        coefficients[p].wait()
+        lax.fori_loop(4 * p, 4 * p + 4, four, 0)
     for p in range(2):
         for c in range(2):
             for f in range(3):
@@ -119,7 +124,7 @@
         scratch_shapes=[
             pltpu.VMEM(it6.shape, jnp.float32),
             pltpu.VMEM((STREAMS, 2, LATS, DEGREES), jnp.bfloat16),
-            pltpu.SemaphoreType.DMA((STREAMS + 1,)),
+            pltpu.SemaphoreType.DMA((STREAMS + 2,)),
             pltpu.VMEM((2, COLS, DEGREES), jnp.float32),
             pltpu.VMEM((128, DEGREES), jnp.float32),
             pltpu.VMEM((8, (COLS + 1) * 2 * PAIRS, 128), jnp.float32),

time: 114 us -> 114 us (level)
  no operation moved by 1% of the time
where the time goes in v10:
time: 114 us; the launch traced here: 113 us
  Pallas kernels  41.5 us (36%)
  blocking collectives  30 us (26%)
  starting transfers between devices  25.8 us (23%)
  waiting for transfers between devices  13.7 us (12%)
    all_to_all x1, blocking collectives, exchange(): return lax.all_to_all(x, axes, split_axis=0, concat_axis=0, tiled=True)  30 us
    all_to_all x2, starting transfers between devices, exchange(): return lax.all_to_all(x, axes, split_axis=0, concat_axis=0, tiled=True)  17.1 us
    pallas_call x1, Pallas kernels, synthesis(): pl.pallas_call(synthesis_kernel, in_specs=[pl.BlockSpec(memory_space=pl.A...  11.9 us
    pallas_call x1, Pallas kernels, grid_stage(): pl.pallas_call(grid_kernel, in_specs=[pl.BlockSpec(memory_space=pltpu.VME...  11.8 us
    ppermute x6, starting transfers between devices, shift(): return lax.ppermute(x, axis, [(i, (i + by) % 4) for i in range(4)])  8.74 us
    all_to_all x2, waiting for transfers between devices, exchange(): return lax.all_to_all(x, axes, split_axis=0, concat_axis=0, tiled=True)  7.85 us
    ppermute x6, waiting for transfers between devices, shift(): return lax.ppermute(x, axis, [(i, (i + by) % 4) for i in range(4)])  5.89 us
    pallas_call x1, Pallas kernels, analysis(): pl.pallas_call(analysis_kernel, grid_spec=pltpu.PrefetchScalarGridSpec(nu...  5.8 us
  transfers between devices with their start and end apart: 8, of which 4 were waited for; matrix products, arithmetic and copies ran while one was open for 1% of the time, Pallas kernels for 11%

profile of v10, /device:TPU:1, one launch (start us, length us, event | category | flops | bytes accessed | tf_op | source)
XLA Modules:
  0.0 113.2 jit_solution(1127344099551960656)
XLA Ops:
  0.6 11.9 %synthesis.1 = bf16[32,64,384]{2,1,0:T(8,128)(2,1)} custom-call(f32[2,16,2,3,4,512]{5,4,3,2,1,0:T(4,128)} %bitcast.43, bf16[16,2,512,512]{3,2,1,0:T(8,128)(2,1)} %bitcast.41), custom_call_target="tpu_custom_call" | custom-call | flops 402653184 | bytes 20971520 | tf_op jit(solution)/shard_map/synthesis/pallas_call | solution.py:120
  12.5 8.6 %all-to-all-start = ((bf16[32,64,384]{2,1,0:T(8,128)(2,1)}), bf16[32,64,384]{2,1,0:T(8,128)(2,1)S(1)}, u32[]{:S(2)}, u32[]{:S(2)}) async-start(bf16[32,64,384]{2,1,0:T(8,128)(2,1)} %synthesis.1), calls=%async_computation | async-start | bytes 3145728 | tf_op jit(solution)/shard_map/all_to_all | solution.py:592
  21.1 0.0 copy-start.6
  21.1 0.0 copy-start.5
  21.1 4.8 %prepare.1 = (bf16[192,512]{1,0:T(8,128)(2,1)}, bf16[192,512]{1,0:T(8,128)(2,1)}, bf16[192,512]{1,0:T(8,128)(2,1)}, bf16[192,512]{1,0:T(8,128)(2,1)}, f32[2,2,8,2,3,4,512]{6,5,4,3,2,1,0:T(4,128)}) custom-call(s32[1]{0:T(128)} %bitcast.id_ref, f32[4,4]{1,0:T(4,128)} %quad_ref.2, f32[2,2,8,2,3,4,512]{6,5,4,3,2,1,0:T(4,128)} %bitcast.32, ...), custom_call_target="tpu_custom_call" | custom-call | flops 3145728 | bytes 6291456 | tf_op jit(solution)/shard_map/prepare/pallas_call | solution.py:190
  25.9 1.6 %collective-permute-start = (bf16[192,512]{1,0:T(8,128)(2,1)}, bf16[192,512]{1,0:T(8,128)(2,1)S(1)}, u32[]{:S(2)}, u32[]{:S(2)}) collective-permute-start(bf16[192,512]{1,0:T(8,128)(2,1)} %get-tuple-element.30), channel_id=1, source_target_pairs={{0,32},{32,64},{64,96},{96,0},{1,33},{33,65},{65,97},{97,1},{2,34}... | collective-permute-start | bytes 589832 | tf_op jit(solution)/shard_map/ppermute | solution.py:596
  27.6 3.3 %collective-permute-start.1 = (bf16[192,512]{1,0:T(8,128)(2,1)}, bf16[192,512]{1,0:T(8,128)(2,1)S(1)}, u32[]{:S(2)}, u32[]{:S(2)}) collective-permute-start(bf16[192,512]{1,0:T(8,128)(2,1)} %get-tuple-element.31), channel_id=1, source_target_pairs={{0,64},{32,96},{64,0},{96,32},{1,65},{33,97},{65,1},{97,33},{2,66}... | collective-permute-start | bytes 589832 | tf_op jit(solution)/shard_map/ppermute | solution.py:596
  30.8 0.7 collective-permute-start.2
  31.5 0.1 dynamic_slice.7
  31.6 0.1 constant_dynamic-slice_fusion
  31.7 0.1 broadcast_select_fusion
  31.8 0.1 reshape.119
  31.9 4.9 %tables.1 = (bf16[4,2,528,512]{3,2,1,0:T(8,128)(2,1)}, bf16[4,2,512,512]{3,2,1,0:T(8,128)(2,1)}) custom-call(f32[2,2,33,512]{3,2,1,0:T(8,128)} %constant.59.clone.row1_ref, f32[2,2,16,512]{3,2,1,0:T(8,128)} %constant.60.clone.row2_ref), custom_call_target="tpu_custom_call" | custom-call | flops 4325376 | bytes 9437184 | tf_op jit(solution)/shard_map/tables/pallas_call | solution.py:272
  36.7 0.1 dynamic-slice_bitcast_fusion
  36.8 0.1 compare_select_fusion
  36.9 0.1 maximum_bitcast_fusion
  37.0 3.1 %collective-permute-done.1 = bf16[192,512]{1,0:T(8,128)(2,1)S(1)} collective-permute-done((bf16[192,512]{1,0:T(8,128)(2,1)}, bf16[192,512]{1,0:T(8,128)(2,1)S(1)}, u32[]{:S(2)}, u32[]{:S(2)}) %collective-permute-start.1) | collective-permute-done | bytes 196640 | tf_op jit(solution)/shard_map/ppermute | solution.py:596
  40.1 3.7 %all-to-all-done.got_ref = bf16[32,64,384]{2,1,0:T(8,128)(2,1)S(1)} async-done(((bf16[32,64,384]{2,1,0:T(8,128)(2,1)}), bf16[32,64,384]{2,1,0:T(8,128)(2,1)S(1)}, u32[]{:S(2)}, u32[]{:S(2)}) %all-to-all-start) | async-done | bytes 1572896 | tf_op jit(solution)/shard_map/all_to_all | solution.py:592
  43.8 11.8 %grid.1 = bf16[32,4,16,384]{3,2,1,0:T(8,128)(2,1)S(1)} custom-call(bf16[32,64,384]{2,1,0:T(8,128)(2,1)S(1)} %all-to-all-done.got_ref, bf16[4,2,528,512]{3,2,1,0:T(8,128)(2,1)} %get-tuple-element.26.tab_hbm, bf16[4,2,512,512]{3,2,1,0:T(8,128)(2,1)} %get-tuple-element.27.back_hbm, f32[3,128]{1,0:T(4,128)S(1)} %pad_maximum_fusion.rows_ref), custom_call_target="tpu_custom_call" | custom-call | flops 5813305344 | bytes 17825792 | tf_op jit(solution)/shard_map/grid/pallas_call | solution.py:390
  55.6 0.0 copy-start
  55.6 0.0 copy-start.2
  55.6 30.0 %all_to_all.15.y_ref = bf16[128,16,384]{2,1,0:T(8,128)(2,1)S(1)} all-to-all(bf16[128,16,384]{2,1,0:T(8,128)(2,1)S(1)} %bitcast.34), channel_id=1, replica_groups=mesh['node'=4,'band_0'=4,'band_1'=4,'band_2'=2] {'band_2','band_1','band..., dimensions={0} | all-to-all | bytes 3145728 | tf_op jit(solution)/shard_map/all_to_all | solution.py:592
  85.6 5.8 %analysis.1 = (bf16[192,512]{1,0:T(8,128)(2,1)S(1)}, bf16[192,512]{1,0:T(8,128)(2,1)S(1)}, bf16[192,512]{1,0:T(8,128)(2,1)S(1)}, bf16[192,512]{1,0:T(8,128)(2,1)S(1)}, f32[16,8,128]{2,1,0:T(8,128)}) custom-call(s32[1]{0:T(128)} %bitcast.id_ref, f32[4,4]{1,0:T(4,128)S(1)} %copy-done.4, bf16[128,16,384]{2,1,0:T(8,128)(2,1)S(1)} %all_to_all.15.y_ref, ...), custom_call_target="tpu_custom_call" | custom-call | flops 402653184 | bytes 10485760 | tf_op jit(solution)/shard_map/analysis/pallas_call | solution.py:511
  91.4 1.9 %collective-permute-start.3 = (bf16[192,512]{1,0:T(8,128)(2,1)S(1)}, bf16[192,512]{1,0:T(8,128)(2,1)S(1)}, u32[]{:S(2)}, u32[]{:S(2)}) collective-permute-start(bf16[192,512]{1,0:T(8,128)(2,1)S(1)} %get-tuple-element.40), channel_id=1, source_target_pairs={{0,96},{32,0},{64,32},{96,64},{1,97},{33,1},{65,33},{97,65},{2,98}... | collective-permute-start | bytes 589832 | tf_op jit(solution)/shard_map/ppermute | solution.py:596
  93.3 0.9 collective-permute-start.4
  94.3 0.3 collective-permute-start.5
  94.6 8.5 %all-to-all-start.2 = ((f32[128,1,128]{2,1,0:T(1,128)}), f32[128,1,128]{2,1,0:T(1,128)S(1)}, u32[]{:S(2)}, u32[]{:S(2)}) async-start(f32[128,1,128]{2,1,0:T(1,128)} %bitcast.19), calls=%async_computation.2 | async-start | bytes 131072 | tf_op jit(solution)/shard_map/all_to_all | solution.py:592
  103.1 2.8 %collective-permute-done.5.mixed3_ref = bf16[192,512]{1,0:T(8,128)(2,1)S(1)} collective-permute-done((bf16[192,512]{1,0:T(8,128)(2,1)S(1)}, bf16[192,512]{1,0:T(8,128)(2,1)S(1)}, u32[]{:S(2)}, u32[]{:S(2)}) %collective-permute-start.5) | collective-permute-done | bytes 196640 | tf_op jit(solution)/shard_map/ppermute | solution.py:596
  105.9 2.4 %update.1 = f32[2,2,8,2,3,4,512]{6,5,4,3,2,1,0:T(4,128)} custom-call(s32[1]{0:T(128)} %bitcast.id_ref, bf16[192,512]{1,0:T(8,128)(2,1)S(1)} %get-tuple-element.39.mixed0_ref, bf16[192,512]{1,0:T(8,128)(2,1)S(1)} %collective-permute-done.3.mixed1_ref, bf16[192,512]{1,0:T(8,128)(2,1)S(1)} %collective-permute-done.4.mixed2_ref, ...), custom_call_target="tpu_custom_call" | custom-call | flops 1572864 | bytes 5242880 | tf_op jit(solution)/shard_map/update/pallas_call | solution.py:573
  108.2 4.2 %all-to-all-done.2 = f32[128,1,128]{2,1,0:T(1,128)S(1)} async-done(((f32[128,1,128]{2,1,0:T(1,128)}), f32[128,1,128]{2,1,0:T(1,128)S(1)}, u32[]{:S(2)}, u32[]{:S(2)}) %all-to-all-start.2) | async-done | bytes 65568 | tf_op jit(solution)/shard_map/all_to_all | solution.py:592
  112.4 0.2 reduce_sum.9
  112.6 0.6 fusion
  (16 shorter events, 0.1 us)
Async XLA Ops:
  12.5 31.3 %all-to-all-start = ((bf16[32,64,384]{2,1,0:T(8,128)(2,1)}), bf16[32,64,384]{2,1,0:T(8,128)(2,1)S(1)}, u32[]{:S(2)}, u32[]{:S(2)}) async-start(bf16[32,64,384]{2,1,0:T(8,128)(2,1)} %synthesis.1), calls=%async_computation | async-start | bytes 3145728 | tf_op jit(solution)/shard_map/all_to_all | solution.py:592
  21.1 10.4 %copy-start.6 = (f32[512]{0:T(512)S(1)}, f32[512]{0:T(512)}, u32[]{:S(2)}) copy-start(f32[512]{0:T(512)} %param.12) | copy-start | bytes 6148
  21.1 10.5 %copy-start.5 = (f32[2,512]{1,0:T(2,128)S(1)}, f32[2,512]{1,0:T(2,128)}, u32[]{:S(2)}) copy-start(f32[2,512]{1,0:T(2,128)} %param.13) | copy-start | bytes 12292
  25.9 11.1 %collective-permute-start = (bf16[192,512]{1,0:T(8,128)(2,1)}, bf16[192,512]{1,0:T(8,128)(2,1)S(1)}, u32[]{:S(2)}, u32[]{:S(2)}) collective-permute-start(bf16[192,512]{1,0:T(8,128)(2,1)} %get-tuple-element.30), channel_id=1, source_target_pairs={{0,32},{32,64},{64,96},{96,0},{1,33},{33,65},{65,97},{97,1},{2,34}... | collective-permute-start | bytes 589832 | tf_op jit(solution)/shard_map/ppermute | solution.py:596
  27.6 12.5 %collective-permute-start.1 = (bf16[192,512]{1,0:T(8,128)(2,1)}, bf16[192,512]{1,0:T(8,128)(2,1)S(1)}, u32[]{:S(2)}, u32[]{:S(2)}) collective-permute-start(bf16[192,512]{1,0:T(8,128)(2,1)} %get-tuple-element.31), channel_id=1, source_target_pairs={{0,64},{32,96},{64,0},{96,32},{1,65},{33,97},{65,1},{97,33},{2,66}... | collective-permute-start | bytes 589832 | tf_op jit(solution)/shard_map/ppermute | solution.py:596
  30.8 9.2 %collective-permute-start.2 = (bf16[192,512]{1,0:T(8,128)(2,1)}, bf16[192,512]{1,0:T(8,128)(2,1)S(1)}, u32[]{:S(2)}, u32[]{:S(2)}) collective-permute-start(bf16[192,512]{1,0:T(8,128)(2,1)} %get-tuple-element.32), channel_id=1, source_target_pairs={{0,96},{32,0},{64,32},{96,64},{1,97},{33,1},{65,33},{97,65},{2,98}... | collective-permute-start | bytes 589832 | tf_op jit(solution)/shard_map/ppermute | solution.py:596
  55.6 30.0 %copy-start = (f32[2,32,4,3,512]{4,2,3,1,0:T(4,128)S(1)}, f32[2,32,4,3,512]{4,2,3,1,0:T(4,128)}, u32[]{:S(2)}) copy-start(f32[2,32,4,3,512]{4,2,3,1,0:T(4,128)} %param.9) | copy-start | bytes 4718596
  55.6 30.0 %copy-start.2 = (f32[32,3,512]{2,0,1:T(8,128)S(1)}, f32[32,3,512]{2,0,1:T(8,128)}, u32[]{:S(2)}) copy-start(f32[32,3,512]{2,0,1:T(8,128)} %param.14) | copy-start | bytes 589828
  55.6 30.0 %copy-start.3 = (bf16[192,512]{1,0:T(8,128)(2,1)S(1)}, bf16[192,512]{1,0:T(8,128)(2,1)}, u32[]{:S(2)}) copy-start(bf16[192,512]{1,0:T(8,128)(2,1)} %get-tuple-element.34) | copy-start | bytes 589828
  55.6 30.0 %copy-start.4 = (f32[4,4]{1,0:T(4,128)S(1)}, f32[4,4]{1,0:T(4,128)}, u32[]{:S(2)}) copy-start(f32[4,4]{1,0:T(4,128)} %quad_ref.2) | copy-start | bytes 196
  85.6 20.3 %copy-start.1 = (f32[2,2,8,2,3,4,512]{6,5,4,3,2,1,0:T(4,128)S(1)}, f32[2,2,8,2,3,4,512]{6,5,4,3,2,1,0:T(4,128)}, u32[]{:S(2)}) copy-start(f32[2,2,8,2,3,4,512]{6,5,4,3,2,1,0:T(4,128)} %get-tuple-element.43.base_ref) | copy-start | bytes 4718596
  91.4 11.6 %collective-permute-start.3 = (bf16[192,512]{1,0:T(8,128)(2,1)S(1)}, bf16[192,512]{1,0:T(8,128)(2,1)S(1)}, u32[]{:S(2)}, u32[]{:S(2)}) collective-permute-start(bf16[192,512]{1,0:T(8,128)(2,1)S(1)} %get-tuple-element.40), channel_id=1, source_target_pairs={{0,96},{32,0},{64,32},{96,64},{1,97},{33,1},{65,33},{97,65},{2,98}... | collective-permute-start | bytes 589832 | tf_op jit(solution)/shard_map/ppermute | solution.py:596
  93.3 9.8 %collective-permute-start.4 = (bf16[192,512]{1,0:T(8,128)(2,1)S(1)}, bf16[192,512]{1,0:T(8,128)(2,1)S(1)}, u32[]{:S(2)}, u32[]{:S(2)}) collective-permute-start(bf16[192,512]{1,0:T(8,128)(2,1)S(1)} %get-tuple-element.41), channel_id=1, source_target_pairs={{0,64},{32,96},{64,0},{96,32},{1,65},{33,97},{65,1},{97,33},{2,66}... | collective-permute-start | bytes 589832 | tf_op jit(solution)/shard_map/ppermute | solution.py:596
  94.3 11.6 %collective-permute-start.5 = (bf16[192,512]{1,0:T(8,128)(2,1)S(1)}, bf16[192,512]{1,0:T(8,128)(2,1)S(1)}, u32[]{:S(2)}, u32[]{:S(2)}) collective-permute-start(bf16[192,512]{1,0:T(8,128)(2,1)S(1)} %get-tuple-element.42), channel_id=1, source_target_pairs={{0,32},{32,64},{64,96},{96,0},{1,33},{33,65},{65,97},{97,1},{2,34}... | collective-permute-start | bytes 589832 | tf_op jit(solution)/shard_map/ppermute | solution.py:596
  94.6 17.8 %all-to-all-start.2 = ((f32[128,1,128]{2,1,0:T(1,128)}), f32[128,1,128]{2,1,0:T(1,128)S(1)}, u32[]{:S(2)}, u32[]{:S(2)}) async-start(f32[128,1,128]{2,1,0:T(1,128)} %bitcast.19), calls=%async_computation.2 | async-start | bytes 131072 | tf_op jit(solution)/shard_map/all_to_all | solution.py:592
